TPU v7x, 32 devices: a whole 2x2x4 slice. The times are simulated.
32 devices in a mesh: seq: 16 (over z, x, core), batch: 2 (over y).
Axes of the slice: x: 2, y: 2, z: 4, core: 2. Of those that a mesh axis runs over, the one named last changes fastest.
Arguments:
- inputs: bfloat16 [2, 4096, 768], P('batch', 'seq'), may hold values from -6 to 6
- lengths: int32 [2], P('batch'), may hold values from 1024 to 4096, as said below
- cotangent: bfloat16 [2, 4096, 768], P('batch', 'seq'), may hold values from -6 to 6
- triple_weight: float32 [768, 2304], P(('seq', 'batch')), may hold values from -0.3125 to 0.3125
- query_bias: float32 [768], P(('seq', 'batch')), may hold values from -3 to 3
- value_bias: float32 [768], P(('seq', 'batch')), may hold values from -3 to 3
- output_weight: float32 [768, 768], P(('seq', 'batch')), may hold values from -1.75 to 1.75
- output_bias: float32 [768], P(('seq', 'batch')), may hold values from -3 to 3
- first_gain: float32 [768], P(('seq', 'batch')), may hold values from 0.5 to 1.5
- first_shift: float32 [768], P(('seq', 'batch')), may hold values from -3 to 3
- expand_weight: float32 [768, 3072], P(('seq', 'batch')), may hold values from -0.21875 to 0.21875
- expand_bias: float32 [3072], P(('seq', 'batch')), may hold values from -3 to 3
- shrink_weight: float32 [3072, 768], P(('seq', 'batch')), may hold values from -0.109375 to 0.109375
- shrink_bias: float32 [768], P(('seq', 'batch')), may hold values from -3 to 3
- second_gain: float32 [768], P(('seq', 'batch')), may hold values from 0.5 to 1.5
- second_shift: float32 [768], P(('seq', 'batch')), may hold values from -3 to 3
Outputs:
- output: bfloat16 [2, 4096, 768], P('batch', 'seq')
- input_grad: bfloat16 [2, 4096, 768], P('batch', 'seq')
- grad_triple_weight: float32 [768, 2304], P(('seq', 'batch'))
- grad_query_bias: float32 [768], P(('seq', 'batch'))
- grad_value_bias: float32 [768], P(('seq', 'batch'))
- grad_output_weight: float32 [768, 768], P(('seq', 'batch'))
- grad_output_bias: float32 [768], P(('seq', 'batch'))
- grad_first_gain: float32 [768], P(('seq', 'batch'))
- grad_first_shift: float32 [768], P(('seq', 'batch'))
- grad_expand_weight: float32 [768, 3072], P(('seq', 'batch'))
- grad_expand_bias: float32 [3072], P(('seq', 'batch'))
- grad_shrink_weight: float32 [3072, 768], P(('seq', 'batch'))
- grad_shrink_bias: float32 [768], P(('seq', 'batch'))
- grad_second_gain: float32 [768], P(('seq', 'batch'))
- grad_second_shift: float32 [768], P(('seq', 'batch'))
Inputs may be any that keep to these rules, and one draw needn't show every extreme that they name: The first lengths slots of a sequence hold its tokens, the others are padding; in every draw some sequence fills all 4096 slots.
All inputs are finite; a program needn't handle non-finite values.
Results may differ from a plain program's by a relative error of at most 0.019.
The roundings to bfloat16 on the way count: a program that leaves them out, or rounds other values in their place, can miss the bound.
Values may be sent and summed in bfloat16 or wider, within the bound.
No kernel may reach another device: no remote copies, remote signals or barrier semaphores. Data moves between devices by JAX's collectives and lax.ppermute only.
A program may use at most 192 MiB of HBM per device.

v0:
```python
from functools import partial
import math

import jax
import jax.numpy as jnp
from jax import lax
from jax.sharding import PartitionSpec as P

HEADS = 12
HEAD_DIM = 64


masked_score = -1e30
norm_eps = 1e-12


def layer_norm(row_block, norm_gain, norm_shift):
    center = row_block - jnp.mean(row_block, axis=-1, keepdims=True)
    spread = jnp.mean(center * center, axis=-1, keepdims=True)
    return center * lax.rsqrt(spread + norm_eps) * norm_gain + norm_shift


def per_device(
    inputs,
    lengths,
    cotangent,
    triple_weight,
    query_bias,
    value_bias,
    output_weight,
    output_bias,
    first_gain,
    first_shift,
    expand_weight,
    expand_bias,
    shrink_weight,
    shrink_bias,
    second_gain,
    second_shift,
):
    masters = (
        triple_weight,
        query_bias,
        value_bias,
        output_weight,
        output_bias,
        first_gain,
        first_shift,
        expand_weight,
        expand_bias,
        shrink_weight,
        shrink_bias,
        second_gain,
        second_shift,
    )
    rounded = tuple((member.astype(jnp.bfloat16) for member in masters))
    fetched = (
        lax.all_gather(rounded[0], ("seq", "batch"), axis=0, tiled=True),
        lax.all_gather(rounded[1], ("seq", "batch"), axis=0, tiled=True),
        lax.all_gather(rounded[2], ("seq", "batch"), axis=0, tiled=True),
        lax.all_gather(rounded[3], ("seq", "batch"), axis=0, tiled=True),
        lax.all_gather(rounded[4], ("seq", "batch"), axis=0, tiled=True),
        lax.all_gather(rounded[5], ("seq", "batch"), axis=0, tiled=True),
        lax.all_gather(rounded[6], ("seq", "batch"), axis=0, tiled=True),
        lax.all_gather(rounded[7], ("seq", "batch"), axis=0, tiled=True),
        lax.all_gather(rounded[8], ("seq", "batch"), axis=0, tiled=True),
        lax.all_gather(rounded[9], ("seq", "batch"), axis=0, tiled=True),
        lax.all_gather(rounded[10], ("seq", "batch"), axis=0, tiled=True),
        lax.all_gather(rounded[11], ("seq", "batch"), axis=0, tiled=True),
        lax.all_gather(rounded[12], ("seq", "batch"), axis=0, tiled=True),
    )
    (
        triple_low,
        qbias_low,
        vbias_low,
        output_low,
        obias_low,
        gain1_low,
        shift1_low,
        expand_low,
        ebias_low,
        shrink_low,
        sbias_low,
        gain2_low,
        shift2_low,
    ) = fetched
    seq_groups, seq_rows, model_width = inputs.shape
    row_count = seq_groups * seq_rows
    head_count = HEADS
    head_size = HEAD_DIM
    score_scale = HEAD_DIM ** (-0.5)
    full_length = seq_rows * lax.axis_size("seq")
    positions = lax.axis_index("seq") * seq_rows + jnp.arange(seq_rows, dtype=jnp.int32)
    row_valid = positions[None, :] < lengths[:, None]
    flat_inputs = inputs.reshape(row_count, model_width)
    joint_rows = jnp.dot(flat_inputs, triple_low, preferred_element_type=jnp.float32)
    query_rows = (joint_rows[:, :model_width] + qbias_low.astype(jnp.float32)).astype(jnp.bfloat16)
    key_rows = joint_rows[:, model_width : 2 * model_width].astype(jnp.bfloat16)
    value_rows = (joint_rows[:, 2 * model_width :] + vbias_low.astype(jnp.float32)).astype(
        jnp.bfloat16
    )
    query_heads = query_rows.reshape(seq_groups, seq_rows, head_count, head_size)
    key_local = key_rows.reshape(seq_groups, seq_rows, model_width)
    value_local = value_rows.reshape(seq_groups, seq_rows, model_width)
    front_state = (
        jnp.full((seq_groups, head_count, seq_rows), masked_score, jnp.float32),
        jnp.zeros((seq_groups, head_count, seq_rows), jnp.float32),
        jnp.zeros((seq_groups, seq_rows, head_count, head_size), jnp.float32),
    )
    key_piece = lax.all_gather(key_local, "seq", axis=1, tiled=True)
    value_piece = lax.all_gather(value_local, "seq", axis=1, tiled=True)
    piece_rows = key_piece.shape[1]
    step_keys = math.gcd(piece_rows, 512)

    def forward_one_block(block_id, state):
        peak_score, prob_total, value_sum = state
        offset = block_id * step_keys
        key_block = lax.dynamic_slice_in_dim(key_piece, offset, step_keys, 1).reshape(
            seq_groups, step_keys, head_count, head_size
        )
        value_block = lax.dynamic_slice_in_dim(value_piece, offset, step_keys, 1).reshape(
            seq_groups, step_keys, head_count, head_size
        )
        key_pos = offset + jnp.arange(step_keys, dtype=jnp.int32)
        key_valid = (key_pos[None, :] < lengths[:, None])[:, None, None, :]
        scores = (
            jnp.einsum(
                "srhd,skhd->shrk", query_heads, key_block, preferred_element_type=jnp.float32
            )
            * score_scale
        )
        scores = jnp.where(key_valid, scores, masked_score)
        new_peak = jnp.maximum(peak_score, jnp.max(scores, axis=-1))
        rescale = jnp.exp(peak_score - new_peak)
        prob_block = jnp.where(key_valid, jnp.exp(scores - new_peak[..., None]), 0.0)
        prob_total = prob_total * rescale + jnp.sum(prob_block, axis=-1)
        value_sum = value_sum * jnp.transpose(rescale, (0, 2, 1))[..., None] + jnp.einsum(
            "shrk,skhd->srhd",
            prob_block.astype(jnp.bfloat16),
            value_block,
            preferred_element_type=jnp.float32,
        )
        return (new_peak, prob_total, value_sum)

    peak_score, prob_total, value_sum = lax.fori_loop(
        0, piece_rows // step_keys, forward_one_block, front_state
    )
    attended = value_sum / jnp.transpose(prob_total, (0, 2, 1))[..., None]
    log_total = peak_score + jnp.log(prob_total)
    attended_low = attended.reshape(row_count, model_width).astype(jnp.bfloat16)
    branch = jnp.dot(
        attended_low, output_low, preferred_element_type=jnp.float32
    ) + obias_low.astype(jnp.float32)
    resid_first = flat_inputs.astype(jnp.float32) + branch
    hidden, first_pull = jax.vjp(
        layer_norm, resid_first, gain1_low.astype(jnp.float32), shift1_low.astype(jnp.float32)
    )
    hidden_low = hidden.astype(jnp.bfloat16)
    expanded = jnp.dot(
        hidden_low, expand_low, preferred_element_type=jnp.float32
    ) + ebias_low.astype(jnp.float32)
    active, gelu_pull = jax.vjp(partial(jax.nn.gelu, approximate=False), expanded)
    active_low = active.astype(jnp.bfloat16)
    shrunk = jnp.dot(active_low, shrink_low, preferred_element_type=jnp.float32) + sbias_low.astype(
        jnp.float32
    )
    result, second_pull = jax.vjp(
        layer_norm, hidden + shrunk, gain2_low.astype(jnp.float32), shift2_low.astype(jnp.float32)
    )
    output = result.reshape(seq_groups, seq_rows, model_width).astype(jnp.bfloat16)
    row_weight = row_valid.reshape(row_count, 1).astype(jnp.float32)
    seed_grad = cotangent.reshape(row_count, model_width).astype(jnp.float32) * row_weight
    resid_second_grad, grad_gain2, grad_shift2 = second_pull(seed_grad)
    shrunk_grad = resid_second_grad.astype(jnp.bfloat16)
    grad_shrink = jnp.einsum(
        "nf,nd->fd", active_low, shrunk_grad, preferred_element_type=jnp.float32
    )
    grad_sbias = jnp.sum(shrunk_grad.astype(jnp.float32), axis=0)
    active_grad = jnp.einsum(
        "nd,fd->nf", shrunk_grad, shrink_low, preferred_element_type=jnp.float32
    )
    (expanded_grad_full,) = gelu_pull(active_grad)
    expanded_grad = expanded_grad_full.astype(jnp.bfloat16)
    grad_expand = jnp.einsum(
        "nd,nf->df", hidden_low, expanded_grad, preferred_element_type=jnp.float32
    )
    grad_ebias = jnp.sum(expanded_grad.astype(jnp.float32), axis=0)
    hidden_grad = resid_second_grad + jnp.einsum(
        "nf,df->nd", expanded_grad, expand_low, preferred_element_type=jnp.float32
    )
    resid_first_grad, grad_gain1, grad_shift1 = first_pull(hidden_grad)
    branch_grad = resid_first_grad.astype(jnp.bfloat16)
    grad_output = jnp.einsum(
        "na,nd->ad", attended_low, branch_grad, preferred_element_type=jnp.float32
    )
    grad_obias = jnp.sum(branch_grad.astype(jnp.float32), axis=0)
    attended_grad = jnp.einsum(
        "nd,ad->na", branch_grad, output_low, preferred_element_type=jnp.float32
    ).astype(jnp.bfloat16)
    grad_heads = attended_grad.reshape(seq_groups, seq_rows, head_count, head_size)
    delta_rows = jnp.transpose(
        jnp.sum(grad_heads.astype(jnp.float32) * attended, axis=-1), (0, 2, 1)
    )
    query_zero = jnp.zeros((seq_groups, seq_rows, head_count, head_size), jnp.float32)
    back_state = (
        query_zero,
        jnp.zeros((seq_groups, full_length, model_width), jnp.float32),
        jnp.zeros((seq_groups, full_length, model_width), jnp.float32),
    )
    backward_key_piece = lax.all_gather(key_local, "seq", axis=1, tiled=True)
    backward_value_piece = lax.all_gather(value_local, "seq", axis=1, tiled=True)
    piece_rows = backward_key_piece.shape[1]
    backward_step_keys = math.gcd(piece_rows, 512)

    def backward_one_block(block_id, state):
        query_acc, key_acc, value_acc = state
        offset = block_id * backward_step_keys
        key_block = lax.dynamic_slice_in_dim(
            backward_key_piece, offset, backward_step_keys, 1
        ).reshape(seq_groups, backward_step_keys, head_count, head_size)
        value_block = lax.dynamic_slice_in_dim(
            backward_value_piece, offset, backward_step_keys, 1
        ).reshape(seq_groups, backward_step_keys, head_count, head_size)
        key_pos = offset + jnp.arange(backward_step_keys, dtype=jnp.int32)
        key_valid = (key_pos[None, :] < lengths[:, None])[:, None, None, :]
        scores = (
            jnp.einsum(
                "srhd,skhd->shrk", query_heads, key_block, preferred_element_type=jnp.float32
            )
            * score_scale
        )
        prob_block = jnp.where(key_valid, jnp.exp(scores - log_total[..., None]), 0.0)
        prob_grad = jnp.einsum(
            "srhd,skhd->shrk", grad_heads, value_block, preferred_element_type=jnp.float32
        )
        score_grad = (prob_block * (prob_grad - delta_rows[..., None])).astype(jnp.bfloat16)
        query_acc = (
            query_acc
            + jnp.einsum(
                "shrk,skhd->srhd", score_grad, key_block, preferred_element_type=jnp.float32
            )
            * score_scale
        )
        key_part = (
            jnp.einsum(
                "shrk,srhd->skhd", score_grad, query_heads, preferred_element_type=jnp.float32
            )
            * score_scale
        ).reshape(seq_groups, backward_step_keys, model_width)
        value_part = jnp.einsum(
            "shrk,srhd->skhd",
            prob_block.astype(jnp.bfloat16),
            grad_heads,
            preferred_element_type=jnp.float32,
        ).reshape(seq_groups, backward_step_keys, model_width)
        key_acc = lax.dynamic_update_slice_in_dim(key_acc, key_part, offset, 1)
        value_acc = lax.dynamic_update_slice_in_dim(value_acc, value_part, offset, 1)
        return (query_acc, key_acc, value_acc)

    query_grad, key_terms, value_terms = lax.fori_loop(
        0, piece_rows // backward_step_keys, backward_one_block, back_state
    )
    key_grad, value_grad = (
        lax.psum_scatter(
            key_terms.astype(jnp.bfloat16), "seq", scatter_dimension=1, tiled=True
        ).astype(jnp.float32),
        lax.psum_scatter(
            value_terms.astype(jnp.bfloat16), "seq", scatter_dimension=1, tiled=True
        ).astype(jnp.float32),
    )
    query_grad_low = query_grad.reshape(row_count, model_width).astype(jnp.bfloat16)
    key_grad_low = key_grad.reshape(row_count, model_width).astype(jnp.bfloat16)
    value_grad_low = value_grad.reshape(row_count, model_width).astype(jnp.bfloat16)
    joint_grad = jnp.concatenate([query_grad_low, key_grad_low, value_grad_low], axis=1)
    grad_triple = jnp.einsum(
        "nd,nj->dj", flat_inputs, joint_grad, preferred_element_type=jnp.float32
    )
    grad_query = jnp.sum(query_grad_low.astype(jnp.float32), axis=0)
    grad_value = jnp.sum(value_grad_low.astype(jnp.float32), axis=0)
    token_grad = resid_first_grad + jnp.einsum(
        "nj,dj->nd", joint_grad, triple_low, preferred_element_type=jnp.float32
    )
    input_grad = token_grad.reshape(seq_groups, seq_rows, model_width).astype(jnp.bfloat16)
    summed = (
        lax.psum_scatter(grad_triple, ("seq", "batch"), scatter_dimension=0, tiled=True),
        lax.psum_scatter(grad_query, ("seq", "batch"), scatter_dimension=0, tiled=True),
        lax.psum_scatter(grad_value, ("seq", "batch"), scatter_dimension=0, tiled=True),
        lax.psum_scatter(grad_output, ("seq", "batch"), scatter_dimension=0, tiled=True),
        lax.psum_scatter(grad_obias, ("seq", "batch"), scatter_dimension=0, tiled=True),
        lax.psum_scatter(grad_gain1, ("seq", "batch"), scatter_dimension=0, tiled=True),
        lax.psum_scatter(grad_shift1, ("seq", "batch"), scatter_dimension=0, tiled=True),
        lax.psum_scatter(grad_expand, ("seq", "batch"), scatter_dimension=0, tiled=True),
        lax.psum_scatter(grad_ebias, ("seq", "batch"), scatter_dimension=0, tiled=True),
        lax.psum_scatter(grad_shrink, ("seq", "batch"), scatter_dimension=0, tiled=True),
        lax.psum_scatter(grad_sbias, ("seq", "batch"), scatter_dimension=0, tiled=True),
        lax.psum_scatter(grad_gain2, ("seq", "batch"), scatter_dimension=0, tiled=True),
        lax.psum_scatter(grad_shift2, ("seq", "batch"), scatter_dimension=0, tiled=True),
    )
    return (
        output,
        input_grad,
        summed[0],
        summed[1],
        summed[2],
        summed[3],
        summed[4],
        summed[5],
        summed[6],
        summed[7],
        summed[8],
        summed[9],
        summed[10],
        summed[11],
        summed[12],
    )


def solution(mesh):
    in_specs = (
        P("batch", "seq", None),
        P("batch"),
        P("batch", "seq", None),
        P(("seq", "batch"), None),
        P(("seq", "batch")),
        P(("seq", "batch")),
        P(("seq", "batch"), None),
        P(("seq", "batch")),
        P(("seq", "batch")),
        P(("seq", "batch")),
        P(("seq", "batch"), None),
        P(("seq", "batch")),
        P(("seq", "batch"), None),
        P(("seq", "batch")),
        P(("seq", "batch")),
        P(("seq", "batch")),
    )
    out_specs = (
        P("batch", "seq", None),
        P("batch", "seq", None),
        P(("seq", "batch"), None),
        P(("seq", "batch")),
        P(("seq", "batch")),
        P(("seq", "batch"), None),
        P(("seq", "batch")),
        P(("seq", "batch")),
        P(("seq", "batch")),
        P(("seq", "batch"), None),
        P(("seq", "batch")),
        P(("seq", "batch"), None),
        P(("seq", "batch")),
        P(("seq", "batch")),
        P(("seq", "batch")),
    )
    return jax.shard_map(
        per_device, mesh=mesh, in_specs=in_specs, out_specs=out_specs, check_vma=False
    )
```

profile of v0, /device:TPU:0, one launch (start us, length us, event | category | flops | bytes accessed | tf_op | source)
XLA Modules:
  0.0 1249.3 jit_solution(14047409236384904523)
XLA Ops:
  9.0 65.4 %all-gather.9.cloned.1.call-done = bf16[768,2304]{1,0:T(8,128)(2,1)} async-done(((bf16[24,2304]{1,0:T(8,128)(2,1)}), bf16[768,2304]{1,0:T(8,128)(2,1)}) %all-gather.9.cloned.1.call-update) | async-done | bytes 3538960 | tf_op jit(solution)/shard_map/all_gather | solution.py:58
  80.6 40.2 %all-reduce.19 = (bf16[3072]{0:T(1024)(128)(2,1)S(1)}, bf16[768]{0:T(1024)(128)(2,1)S(1)}, bf16[768]{0:T(1024)(128)(2,1)S(1)}, bf16[768]{0:T(1024)(128)(2,1)S(1)...) all-reduce(bf16[3072]{0:T(1024)(128)(2,1)S(1)} %dynamic-update-slic, ...), channel_id=1, replica_groups=mesh['seq'=16,'batch'=2] {'seq','batch'}, use_global_device_ids=true, to_apply=%add.5 | all-reduce | flops 9216 | bytes 36864
  125.2 15.1 %all-gather.17.cloned.1.call-done = bf16[4096,768]{1,0:T(8,128)(2,1)} async-done(((bf16[256,768]{1,0:T(8,128)(2,1)}), bf16[4096,768]{1,0:T(8,128)(2,1)}) %all-gather.17.cloned.1.call-update) | async-done | bytes 6291472 | tf_op jit(solution)/shard_map/all_gather | solution.py:110
  140.2 8.7 copy.51
  148.9 54.7 %all-gather.19.cloned.1.call-done = bf16[4096,768]{1,0:T(8,128)(2,1)} async-done(((bf16[256,768]{1,0:T(8,128)(2,1)}), bf16[4096,768]{1,0:T(8,128)(2,1)}) %all-gather.19.cloned.1.call-update) | async-done | bytes 6291472 | tf_op jit(solution)/shard_map/all_gather | solution.py:111
  203.6 8.8 copy.52
  212.4 101.7 %while.36 = (s32[]{:T(128)}, f32[1,12,256]{2,1,0:T(8,128)S(1)}, f32[1,12,256]{2,1,0:T(8,128)S(1)}, f32[1,256,12,64]{1,3,2,0:T(8,128)S(1)}, s32[1]{0:T(128)}, /*i...) while((s32[]{:T(128)}, f32[1,12,256]{2,1,0:T(8,128)S(1)}, ...), condition=%wide.region_3.4_spmd.clone, body=%wide.region_0.3_spmd.clone.sunk | while | flops 423709696 | bytes 50923740 | solution.py:145
  214.6 4.1 bitcast_reduce_fusion.2
  227.2 4.1 bitcast_reduce_fusion.2
  239.9 4.1 bitcast_reduce_fusion.2
  252.7 4.1 bitcast_reduce_fusion.2
  265.4 4.1 bitcast_reduce_fusion.2
  278.1 4.1 bitcast_reduce_fusion.2
  290.7 4.1 bitcast_reduce_fusion.2
  303.4 4.2 bitcast_reduce_fusion.2
  316.4 9.3 all-gather.13.cloned.1.call-done
  325.7 11.6 multiply_convert_fusion.1
  337.3 54.2 %all-gather.15.cloned.1.call-done = bf16[3072,768]{1,0:T(8,128)(2,1)} async-done(((bf16[96,768]{1,0:T(8,128)(2,1)}), bf16[3072,768]{1,0:T(8,128)(2,1)}) %all-gather.15.cloned.1.call-update) | async-done | bytes 4718608 | tf_op jit(solution)/shard_map/all_gather | solution.py:67
  391.6 4.4 fusion.72
  414.0 143.0 %while.37 = (s32[]{:T(128)}, f32[1,256,12,64]{1,3,2,0:T(8,128)}, bf16[1,4096,768]{1,2,0:T(8,128)(2,1)}, bf16[1,4096,768]{1,2,0:T(8,128)(2,1)}, bf16[1,4096,768]{...) while((s32[]{:T(128)}, f32[1,256,12,64]{1,3,2,0:T(8,128)}, ...), condition=%wide.region_14.15_spmd.clone, body=%wide.region_13.14_spmd.clone.sunk | while | flops 1023738880 | bytes 73377784 | solution.py:260
  496.7 4.1 fusion.137
  560.1 5.4 fusion.65
  567.2 5.4 fusion.74
  573.9 67.3 %reduce-scatter.11.cloned.1.call-done = bf16[1,256,768]{1,2,0:T(8,128)(2,1)} async-done(((bf16[1,4096,768]{1,2,0:T(8,128)(2,1)}), bf16[1,256,768]{1,2,0:T(8,128)(2,1)}) %reduce-scatter.11.cloned.1.call-update) | async-done | bytes 393232 | tf_op jit(solution)/shard_map/reduce_scatter | solution.py:267
  641.2 88.9 %reduce-scatter.9.cloned.1.call-done = bf16[1,256,768]{1,2,0:T(8,128)(2,1)} async-done(((bf16[1,4096,768]{1,2,0:T(8,128)(2,1)}), bf16[1,256,768]{1,2,0:T(8,128)(2,1)}) %reduce-scatter.9.cloned.1.call-update) | async-done | bytes 393232 | tf_op jit(solution)/shard_map/reduce_scatter | solution.py:264
  730.1 5.0 convolution_bitcast_fusion
  735.1 8.0 copy.58
  745.4 41.3 %all-reduce.18 = (f32[768]{0:T(1024)}, f32[768]{0:T(1024)}, f32[768]{0:T(1024)}, f32[768]{0:T(1024)}, f32[768]{0:T(1024)}, /*index=5*/f32[3072]{0:T(1024)}, f32[768]{0:T(1024)}, f32[768]{0:T(1024)}, f32[768]{0:T(1024)S(1)}) all-reduce(f32[768]{0:T(1024)} %reduce_sum.222, ...), channel_id=7, replica_groups=mesh['seq'=16,'batch'=2] {'seq','batch'}, use_global_device_ids=true, to_apply=%region_19.20.clone | all-reduce | flops 9216 | bytes 73728
  800.7 33.6 %reduce-scatter.13.cloned.1.call-done = f32[24,768]{1,0:T(8,128)} async-done(((f32[768,768]{1,0:T(8,128)}), f32[24,768]{1,0:T(8,128)}) %reduce-scatter.13.cloned.1.call-update) | async-done | bytes 73744 | tf_op jit(solution)/shard_map/reduce_scatter | solution.py:288
  834.3 141.9 %reduce-scatter.15.cloned.1.call-done = f32[24,3072]{1,0:T(8,128)} async-done(((f32[768,3072]{1,0:T(8,128)}), f32[24,3072]{1,0:T(8,128)}) %reduce-scatter.15.cloned.1.call-update) | async-done | bytes 294928 | tf_op jit(solution)/shard_map/reduce_scatter | solution.py:292
  976.3 141.0 %reduce-scatter.17.cloned.1.call-done = f32[96,768]{1,0:T(8,128)} async-done(((f32[3072,768]{1,0:T(8,128)}), f32[96,768]{1,0:T(8,128)}) %reduce-scatter.17.cloned.1.call-update) | async-done | bytes 294928 | tf_op jit(solution)/shard_map/reduce_scatter | solution.py:294
  1117.3 125.2 %reduce-scatter.19.cloned.1.call-done = f32[24,2304]{1,0:T(8,128)} async-done(((f32[768,2304]{1,0:T(8,128)}), f32[24,2304]{1,0:T(8,128)}) %reduce-scatter.19.cloned.1.call-update) | async-done | bytes 221200
  (500 shorter events, 259.3 us)
Async XLA Ops:
  7.2 67.2 %all-gather.9.cloned.1.call-start = ((), (), s32[]{:S(2)}) async-start(), calls=%async_computation.6 | async-start | bytes 3649536 | tf_op jit(solution)/shard_map/all_gather | solution.py:58
  8.8 69.7 %copy-start.35 = (f32[96]{0:T(128)S(1)}, f32[96]{0:T(128)}, u32[]{:S(2)}) copy-start(f32[96]{0:T(128)} %param.31) | copy-start | bytes 1156
  8.9 69.7 %copy-start.36 = (f32[24]{0:T(128)S(1)}, f32[24]{0:T(128)}, u32[]{:S(2)}) copy-start(f32[24]{0:T(128)} %param.24) | copy-start | bytes 292
  8.9 69.7 %copy-start.37 = (f32[24]{0:T(128)S(1)}, f32[24]{0:T(128)}, u32[]{:S(2)}) copy-start(f32[24]{0:T(128)} %param.25) | copy-start | bytes 292
  8.9 69.7 %copy-start.38 = (f32[24]{0:T(128)S(1)}, f32[24]{0:T(128)}, u32[]{:S(2)}) copy-start(f32[24]{0:T(128)} %param.27) | copy-start | bytes 292
  8.9 69.8 %copy-start.39 = (f32[24]{0:T(128)S(1)}, f32[24]{0:T(128)}, u32[]{:S(2)}) copy-start(f32[24]{0:T(128)} %param.29) | copy-start | bytes 292
  8.9 69.8 %copy-start.40 = (f32[24]{0:T(128)S(1)}, f32[24]{0:T(128)}, u32[]{:S(2)}) copy-start(f32[24]{0:T(128)} %param.28) | copy-start | bytes 292
  8.9 69.8 %copy-start.41 = (f32[24]{0:T(128)S(1)}, f32[24]{0:T(128)}, u32[]{:S(2)}) copy-start(f32[24]{0:T(128)} %param.33) | copy-start | bytes 292
  8.9 69.8 %copy-start.42 = (f32[24]{0:T(128)S(1)}, f32[24]{0:T(128)}, u32[]{:S(2)}) copy-start(f32[24]{0:T(128)} %param.35) | copy-start | bytes 292
  8.9 69.8 %copy-start.43 = (f32[24]{0:T(128)S(1)}, f32[24]{0:T(128)}, u32[]{:S(2)}) copy-start(f32[24]{0:T(128)} %param.34) | copy-start | bytes 292
  9.0 131.3 %all-gather.17.cloned.1.call-start = ((), (), s32[]{:S(2)}) async-start(), calls=%async_computation.15 | async-start | bytes 6684672 | tf_op jit(solution)/shard_map/all_gather | solution.py:110
  77.6 44.1 %copy-start.26 = (f32[24,768]{1,0:T(8,128)S(1)}, f32[24,768]{1,0:T(8,128)}, u32[]{:S(2)}) copy-start(f32[24,768]{1,0:T(8,128)} %param.26) | copy-start | bytes 221188
  77.7 44.8 %copy-start.24 = (f32[24,3072]{1,0:T(8,128)S(1)}, f32[24,3072]{1,0:T(8,128)}, u32[]{:S(2)}) copy-start(f32[24,3072]{1,0:T(8,128)} %param.30) | copy-start | bytes 884740
  77.7 45.6 %copy-start.25 = (f32[96,768]{1,0:T(8,128)S(1)}, f32[96,768]{1,0:T(8,128)}, u32[]{:S(2)}) copy-start(f32[96,768]{1,0:T(8,128)} %param.32) | copy-start | bytes 884740
  78.5 125.1 %all-gather.19.cloned.1.call-start = ((), (), s32[]{:S(2)}) async-start(), calls=%async_computation.16 | async-start | bytes 6684672 | tf_op jit(solution)/shard_map/all_gather | solution.py:111
  121.7 192.5 %all-gather.11.cloned.1.call-start = ((), (), s32[]{:S(2)}) async-start(), calls=%async_computation.7 | async-start | bytes 1216512 | tf_op jit(solution)/shard_map/all_gather | solution.py:61
  122.4 203.3 %all-gather.13.cloned.1.call-start = ((), (), s32[]{:S(2)}) async-start(), calls=%async_computation.8 | async-start | bytes 4866048 | tf_op jit(solution)/shard_map/all_gather | solution.py:65
  123.2 268.3 %all-gather.15.cloned.1.call-start = ((), (), s32[]{:S(2)}) async-start(), calls=%async_computation.9 | async-start | bytes 4866048 | tf_op jit(solution)/shard_map/all_gather | solution.py:67
  124.0 517.2 %reduce-scatter.11.cloned.1.call-start = ((), (), s32[]{:S(2)}) async-start(), calls=%async_computation.11 | async-start | bytes 6684672 | tf_op jit(solution)/shard_map/reduce_scatter | solution.py:267
  212.4 101.8 %copy-start.7 = (bf16[1,256,768]{2,1,0:T(8,128)(2,1)S(1)}, bf16[1,256,768]{2,1,0:T(8,128)(2,1)}, u32[]{:S(2)}) copy-start(bf16[1,256,768]{2,1,0:T(8,128)(2,1)} %param.20) | copy-start | bytes 1179652
  314.2 23.2 %copy-start.10 = (bf16[1,256,12,64]{1,3,2,0:T(8,128)(2,1)}, bf16[1,256,12,64]{1,3,2,0:T(8,128)(2,1)S(1)}, u32[]{:S(2)}) copy-start(bf16[1,256,12,64]{1,3,2,0:T(8,128)(2,1)S(1)} %fusion.60) | copy-start | bytes 1179652
  316.2 88.0 %copy-start.4 = (f32[256,768]{1,0:T(8,128)}, f32[256,768]{1,0:T(8,128)S(1)}, u32[]{:S(2)}) copy-start(f32[256,768]{1,0:T(8,128)S(1)} %get-tuple-element.601) | copy-start | bytes 2359300
  316.4 87.8 %copy-start.32 = (f32[256]{0:T(256)}, f32[256]{0:T(256)S(1)}, u32[]{:S(2)}) copy-start(f32[256]{0:T(256)S(1)} %fusion.61) | copy-start | bytes 3076
  391.6 7.6 slice-start.2
  557.0 173.1 %reduce-scatter.9.cloned.1.call-start = ((), (), s32[]{:S(2)}) async-start(), calls=%async_computation.10 | async-start | bytes 6684672 | tf_op jit(solution)/shard_map/reduce_scatter | solution.py:264
  557.8 276.6 %reduce-scatter.13.cloned.1.call-start = ((), (), s32[]{:S(2)}) async-start(), calls=%async_computation.12 | async-start | bytes 2433024 | tf_op jit(solution)/shard_map/reduce_scatter | solution.py:288
  560.0 416.3 %reduce-scatter.15.cloned.1.call-start = ((), (), s32[]{:S(2)}) async-start(), calls=%async_computation.13 | async-start | bytes 9732096 | tf_op jit(solution)/shard_map/reduce_scatter | solution.py:292
  565.6 551.8 %reduce-scatter.17.cloned.1.call-start = ((), (), s32[]{:S(2)}) async-start(), calls=%async_computation.14 | async-start | bytes 9732096 | tf_op jit(solution)/shard_map/reduce_scatter | solution.py:294
  572.5 157.6 %copy-start.8 = (bf16[1,256,768]{2,1,0:T(8,128)(2,1)S(1)}, bf16[1,256,768]{2,1,0:T(8,128)(2,1)}, u32[]{:S(2)}) copy-start(bf16[1,256,768]{2,1,0:T(8,128)(2,1)} %param.20) | copy-start | bytes 1179652
  572.6 669.9 %reduce-scatter.19.cloned.1.call-start = ((), (), s32[]{:S(2)}) async-start(), calls=%async_computation.17 | async-start | bytes 7299072
  573.9 161.2 %copy-start.18 = (bf16[1,256,12,64]{1,3,2,0:T(8,128)(2,1)}, bf16[1,256,12,64]{1,3,2,0:T(8,128)(2,1)S(1)}, u32[]{:S(2)}) copy-start(bf16[1,256,12,64]{1,3,2,0:T(8,128)(2,1)S(1)} %get-tuple-element.584) | copy-start | bytes 1179652
  743.1 54.2 %copy-start.9 = (bf16[768,2304]{1,0:T(8,128)(2,1)S(1)}, bf16[768,2304]{1,0:T(8,128)(2,1)}, u32[]{:S(2)}) copy-start(bf16[768,2304]{1,0:T(8,128)(2,1)} %all-gather.9.cloned.1.call-done) | copy-start | bytes 10616836
  (109 other events, 310.8 us)
Sparse Core Ops, SparseCore 0:
  11.5 62.8 all-gather.8
  78.6 61.5 all-gather.16
  143.1 60.4 all-gather.18
  206.9 52.7 all-gather.10
  263.0 62.6 all-gather.12
  329.1 62.4 all-gather.14
  557.1 84.0 reduce-scatter.10
  645.6 84.4 reduce-scatter.8
  735.9 98.3 reduce-scatter.12
  841.7 134.5 reduce-scatter.14
  982.8 134.5 reduce-scatter.16
  1124.4 118.0 reduce-scatter.18
where the time goes:
time: 1250 us
  waiting for transfers between devices  797 us (64%)
  matrix products  194 us (16%)
  local copies, waits for them, and re-layouts  105 us (8%)
  blocking collectives  81.5 us (7%)
  other arithmetic  53 us (4%)
  between operations  15.6 us (1%)
    reduce_scatter x1, waiting for transfers between devices, per_device(): lax.psum_scatter(grad_expand, ('seq', 'batch'), scatter_dimension=0, tile...  142 us
    reduce_scatter x1, waiting for transfers between devices, per_device(): lax.psum_scatter(grad_shrink, ('seq', 'batch'), scatter_dimension=0, tile...  141 us
    unnamed x13, waiting for transfers between devices  126 us
    reduce_scatter x1, waiting for transfers between devices, per_device(): lax.psum_scatter(key_terms.astype(jnp.bfloat16), 'seq', scatter_dimension...  88.9 us
    unnamed x2, blocking collectives  81.5 us
    reduce_scatter x1, waiting for transfers between devices, per_device(): lax.psum_scatter(value_terms.astype(jnp.bfloat16), 'seq', scatter_dimensi...  67.3 us
    all_gather x1, waiting for transfers between devices, per_device(): lax.all_gather(rounded[0], ('seq', 'batch'), axis=0, tiled=True)  65.4 us
    all_gather x1, waiting for transfers between devices, per_device(): value_piece = lax.all_gather(value_local, 'seq', axis=1, tiled=True)  54.7 us
  transfers between devices with their start and end apart: 12, of which 11 were waited for; matrix products, arithmetic and copies ran while one was open for 14% of the time, Pallas kernels for 0%

commit v1 on v0

v1 whole, which is shorter than its diff:
```python
from functools import partial

import jax
import jax.numpy as jnp
from jax import lax
from jax.experimental import pallas as pl
from jax.experimental.pallas import tpu as pltpu
from jax.sharding import Mesh, PartitionSpec as P

HEADS = 12
HEAD_DIM = 64
GROUPS = 4
OWN_HEADS = HEADS // GROUPS
OWN_WIDTH = OWN_HEADS * HEAD_DIM
LANES = 128

bf16 = jnp.bfloat16
f32 = jnp.float32
masked_score = -1e30
norm_eps = 1e-12
log2_e = 1.4426950408889634
CONTRACT_LAST = (((1,), (1,)), ((), ()))
VMEM_BYTES = 60 * 1024 * 1024
AXES = ("q", "x", "c", "b")


def layer_norm(row_block, norm_gain, norm_shift):
    center = row_block - jnp.mean(row_block, axis=-1, keepdims=True)
    spread = jnp.mean(center * center, axis=-1, keepdims=True)
    return center * lax.rsqrt(spread + norm_eps) * norm_gain + norm_shift


def split_three(value):
    high = value.astype(bf16).astype(f32)
    rest = value - high
    mid = rest.astype(bf16).astype(f32)
    low = (rest - mid).astype(bf16).astype(f32)
    return high, mid, low


def forward_kernel(first, last, block_q, block_k, *refs):
    refs = list(refs)
    where_ref = refs.pop(0)
    pieces = [refs.pop(0) for _ in range(4)]
    wk_ref, wv_ref, vb_ref = [refs.pop(0) for _ in range(3)]
    if first:
        wq_ref, qb_ref = [refs.pop(0) for _ in range(2)]
    else:
        qx_ref, peak_in, sum_in = [refs.pop(0) for _ in range(3)]
    kx_ref, vx_ref = [refs.pop(0) for _ in range(2)]
    if first:
        qx_ref, qp_ref = [refs.pop(0) for _ in range(2)]
    if last:
        att_ref, attx_ref, qx2_ref = [refs.pop(0) for _ in range(3)]
    else:
        peak_out, sum_out = [refs.pop(0) for _ in range(2)]
    (vt_ref,) = refs
    piece_rows = pieces[0].shape[0]
    rows_in = 4 * piece_rows
    lane = lax.broadcasted_iota(jnp.int32, (piece_rows, LANES), 1)
    row = lax.broadcasted_iota(jnp.int32, (piece_rows, LANES), 0)
    length = where_ref[4]
    three = (lane >= HEAD_DIM) & (lane < HEAD_DIM + 3)
    for p in range(4):
        rows = slice(p * piece_rows, (p + 1) * piece_rows)
        x = pieces[p][...]
        keys = jnp.dot(x, wk_ref[...], preferred_element_type=f32)
        values = jnp.dot(x, wv_ref[...], preferred_element_type=f32) + vb_ref[...]
        bias = jnp.where(where_ref[p] + row < length, 0.0, masked_score)
        key_extra = jnp.where(three, 1.0, jnp.where(lane == HEAD_DIM + 3, bias, 0.0))
        if first:
            queries = jnp.dot(x, wq_ref[...], preferred_element_type=f32) + qb_ref[...]
        for h in range(OWN_HEADS):
            cols = slice(h * LANES, (h + 1) * LANES)
            k = keys[:, cols]
            kx_ref[h, rows, :LANES] = (k + pltpu.roll(k, HEAD_DIM, 1)).astype(bf16)
            kx_ref[h, rows, LANES:] = (k + key_extra).astype(bf16)
            v = values[:, cols]
            vx_ref[h, rows, :] = jnp.where(three, -1.0, v).astype(bf16)
            vt = jnp.where(lane == HEAD_DIM, 1.0, v).T
            vt_ref[h, :, rows] = vt[:80].astype(bf16)
            if first:
                q = queries[:, cols].astype(bf16).astype(f32)
                qp_ref[h, rows, :] = q.astype(bf16)
                high, mid, low = split_three(q * (HEAD_DIM**-0.5 * log2_e))
                qx_ref[h, rows, :LANES] = (high + pltpu.roll(mid, HEAD_DIM, 1)).astype(bf16)
                qx_ref[h, rows, LANES:] = jnp.where(lane == HEAD_DIM + 3, 1.0, low).astype(bf16)
    for h in range(OWN_HEADS):
        for i in range(rows_in // block_q):
            cols = slice(i * block_q, (i + 1) * block_q)
            q = qx_ref[h, cols, :]
            if first:
                peak = jnp.full((1, block_q), masked_score, f32)
                total = jnp.zeros((80, block_q), f32)
            else:
                peak = peak_in[h, :1, cols]
                total = sum_in[h, :, cols]
            for j in range(rows_in // block_k):
                ks = slice(j * block_k, (j + 1) * block_k)
                s = lax.dot_general(kx_ref[h, ks, :], q, CONTRACT_LAST, preferred_element_type=f32)
                new_peak = jnp.maximum(peak, jnp.max(s, axis=0, keepdims=True))
                prob = jnp.exp2(s - new_peak).astype(bf16)
                total = total * jnp.exp2(peak - new_peak) + jnp.dot(
                    vt_ref[h, :, ks], prob, preferred_element_type=f32
                )
                peak = new_peak
            if last:
                denom = total[HEAD_DIM : HEAD_DIM + 1]
                n_high, n_mid, n_low = split_three(-(peak + jnp.log2(denom)))
                tall = jnp.concatenate(
                    [
                        total[:HEAD_DIM] / denom,
                        n_high,
                        n_mid,
                        n_low,
                        jnp.zeros((HEAD_DIM - 3, block_q), f32),
                    ],
                    axis=0,
                )
                attx_ref[h, cols, :] = tall.T
            else:
                peak_out[h, :, cols] = jnp.broadcast_to(peak, (8, block_q))
                sum_out[h, :, cols] = total
    if last:
        lane_all = lax.broadcasted_iota(jnp.int32, (rows_in, LANES), 1)
        heads = [jnp.where(lane_all < HEAD_DIM, attx_ref[h], 0.0) for h in range(OWN_HEADS)]
        att_ref[:, :LANES] = (heads[0] + pltpu.roll(heads[1], HEAD_DIM, 1)).astype(bf16)
        att_ref[:, LANES:] = heads[2][:, :HEAD_DIM].astype(bf16)
        mark = (lane_all >= HEAD_DIM) & (lane_all < HEAD_DIM + 3)
        for h in range(OWN_HEADS):
            qx2_ref[h, :, :LANES] = qx_ref[h, :, :LANES]
            qx2_ref[h, :, LANES:] = jnp.where(
                mark, attx_ref[h], qx_ref[h, :, LANES:].astype(f32)
            ).astype(bf16)


def vmem_specs(n):
    return [pl.BlockSpec(memory_space=pltpu.VMEM) for _ in range(n)]


def attend_chunk(first, last, where, pieces, weights, carry):
    rows = 4 * pieces[0].shape[0]
    wk, wv, vb, wq, qb = weights
    operands = [where, *pieces, wk, wv, vb]
    operands += [wq, qb] if first else list(carry)
    out_shape = [
        jax.ShapeDtypeStruct((OWN_HEADS, rows, 2 * LANES), bf16),
        jax.ShapeDtypeStruct((OWN_HEADS, rows, LANES), bf16),
    ]
    if first:
        out_shape += [
            jax.ShapeDtypeStruct((OWN_HEADS, rows, 2 * LANES), bf16),
            jax.ShapeDtypeStruct((OWN_HEADS, rows, LANES), bf16),
        ]
    if last:
        out_shape += [
            jax.ShapeDtypeStruct((rows, OWN_WIDTH), bf16),
            jax.ShapeDtypeStruct((OWN_HEADS, rows, LANES), f32),
            jax.ShapeDtypeStruct((OWN_HEADS, rows, 2 * LANES), bf16),
        ]
    else:
        out_shape += [
            jax.ShapeDtypeStruct((OWN_HEADS, 8, rows), f32),
            jax.ShapeDtypeStruct((OWN_HEADS, 80, rows), f32),
        ]
    return pl.pallas_call(
        partial(forward_kernel, first, last, min(512, rows), min(1024, rows)),
        out_shape=out_shape,
        in_specs=[pl.BlockSpec(memory_space=pltpu.SMEM)] + vmem_specs(len(operands) - 1),
        out_specs=vmem_specs(len(out_shape)),
        scratch_shapes=[pltpu.VMEM((OWN_HEADS, 80, rows), bf16)],
        compiler_params=pltpu.CompilerParams(vmem_limit_bytes=VMEM_BYTES),
        cost_estimate=pl.CostEstimate(
            flops=int(8e9), transcendentals=OWN_HEADS * rows * rows, bytes_accessed=int(1e7)
        ),
        name="attend_forward",
    )(*operands)


def backward_kernel(first, last, block_q, block_k, *refs):
    refs = list(refs)
    kx_ref, vx_ref, qx_ref, qp_ref, wk_ref, wv_ref = [refs.pop(0) for _ in range(6)]
    if first:
        pieces = [refs.pop(0) for _ in range(4)]
        attx_ref = refs.pop(0)
    else:
        dox_ref, dqt_in = [refs.pop(0) for _ in range(2)]
    if last:
        wq_ref = refs.pop(0)
    dkv_ref, dx_ref = [refs.pop(0) for _ in range(2)]
    if first:
        dox_ref = refs.pop(0)
    if last:
        dq_ref = refs.pop(0)
        dqt_ref = refs.pop()
    else:
        dqt_ref = refs.pop(0)
    (kt_ref,) = refs
    rows_in = kx_ref.shape[1]
    scale = HEAD_DIM**-0.5
    if first:
        piece_rows = pieces[0].shape[0]
        lane = lax.broadcasted_iota(jnp.int32, (piece_rows, LANES), 1)
        for p in range(4):
            rows = slice(p * piece_rows, (p + 1) * piece_rows)
            left = pieces[p][:, :LANES].astype(f32)
            right = pieces[p][:, LANES:].astype(f32)
            right = jnp.concatenate([right, jnp.zeros_like(right)], axis=1)
            for h, wide in enumerate((left, pltpu.roll(left, HEAD_DIM, 1), right)):
                grad = jnp.where(lane < HEAD_DIM, wide, 0.0)
                delta = jnp.sum(grad * attx_ref[h, rows, :], axis=1, keepdims=True)
                d_high, d_mid, d_low = split_three(delta)
                grad = jnp.where(lane == HEAD_DIM, d_high, grad)
                grad = jnp.where(lane == HEAD_DIM + 1, d_mid, grad)
                grad = jnp.where(lane == HEAD_DIM + 2, d_low, grad)
                dox_ref[h, rows, :] = grad.astype(bf16)
        dqt_ref[...] = jnp.zeros_like(dqt_ref)
    else:
        dqt_ref[...] = dqt_in[...]
    for h in range(OWN_HEADS):
        kt_ref[h] = kx_ref[h, :, LANES:].astype(f32).T[:HEAD_DIM].astype(bf16)
    for h in range(OWN_HEADS):
        for j in range(rows_in // block_k):
            ks = slice(j * block_k, (j + 1) * block_k)
            k = kx_ref[h, ks, :]
            v = vx_ref[h, ks, :]
            kt = kt_ref[h, :, ks]
            dk = jnp.zeros((block_k, LANES), f32)
            dv = jnp.zeros((block_k, LANES), f32)
            for i in range(rows_in // block_q):
                qs = slice(i * block_q, (i + 1) * block_q)
                s = lax.dot_general(k, qx_ref[h, qs, :], CONTRACT_LAST, preferred_element_type=f32)
                prob = jnp.exp2(s)
                do = dox_ref[h, qs, :]
                dp = lax.dot_general(v, do, CONTRACT_LAST, preferred_element_type=f32)
                ds = (prob * dp).astype(bf16)
                dv = dv + jnp.dot(prob.astype(bf16), do, preferred_element_type=f32)
                dk = dk + jnp.dot(ds, qp_ref[h, qs, :], preferred_element_type=f32)
                dqt_ref[h, :, qs] += jnp.dot(kt, ds, preferred_element_type=f32)
            dkv_ref[ks, h * LANES : (h + 1) * LANES] = (dk * scale).astype(bf16)
            cols = slice((OWN_HEADS + h) * LANES, (OWN_HEADS + h + 1) * LANES)
            dkv_ref[ks, cols] = dv.astype(bf16)
    wide = OWN_HEADS * LANES
    if last:
        for h in range(OWN_HEADS):
            dqt = dqt_ref[h] * scale
            dqt = jnp.concatenate([dqt, jnp.zeros_like(dqt)], axis=0)
            dq_ref[:, h * LANES : (h + 1) * LANES] = dqt.T.astype(bf16)
    for j in range(rows_in // block_k):
        ks = slice(j * block_k, (j + 1) * block_k)
        dx = lax.dot_general(
            dkv_ref[ks, :wide], wk_ref[...], CONTRACT_LAST, preferred_element_type=f32
        )
        dx = dx + lax.dot_general(
            dkv_ref[ks, wide:], wv_ref[...], CONTRACT_LAST, preferred_element_type=f32
        )
        if last:
            dx = dx + lax.dot_general(
                dq_ref[ks, :], wq_ref[...], CONTRACT_LAST, preferred_element_type=f32
            )
        dx_ref[ks, :] = dx.astype(bf16)


def attend_back_chunk(first, last, chunk, shared, carry):
    kx, vx = chunk
    qx2, qp, wk, wv, wq, grads, attx = shared
    rows, width = kx.shape[1], wk.shape[0]
    operands = [kx, vx, qx2, qp, wk, wv]
    operands += [*grads, attx] if first else list(carry)
    if last:
        operands.append(wq)
    out_shape = [
        jax.ShapeDtypeStruct((rows, 2 * OWN_HEADS * LANES), bf16),
        jax.ShapeDtypeStruct((rows, width), bf16),
    ]
    if first:
        out_shape.append(jax.ShapeDtypeStruct((OWN_HEADS, rows, LANES), bf16))
    scratch = [pltpu.VMEM((OWN_HEADS, HEAD_DIM, rows), bf16)]
    if last:
        out_shape.append(jax.ShapeDtypeStruct((rows, OWN_HEADS * LANES), bf16))
        scratch.append(pltpu.VMEM((OWN_HEADS, HEAD_DIM, rows), f32))
    else:
        out_shape.append(jax.ShapeDtypeStruct((OWN_HEADS, HEAD_DIM, rows), f32))
    return pl.pallas_call(
        partial(backward_kernel, first, last, min(512, rows), min(512, rows)),
        out_shape=out_shape,
        in_specs=vmem_specs(len(operands)),
        out_specs=vmem_specs(len(out_shape)),
        scratch_shapes=scratch,
        compiler_params=pltpu.CompilerParams(vmem_limit_bytes=VMEM_BYTES),
        cost_estimate=pl.CostEstimate(
            flops=int(1.5e10), transcendentals=OWN_HEADS * rows * rows, bytes_accessed=int(1e7)
        ),
        name="attend_backward",
    )(*operands)


def from_shift(value, axis, count, step):
    return lax.ppermute(value, axis, [((i + step) % count, i) for i in range(count)])


def square_swap(value, r):
    if r == 0:
        return value
    if r == 1:
        return lax.ppermute(value, "c", [(0, 1), (1, 0)])
    if r == 2:
        return lax.ppermute(value, "x", [(0, 1), (1, 0)])
    return lax.ppermute(value, ("x", "c"), [(0, 3), (3, 0), (1, 2), (2, 1)])


def pick(stacked, index):
    return lax.dynamic_index_in_dim(stacked, index, 0, keepdims=False)


def pad_heads(matrix):
    lead = matrix.shape[:-1]
    heads = matrix.reshape(*lead, OWN_HEADS, HEAD_DIM)
    pad = [(0, 0)] * len(lead) + [(0, 0), (0, LANES - HEAD_DIM)]
    return jnp.pad(heads, pad).reshape(*lead, OWN_HEADS * LANES)


def per_device(
    n_q,
    n_b,
    inputs,
    lengths,
    cotangent,
    triple_weight,
    query_bias,
    value_bias,
    output_weight,
    output_bias,
    first_gain,
    first_shift,
    expand_weight,
    expand_bias,
    shrink_weight,
    shrink_bias,
    second_gain,
    second_shift,
):
    zi, xi, ci, bi = [lax.axis_index(a) for a in AXES]
    group = 2 * xi + ci
    _, seq_rows, width = inputs.shape
    own_rows = triple_weight.shape[0]
    ff = expand_weight.shape[1]
    own_ff = shrink_weight.shape[0]
    n_dev = 4 * n_q * n_b
    x_own = inputs[0]

    fold = ff // width
    packed = jnp.concatenate(
        [
            output_weight.astype(bf16),
            expand_weight.astype(bf16)
            .reshape(own_rows, fold, width)
            .transpose(1, 0, 2)
            .reshape(fold * own_rows, width),
            shrink_weight.astype(bf16),
        ],
        axis=0,
    )

    thirds = triple_weight.astype(bf16).reshape(own_rows, 3, GROUPS, OWN_WIDTH)
    thirds = thirds.transpose(2, 1, 0, 3).reshape(GROUPS, 3 * own_rows, OWN_WIDTH)
    small = jnp.concatenate(
        [
            query_bias,
            value_bias,
            output_bias,
            first_gain,
            first_shift,
            shrink_bias,
            second_gain,
            second_shift,
            expand_bias,
        ]
    ).astype(bf16)
    small_size = small.shape[0]
    small_rows = -(-small_size // OWN_WIDTH)
    small = jnp.pad(small, (0, small_rows * OWN_WIDTH - small_size)).reshape(small_rows, OWN_WIDTH)
    parts = []
    for r in range(4):
        block = jnp.concatenate([pick(thirds, group ^ r), small], axis=0)
        parts.append(square_swap(block, r))
    square = jnp.stack(parts)
    square = jnp.stack([pick(square, group ^ g) for g in range(4)])
    rows_b = jnp.stack([square] + [from_shift(square, "b", n_b, j) for j in range(1, n_b)])
    rows_q = jnp.stack([rows_b] + [from_shift(rows_b, "q", n_q, j) for j in range(1, n_q)])
    rows_q = jnp.stack([pick(rows_q, (i - zi) % n_q) for i in range(n_q)])
    gathered = jnp.stack(
        [lax.dynamic_index_in_dim(rows_q, (i - bi) % n_b, 1, keepdims=False) for i in range(n_b)],
        axis=1,
    )
    gathered = gathered.transpose(0, 2, 1, 3, 4).reshape(n_dev, -1, OWN_WIDTH)
    joint = gathered[:, : 3 * own_rows].reshape(n_dev, 3, own_rows, OWN_WIDTH)
    joint = joint.transpose(1, 0, 2, 3).reshape(3, width, OWN_WIDTH)
    wq, wk, wv = [pad_heads(joint[i]) for i in range(3)]
    smalls = gathered[:, 3 * own_rows :].reshape(n_dev, -1)[:, :small_size].astype(f32)

    def small_vector(i):
        return smalls[:, i * own_rows : (i + 1) * own_rows].reshape(1, width)

    qbias, vbias, obias, gain1, shift1, sbias, gain2, shift2 = [small_vector(i) for i in range(8)]
    ebias = smalls[:, 8 * own_rows :].reshape(1, ff)
    qb = pad_heads(lax.dynamic_slice_in_dim(qbias, group * OWN_WIDTH, OWN_WIDTH, 1))
    vb = pad_heads(lax.dynamic_slice_in_dim(vbias, group * OWN_WIDTH, OWN_WIDTH, 1))

    chunk_x = []
    for j in range(n_q):
        own = x_own if j == 0 else from_shift(x_own, "q", n_q, j)
        other = square_swap(own, 2)
        chunk_x.append([own, square_swap(own, 1), other, square_swap(other, 1)])

    gathered_ffn = lax.all_gather(packed, AXES, axis=0, tiled=False)

    def where_of(j):
        zj = (zi + j) % n_q
        spots = [(zj * 4 + (group ^ r)) * seq_rows for r in range(4)]
        return jnp.stack(spots + [lengths[0]]).astype(jnp.int32)

    weights = (wk, wv, vb, wq, qb)
    kept = []
    carry = None
    for j in range(n_q):
        first, last = j == 0, j == n_q - 1
        outs = attend_chunk(first, last, where_of(j), chunk_x[j], weights, carry)
        kept.append((outs[0], outs[1]))
        outs = outs[2:]
        if first:
            qx, qp = outs[:2]
            outs = outs[2:]
        carry = (qx, *outs)
    _, att, attx, qx2 = carry

    blocks = jnp.stack(
        [square_swap(att[r * seq_rows : (r + 1) * seq_rows], r) for r in range(4)]
    )
    attended_low = jnp.concatenate([pick(blocks, group ^ g) for g in range(4)], axis=1)

    output_low = gathered_ffn[:, :own_rows].reshape(width, width)
    expand_low = gathered_ffn[:, own_rows : (1 + fold) * own_rows]
    expand_low = (
        expand_low.reshape(n_dev, fold, own_rows, width).transpose(0, 2, 1, 3).reshape(width, ff)
    )
    shrink_low = gathered_ffn[:, (1 + fold) * own_rows :].reshape(ff, width)
    branch = jnp.dot(attended_low, output_low, preferred_element_type=f32) + obias
    resid_first = x_own.astype(f32) + branch
    hidden, first_pull = jax.vjp(layer_norm, resid_first, gain1[0], shift1[0])
    hidden_low = hidden.astype(bf16)
    expanded = jnp.dot(hidden_low, expand_low, preferred_element_type=f32) + ebias
    active, gelu_pull = jax.vjp(partial(jax.nn.gelu, approximate=False), expanded)
    active_low = active.astype(bf16)
    shrunk = jnp.dot(active_low, shrink_low, preferred_element_type=f32) + sbias
    result, second_pull = jax.vjp(layer_norm, hidden + shrunk, gain2[0], shift2[0])
    output = result[None].astype(bf16)
    positions = (zi * 4 + group) * seq_rows + jnp.arange(seq_rows, dtype=jnp.int32)
    row_weight = (positions < lengths[0]).astype(f32)[:, None]
    seed_grad = cotangent[0].astype(f32) * row_weight
    resid_second_grad, grad_gain2, grad_shift2 = second_pull(seed_grad)
    shrunk_grad = resid_second_grad.astype(bf16)
    grad_shrink = jnp.einsum("nf,nd->fd", active_low, shrunk_grad, preferred_element_type=f32)
    grad_sbias = jnp.sum(shrunk_grad.astype(f32), axis=0)
    active_grad = jnp.einsum("nd,fd->nf", shrunk_grad, shrink_low, preferred_element_type=f32)
    (expanded_grad_full,) = gelu_pull(active_grad)
    expanded_grad = expanded_grad_full.astype(bf16)
    grad_expand = jnp.einsum("nd,nf->df", hidden_low, expanded_grad, preferred_element_type=f32)
    grad_ebias = jnp.sum(expanded_grad.astype(f32), axis=0)
    hidden_grad = resid_second_grad + jnp.einsum(
        "nf,df->nd", expanded_grad, expand_low, preferred_element_type=f32
    )
    resid_first_grad, grad_gain1, grad_shift1 = first_pull(hidden_grad)
    branch_grad = resid_first_grad.astype(bf16)
    grad_output = jnp.einsum("na,nd->ad", attended_low, branch_grad, preferred_element_type=f32)
    grad_obias = jnp.sum(branch_grad.astype(f32), axis=0)
    attended_grad = jnp.einsum(
        "nd,ad->na", branch_grad, output_low, preferred_element_type=f32
    ).astype(bf16)

    grad_packed = jnp.concatenate(
        [
            grad_output.astype(bf16).reshape(n_dev, own_rows, width),
            grad_expand.astype(bf16)
            .reshape(n_dev, own_rows, fold, width)
            .transpose(0, 2, 1, 3)
            .reshape(n_dev, fold * own_rows, width),
            grad_shrink.astype(bf16).reshape(n_dev, own_ff, width),
        ],
        axis=1,
    )
    summed = lax.psum_scatter(grad_packed, AXES, scatter_dimension=0, tiled=False).astype(f32)

    grad_groups = attended_grad.reshape(seq_rows, GROUPS, OWN_WIDTH).transpose(1, 0, 2)
    grads = [square_swap(pick(grad_groups, group ^ r), r) for r in range(4)]
    shared = (qx2, qp, wk, wv, wq, grads, attx)
    carry = None
    order = list(range(1, n_q)) + [0]
    dkv, arrived = {}, []
    for step, j in enumerate(order):
        first, last = step == 0, step == n_q - 1
        outs = attend_back_chunk(first, last, kept[j], shared, carry)
        dkv[j], dx = outs[:2]
        if first:
            dox, dqt = outs[2:]
            carry = (dox, dqt)
        elif not last:
            carry = (dox, outs[2])
        else:
            dq = outs[2]
        dx = dx.reshape(2, 2, seq_rows, width)
        dx = dx[:, 0].astype(f32) + square_swap(dx[:, 1], 1).astype(f32)
        dx = dx[0] + square_swap(dx[1].astype(bf16), 2).astype(f32)
        if j:
            dx = from_shift(dx.astype(bf16), "q", n_q, n_q - j).astype(f32)
        arrived.append(dx)
    token_grad = resid_first_grad
    for part in arrived:
        token_grad = token_grad + part
    input_grad = token_grad[None].astype(bf16)

    grad_kv = sum(
        jnp.einsum("nd,nj->dj", jnp.concatenate(chunk_x[j], axis=0), dkv[j], preferred_element_type=f32)
        for j in range(n_q)
    )
    grad_q = jnp.einsum(
        "nd,nj->dj", jnp.concatenate(chunk_x[0], axis=0), dq, preferred_element_type=f32
    )
    grad_joint = jnp.concatenate([grad_q, grad_kv], axis=1).reshape(width, 3, OWN_HEADS, LANES)
    grad_joint = grad_joint[..., :HEAD_DIM].reshape(width, 3 * OWN_WIDTH)
    col_q = jnp.sum(dq.astype(f32), axis=0)
    col_v = sum(jnp.sum(dkv[j][:, OWN_HEADS * LANES :].astype(f32), axis=0) for j in range(n_q))
    bias_grads = jnp.zeros((2, GROUPS, OWN_WIDTH), f32)
    own_bias = jnp.stack([col_q, col_v]).reshape(2, OWN_HEADS, LANES)[..., :HEAD_DIM]
    bias_grads = lax.dynamic_update_slice(
        bias_grads, own_bias.reshape(2, 1, OWN_WIDTH), (0, group, 0)
    ).reshape(2, width)
    vectors = [
        bias_grads[0],
        bias_grads[1],
        grad_obias,
        grad_gain1,
        grad_shift1,
        grad_sbias,
        grad_gain2,
        grad_shift2,
    ]
    small_grads = jnp.concatenate(
        [v.reshape(n_dev, own_rows) for v in vectors] + [grad_ebias.reshape(n_dev, own_ff)], axis=1
    )

    def reduce_axis(value, axis, count, index, dim, dtype):
        part = lax.dynamic_index_in_dim(value, index, dim, keepdims=False).astype(f32)
        for j in range(1, count):
            away = lax.dynamic_index_in_dim(value, (index + j) % count, dim, keepdims=False)
            part = part + from_shift(away.astype(dtype), axis, count, count - j).astype(f32)
        return part

    def reduce_rows(value, dtype):
        value = value.reshape(n_q, 4, n_b, *value.shape[1:])
        value = reduce_axis(value, "b", n_b, bi, 2, dtype)
        value = reduce_axis(value, "q", n_q, zi, 0, dtype)
        return [square_swap(pick(value, group ^ r), r) for r in range(4)]

    joint_parts = reduce_rows(grad_joint.reshape(n_dev, own_rows, 3 * OWN_WIDTH), bf16)
    joint_parts = jnp.stack(joint_parts)
    joint_parts = jnp.stack([pick(joint_parts, group ^ g) for g in range(4)])
    grad_triple = (
        joint_parts.reshape(GROUPS, own_rows, 3, OWN_WIDTH).transpose(1, 2, 0, 3).reshape(own_rows, -1)
    )
    small_sum = sum(reduce_rows(small_grads, f32))

    def small_grad(i):
        return small_sum[i * own_rows : (i + 1) * own_rows]

    grad_expand_own = (
        summed[own_rows : (1 + fold) * own_rows]
        .reshape(fold, own_rows, width)
        .transpose(1, 0, 2)
        .reshape(own_rows, ff)
    )
    return (
        output,
        input_grad,
        grad_triple,
        small_grad(0),
        small_grad(1),
        summed[:own_rows],
        small_grad(2),
        small_grad(3),
        small_grad(4),
        grad_expand_own,
        small_sum[8 * own_rows :],
        summed[(1 + fold) * own_rows :],
        small_grad(5),
        small_grad(6),
        small_grad(7),
    )


def solution(mesh):
    n_seq, n_b = mesh.shape["seq"], mesh.shape["batch"]
    n_q = n_seq // GROUPS
    fine = Mesh(mesh.devices.reshape(n_q, 2, 2, n_b), AXES)
    tokens = P("b", ("q", "x", "c"), None)
    matrix = P(AXES, None)
    vector = P(AXES)
    in_specs = (
        tokens,
        P("b"),
        tokens,
        matrix,
        vector,
        vector,
        matrix,
        vector,
        vector,
        vector,
        matrix,
        vector,
        matrix,
        vector,
        vector,
        vector,
    )
    out_specs = (
        tokens,
        tokens,
        matrix,
        vector,
        vector,
        matrix,
        vector,
        vector,
        vector,
        matrix,
        vector,
        matrix,
        vector,
        vector,
        vector,
    )
    return jax.shard_map(
        partial(per_device, n_q, n_b),
        mesh=fine,
        in_specs=in_specs,
        out_specs=out_specs,
        check_vma=False,
    )
```

time: 1250 us -> 495 us (0.40)
  waiting for transfers between devices: 797 us -> 157 us
  matrix products: 194 us -> 36.3 us
  Pallas kernels: 0 us -> 111 us
  blocking collectives: 81.5 us -> 0 us
  starting transfers between devices: 0.68 us -> 67 us
  local copies, waits for them, and re-layouts: 105 us -> 66.9 us
  other arithmetic: 53 us -> 33.6 us
    reduce_scatter x5 -> x1, waiting for transfers between devices: 473 us -> 0.01 us  [per_device(): lax.psum_scatter(grad_packed, AXES, scatter_dimension=0, tiled=False)]
    all_gather x6 -> x1, waiting for transfers between devices: 199 us -> 0.02 us  [per_device(): gathered_ffn = lax.all_gather(packed, AXES, axis=0, tiled=False)]
    ppermute x0 -> x53, waiting for transfers between devices: none -> 156 us  [the longest x18 118 us: from_shift(): lax.ppermute(value, axis, [((i + step) % count, i) for i in range(count)])]
    dot_general x65 -> x11, matrix products: 185 us -> 29.1 us  [the longest x4 9.98 us: per_device(): jnp.einsum('nd,nj->dj', jnp.concatenate(chunk_x[j], axis=0), dkv[j], pref...]
    unnamed x13 -> x2, waiting for transfers between devices: 126 us -> 0.03 us
    pallas_call x0 -> x8, Pallas kernels: none -> 111 us  [the longest x4 65.2 us: attend_back_chunk(): pl.pallas_call(partial(backward_kernel, first, last, min(512, rows), min(...]
    unnamed x2 -> x0, blocking collectives: 81.5 us -> none
    ppermute x0 -> x53, starting transfers between devices: none -> 67 us  [the longest x18 46.7 us: from_shift(): lax.ppermute(value, axis, [((i + step) % count, i) for i in range(count)])]
  transfers between devices with their start and end apart: 12 -> 55, of which waited for: 11 -> 21; matrix products, arithmetic and copies ran while one was open for 14% -> 18% of each run, Pallas kernels for 0% -> 23%
where the time goes in v1:
time: 495 us; the launch traced here: 488 us
  waiting for transfers between devices  157 us (32%)
  Pallas kernels  111 us (22%)
  starting transfers between devices  67 us (14%)
  local copies, waits for them, and re-layouts  66.9 us (14%)
  matrix products  36.3 us (7%)
  other arithmetic  33.6 us (7%)
  between operations  16.3 us (3%)
    ppermute x18, waiting for transfers between devices, from_shift(): lax.ppermute(value, axis, [((i + step) % count, i) for i in range(count)])  118 us
    pallas_call x4, Pallas kernels, attend_back_chunk(): pl.pallas_call(partial(backward_kernel, first, last, min(512, rows), min(...  65.2 us
    ppermute x18, starting transfers between devices, from_shift(): lax.ppermute(value, axis, [((i + step) % count, i) for i in range(count)])  46.7 us
    pallas_call x4, Pallas kernels, attend_chunk(): pl.pallas_call(partial(forward_kernel, first, last, min(512, rows), min(1...  46 us
    ppermute x13, waiting for transfers between devices, square_swap(): return lax.ppermute(value, 'x', [(0, 1), (1, 0)])  34.7 us
    ppermute x13, starting transfers between devices, square_swap(): return lax.ppermute(value, 'x', [(0, 1), (1, 0)])  12.4 us
    unnamed x90, local copies, waits for them, and re-layouts  10.9 us
    dot_general x4, matrix products, per_device(): jnp.einsum('nd,nj->dj', jnp.concatenate(chunk_x[j], axis=0), dkv[j], pref...  9.98 us
  transfers between devices with their start and end apart: 55, of which 21 were waited for; matrix products, arithmetic and copies ran while one was open for 18% of the time, Pallas kernels for 23%

profile of v1, /device:TPU:0, one launch (start us, length us, event | category | flops | bytes accessed | tf_op | source)
XLA Modules:
  0.0 488.0 jit_solution(14709515115078235755)
XLA Ops:
  26.7 4.8 collective-permute-done.7
  40.7 3.6 collective-permute-done.10
  45.7 14.6 %collective-permute-done.9 = bf16[2,4,74,192]{3,2,1,0:T(8,128)(2,1)S(1)} collective-permute-done((bf16[2,4,74,192]{3,2,1,0:T(8,128)(2,1)S(1)}, bf16[2,4,74,192]{3,2,1,0:T(8,128)(2,1)S(1)}, u32[]{:S(2)}, u32[]{:S(2)}) %collective-permute-start.9) | collective-permute-done | bytes 227360 | tf_op jit(solution)/shard_map/ppermute | solution.py:299
  61.4 26.3 %collective-permute-start.18 = (bf16[256,768]{1,0:T(8,128)(2,1)S(1)}, bf16[256,768]{1,0:T(8,128)(2,1)}, u32[]{:S(2)}, u32[]{:S(2)}) collective-permute-start(bf16[256,768]{1,0:T(8,128)(2,1)S(1)} %bitcast.353), channel_id=1, source_target_pairs={{8,0},{16,8},{24,16},{0,24},{9,1},{17,9},{25,17},{1,25},{10,2},{18... | collective-permute-start | bytes 1179656 | tf_op jit(solution)/shard_map/ppermute | solution.py:299
  95.9 37.9 %collective-permute-done.18.refs_1_ = bf16[256,768]{1,0:T(8,128)(2,1)} collective-permute-done((bf16[256,768]{1,0:T(8,128)(2,1)S(1)}, bf16[256,768]{1,0:T(8,128)(2,1)}, u32[]{:S(2)}, u32[]{:S(2)}) %collective-permute-start.18) | collective-permute-done | bytes 393248 | tf_op jit(solution)/shard_map/ppermute | solution.py:299
  142.3 11.2 %attend_forward.4 = (bf16[3,1024,256]{2,1,0:T(8,128)(2,1)}, bf16[3,1024,128]{2,1,0:T(8,128)(2,1)}, bf16[3,1024,256]{2,1,0:T(8,128)(2,1)}, bf16[3,1024,128]{2,1,0...) custom-call(s32[5]{0:T(128)} %stack.185.refs_0_, bf16[256,768]{1,0:T(8,128)(2,1)} %bitcast.348, ...), custom_call_target="tpu_custom_call" | custom-call | flops 8000000000 | bytes 10000000 | tf_op jit(solution)/shard_map/attend_forward/pallas_call | solution.py:166
  154.0 4.7 collective-permute-done.16.refs_3_
  159.9 11.2 %attend_forward.5 = (bf16[3,1024,256]{2,1,0:T(8,128)(2,1)}, bf16[3,1024,128]{2,1,0:T(8,128)(2,1)}, f32[3,8,1024]{2,1,0:T(8,128)}, f32[3,80,1024]{2,1,0:T(8,128)}) custom-call(s32[5]{0:T(128)} %stack.195.refs_0_, bf16[256,768]{1,0:T(8,128)(2,1)} %collective-permute-done.18.refs_1_, bf16[256,768]{1,0:T(8,128)(2,1)} %copy-done.25, bf16[256,768]{1,0:T(8,128)(2,1)} %copy-done.19, ...), custom_call_target="tpu_custom_call" | custom-call | flops 8000000000 | bytes 10000000 | tf_op jit(solution)/shard_map/attend_forward/pallas_call | solution.py:166
  171.2 10.9 %attend_forward.6 = (bf16[3,1024,256]{2,1,0:T(8,128)(2,1)}, bf16[3,1024,128]{2,1,0:T(8,128)(2,1)}, f32[3,8,1024]{2,1,0:T(8,128)}, f32[3,80,1024]{2,1,0:T(8,128)}) custom-call(s32[5]{0:T(128)} %stack.190.refs_0_, bf16[256,768]{1,0:T(8,128)(2,1)} %collective-permute-done.14.refs_1_, bf16[256,768]{1,0:T(8,128)(2,1)} %collective-permute-done.15.refs_2_, ...), custom_call_target="tpu_custom_call" | custom-call | flops 8000000000 | bytes 10000000 | tf_op jit(solution)/shard_map/attend_forward/pallas_call | solution.py:166
  183.0 12.6 %attend_forward.7 = (bf16[3,1024,256]{2,1,0:T(8,128)(2,1)}, bf16[3,1024,128]{2,1,0:T(8,128)(2,1)}, bf16[1024,192]{1,0:T(8,128)(2,1)}, f32[3,1024,128]{2,1,0:T(8,128)}, bf16[3,1024,256]{2,1,0:T(8,128)(2,1)}) custom-call(s32[5]{0:T(128)} %stack.164.refs_0_, bf16[256,768]{1,0:T(8,128)(2,1)} %copy-done.15, bf16[256,768]{1,0:T(8,128)(2,1)} %copy-done.21, ...), custom_call_target="tpu_custom_call" | custom-call | flops 8000000000 | bytes 10000000 | tf_op jit(solution)/shard_map/attend_forward/pallas_call | solution.py:166
  202.4 3.1 collective-permute-done.23
  205.7 6.5 %fusion.95 = (bf16[32,96,768]{2,1,0:T(8,128)(2,1)}, bf16[32,96,768]{2,1,0:T(8,128)(2,1)S(1)}) fusion(bf16[32,216,768]{2,1,0:T(8,128)(2,1)} %bitcast.292), kind=kLoop, calls=%fused_computation.241 | loop fusion | bytes 18874368 | tf_op jit(solution)/shard_map/slice | solution.py:447
  217.9 8.3 %multiply_convert_fusion = (bf16[256,3072]{1,0:T(8,128)(2,1)S(1)}, f32[256,3072]{1,0:T(8,128)S(1)}, f32[256,3072]{1,0:T(8,128)S(1)}) fusion(f32[3072]{0:T(1024)S(1)} %add.476, bf16[768,3072]{1,0:T(8,128)(2,1)S(1)} %bitcast.295, f32[256,768]{1,0:T(8,128)S(1)} %get-tuple-element.176, f32[768]{0:T(1024)S(1)} %add.473, f32[768]{0:T(1024)S(1)} %mul.258, ...), kind=kOutput, calls=%fused_computation.9 | convolution fusion | flops 1260847104 | bytes 13389824 | tf_op jit(solution)/shard_map/dot_general | solution.py:452
  229.8 3.6 convolution_convert_fusion
  237.5 3.7 convolution_convert_fusion.1
  246.5 9.7 %reshape.368 = bf16[32,24,4,768]{3,2,1,0:T(4,128)(2,1)} reshape(bf16[768,3072]{1,0:T(8,128)(2,1)} %convolution_convert_fusion.1) | data formatting | bytes 9437184 | tf_op jit(solution)/shard_map/reshape | solution.py:485
  256.3 3.4 copy.223
  260.4 5.3 %pad_maximum_fusion = bf16[32,216,768]{2,1,0:T(8,128)(2,1)} fusion(bf16[32,96,768]{2,1,0:T(8,128)(2,1)S(1)} %bitcast.287, bf16[32,96,768]{2,1,0:T(8,128)(2,1)S(1)} %bitcast.291, bf16[32,24,768]{2,1,0:T(8,128)(2,1)S(1)} %bitcast.318), kind=kLoop, calls=%fused_computation | loop fusion | flops 31850496 | bytes 21233664 | tf_op jit(solution)/shard_map/concatenate | solution.py:481
  267.9 15.6 %attend_backward.4 = (bf16[1024,768]{1,0:T(8,128)(2,1)}, bf16[1024,768]{1,0:T(8,128)(2,1)}, bf16[3,1024,128]{2,1,0:T(8,128)(2,1)}, f32[3,64,1024]{2,1,0:T(8,128)}) custom-call(bf16[3,1024,256]{2,1,0:T(8,128)(2,1)} %get-tuple-element.55.refs_0_, bf16[3,1024,128]{2,1,0:T(8,128)(2,1)} %get-tuple-element.56.refs_1_, ...), custom_call_target="tpu_custom_call" | custom-call | flops 15000000512 | bytes 10000000 | tf_op jit(solution)/shard_map/attend_backward/pallas_call | solution.py:284
  283.4 15.6 %attend_backward.5 = (bf16[1024,768]{1,0:T(8,128)(2,1)}, bf16[1024,768]{1,0:T(8,128)(2,1)}, f32[3,64,1024]{2,1,0:T(8,128)}) custom-call(bf16[3,1024,256]{2,1,0:T(8,128)(2,1)} %get-tuple-element.61.refs_0_, bf16[3,1024,128]{2,1,0:T(8,128)(2,1)} %get-tuple-element.62.refs_1_, bf16[3,1024,256]{2,1,0:T(8,128)(2,1)} %get-tuple-element.57.refs_2_, ...), custom_call_target="tpu_custom_call" | custom-call | flops 15000000512 | bytes 10000000 | tf_op jit(solution)/shard_map/attend_backward/pallas_call | solution.py:284
  299.0 15.8 %attend_backward.6 = (bf16[1024,768]{1,0:T(8,128)(2,1)}, bf16[1024,768]{1,0:T(8,128)(2,1)}, f32[3,64,1024]{2,1,0:T(8,128)}) custom-call(bf16[3,1024,256]{2,1,0:T(8,128)(2,1)} %get-tuple-element.66.refs_0_, bf16[3,1024,128]{2,1,0:T(8,128)(2,1)} %get-tuple-element.67.refs_1_, bf16[3,1024,256]{2,1,0:T(8,128)(2,1)} %get-tuple-element.57.refs_2_, ...), custom_call_target="tpu_custom_call" | custom-call | flops 15000000512 | bytes 10000000 | tf_op jit(solution)/shard_map/attend_backward/pallas_call | solution.py:284
  316.4 18.2 %attend_backward.7 = (bf16[1024,768]{1,0:T(8,128)(2,1)}, bf16[1024,768]{1,0:T(8,128)(2,1)}, bf16[1024,384]{1,0:T(8,128)(2,1)}) custom-call(bf16[3,1024,256]{2,1,0:T(8,128)(2,1)} %get-tuple-element.70.refs_0_, bf16[3,1024,128]{2,1,0:T(8,128)(2,1)} %get-tuple-element.71.refs_1_, bf16[3,1024,256]{2,1,0:T(8,128)(2,1)} %get-tuple-element.57.refs_2_, ...), custom_call_target="tpu_custom_call" | custom-call | flops 15000000512 | bytes 10000000 | tf_op jit(solution)/shard_map/attend_backward/pallas_call | solution.py:284
  347.6 3.9 copy.237
  351.4 5.9 %reshape_reshape_reshape.3 = f32[4,4,2,24,576]{4,3,2,1,0:T(8,128)} reshape(f32[768,3,3,64]{3,2,1,0:T(4,128)} %copy.237) | data formatting | bytes 3538944 | tf_op jit(solution)/shard_map/reshape;reshape;reshape | solution.py:560
  375.5 12.7 %collective-permute-done.39 = bf16[4,4,24,576]{3,2,1,0:T(8,128)(2,1)S(1)} collective-permute-done((bf16[4,4,24,576]{3,2,1,0:T(8,128)(2,1)S(1)}, bf16[4,4,24,576]{3,2,1,0:T(8,128)(2,1)S(1)}, u32[]{:S(2)}, u32[]{:S(2)}) %collective-permute-start.39) | collective-permute-done | bytes 442400 | tf_op jit(solution)/shard_map/ppermute | solution.py:299
  391.8 4.7 collective-permute-done.42
  396.6 5.8 %collective-permute-done.41 = bf16[4,24,576]{2,1,0:T(8,128)(2,1)S(1)} collective-permute-done((bf16[4,24,576]{2,1,0:T(8,128)(2,1)S(1)}, bf16[4,24,576]{2,1,0:T(8,128)(2,1)S(1)}, u32[]{:S(2)}, u32[]{:S(2)}) %collective-permute-start.41) | collective-permute-done | bytes 110624 | tf_op jit(solution)/shard_map/ppermute | solution.py:299
  410.4 9.5 %collective-permute-done.35 = bf16[256,768]{1,0:T(8,128)(2,1)S(1)} collective-permute-done((bf16[256,768]{1,0:T(8,128)(2,1)S(1)}, bf16[256,768]{1,0:T(8,128)(2,1)S(1)}, u32[]{:S(2)}, u32[]{:S(2)}) %collective-permute-start.35) | collective-permute-done | bytes 393248 | tf_op jit(solution)/shard_map/ppermute | solution.py:308
  421.6 6.7 %collective-permute-done.32 = bf16[256,768]{1,0:T(8,128)(2,1)S(1)} collective-permute-done((bf16[256,768]{1,0:T(8,128)(2,1)S(1)}, bf16[256,768]{1,0:T(8,128)(2,1)S(1)}, u32[]{:S(2)}, u32[]{:S(2)}) %collective-permute-start.32) | collective-permute-done | bytes 393248 | tf_op jit(solution)/shard_map/ppermute | solution.py:308
  430.1 6.7 %collective-permute-done.29 = bf16[256,768]{1,0:T(8,128)(2,1)S(1)} collective-permute-done((bf16[256,768]{1,0:T(8,128)(2,1)S(1)}, bf16[256,768]{1,0:T(8,128)(2,1)S(1)}, u32[]{:S(2)}, u32[]{:S(2)}) %collective-permute-start.29) | collective-permute-done | bytes 393248 | tf_op jit(solution)/shard_map/ppermute | solution.py:308
  445.3 4.1 collective-permute-done.36
  449.4 25.1 %collective-permute-done.33 = bf16[256,768]{1,0:T(8,128)(2,1)} collective-permute-done((bf16[256,768]{1,0:T(8,128)(2,1)}, bf16[256,768]{1,0:T(8,128)(2,1)}, u32[]{:S(2)}, u32[]{:S(2)}) %collective-permute-start.33) | collective-permute-done | bytes 393248 | tf_op jit(solution)/shard_map/ppermute | solution.py:299
  (356 shorter events, 139.9 us)
Async XLA Ops:
  7.2 198.5 %all-gather.3.cloned.1.call-start = ((), (), s32[]{:S(2)}) async-start(), calls=%async_computation.2 | async-start | bytes 10948608 | tf_op jit(solution)/shard_map/all_gather | solution.py:416
  10.9 465.9 %reduce-scatter.2.cloned.1.call-start = ((), (), s32[]{:S(2)}) async-start(), calls=%async_computation.1 | async-start | bytes 10948608 | tf_op jit(solution)/shard_map/reduce_scatter | solution.py:492
  33.1 27.1 %collective-permute-start.9 = (bf16[2,4,74,192]{3,2,1,0:T(8,128)(2,1)S(1)}, bf16[2,4,74,192]{3,2,1,0:T(8,128)(2,1)S(1)}, u32[]{:S(2)}, u32[]{:S(2)}) collective-permute-start(bf16[2,4,74,192]{3,2,1,0:T(8,128)(2,1)S(1)} %get-tuple-element.131), channel_id=1, source_target_pairs={{16,0},{24,8},{0,16},{8,24},{17,1},{25,9},{1,17},{9,25},{18,2},{26... | collective-permute-start | bytes 681992 | tf_op jit(solution)/shard_map/ppermute | solution.py:299
  35.5 25.9 %collective-permute-start.8 = (bf16[2,4,74,192]{3,2,1,0:T(8,128)(2,1)S(1)}, bf16[2,4,74,192]{3,2,1,0:T(8,128)(2,1)S(1)}, u32[]{:S(2)}, u32[]{:S(2)}) collective-permute-start(bf16[2,4,74,192]{3,2,1,0:T(8,128)(2,1)S(1)} %get-tuple-element.131), channel_id=1, source_target_pairs={{8,0},{16,8},{24,16},{0,24},{9,1},{17,9},{25,17},{1,25},{10,2},{18... | collective-permute-start | bytes 681992 | tf_op jit(solution)/shard_map/ppermute | solution.py:299
  37.0 101.2 %collective-permute-start = (bf16[256,768]{1,0:T(8,128)(2,1)S(1)}, bf16[256,768]{1,0:T(8,128)(2,1)S(1)}, u32[]{:S(2)}, u32[]{:S(2)}) collective-permute-start(bf16[256,768]{1,0:T(8,128)(2,1)S(1)} %bitcast.349), channel_id=1, source_target_pairs={{24,0},{0,8},{8,16},{16,24},{25,1},{1,9},{9,17},{17,25},{26,2},{2,... | collective-permute-start | bytes 1179656 | tf_op jit(solution)/shard_map/ppermute | solution.py:299
  37.5 100.6 %collective-permute-start.11 = (bf16[256,768]{1,0:T(8,128)(2,1)S(1)}, bf16[256,768]{1,0:T(8,128)(2,1)}, u32[]{:S(2)}, u32[]{:S(2)}) collective-permute-start(bf16[256,768]{1,0:T(8,128)(2,1)S(1)} %bitcast.350), channel_id=1, source_target_pairs={{0,2},{2,0},{1,3},{3,1},{4,6},{6,4},{5,7},{7,5},{8,10},{10,8},{9,1... | collective-permute-start | bytes 1179656 | tf_op jit(solution)/shard_map/ppermute | solution.py:306
  44.3 51.6 %collective-permute-start.12 = (bf16[256,768]{1,0:T(8,128)(2,1)S(1)}, bf16[256,768]{1,0:T(8,128)(2,1)}, u32[]{:S(2)}, u32[]{:S(2)}) collective-permute-start(bf16[256,768]{1,0:T(8,128)(2,1)S(1)} %bitcast.351), channel_id=1, source_target_pairs={{0,4},{4,0},{1,5},{5,1},{2,6},{6,2},{3,7},{7,3},{8,12},{12,8},{9,1... | collective-permute-start | bytes 1179656 | tf_op jit(solution)/shard_map/ppermute | solution.py:308
  60.2 79.4 %collective-permute-start.14 = (bf16[256,768]{1,0:T(8,128)(2,1)S(1)}, bf16[256,768]{1,0:T(8,128)(2,1)}, u32[]{:S(2)}, u32[]{:S(2)}) collective-permute-start(bf16[256,768]{1,0:T(8,128)(2,1)S(1)} %bitcast.352), channel_id=1, source_target_pairs={{16,0},{24,8},{0,16},{8,24},{17,1},{25,9},{1,17},{9,25},{18,2},{26... | collective-permute-start | bytes 1179656 | tf_op jit(solution)/shard_map/ppermute | solution.py:299
  61.4 72.4 %collective-permute-start.18 = (bf16[256,768]{1,0:T(8,128)(2,1)S(1)}, bf16[256,768]{1,0:T(8,128)(2,1)}, u32[]{:S(2)}, u32[]{:S(2)}) collective-permute-start(bf16[256,768]{1,0:T(8,128)(2,1)S(1)} %bitcast.353), channel_id=1, source_target_pairs={{8,0},{16,8},{24,16},{0,24},{9,1},{17,9},{25,17},{1,25},{10,2},{18... | collective-permute-start | bytes 1179656 | tf_op jit(solution)/shard_map/ppermute | solution.py:299
  95.9 43.9 %collective-permute-start.13 = (bf16[256,768]{1,0:T(8,128)(2,1)}, bf16[256,768]{1,0:T(8,128)(2,1)S(1)}, u32[]{:S(2)}, u32[]{:S(2)}) collective-permute-start(bf16[256,768]{1,0:T(8,128)(2,1)} %collective-permute-done.12.refs_3_), channel_id=1, source_target_pairs={{0,2},{2,0},{1,3},{3,1},{4,6},{6,4},{5,7},{7,5},{8,10},{10,8},{9,1... | collective-permute-start | bytes 1179656 | tf_op jit(solution)/shard_map/ppermute | solution.py:306
  138.1 44.0 %collective-permute-start.1 = (bf16[256,768]{1,0:T(8,128)(2,1)S(1)}, bf16[256,768]{1,0:T(8,128)(2,1)S(1)}, u32[]{:S(2)}, u32[]{:S(2)}) collective-permute-start(bf16[256,768]{1,0:T(8,128)(2,1)S(1)} %collective-permute-done.refs_1_), channel_id=1, source_target_pairs={{0,2},{2,0},{1,3},{3,1},{4,6},{6,4},{5,7},{7,5},{8,10},{10,8},{9,1... | collective-permute-start | bytes 1179656 | tf_op jit(solution)/shard_map/ppermute | solution.py:306
  138.1 15.4 %collective-permute-start.2 = (bf16[256,768]{1,0:T(8,128)(2,1)S(1)}, bf16[256,768]{1,0:T(8,128)(2,1)S(1)}, u32[]{:S(2)}, u32[]{:S(2)}) collective-permute-start(bf16[256,768]{1,0:T(8,128)(2,1)S(1)} %collective-permute-done.refs_1_), channel_id=1, source_target_pairs={{0,4},{4,0},{1,5},{5,1},{2,6},{6,2},{3,7},{7,3},{8,12},{12,8},{9,1... | collective-permute-start | bytes 1179656 | tf_op jit(solution)/shard_map/ppermute | solution.py:308
  139.6 19.1 %collective-permute-start.19 = (bf16[256,768]{1,0:T(8,128)(2,1)}, bf16[256,768]{1,0:T(8,128)(2,1)S(1)}, u32[]{:S(2)}, u32[]{:S(2)}) collective-permute-start(bf16[256,768]{1,0:T(8,128)(2,1)} %collective-permute-done.18.refs_1_), channel_id=1, source_target_pairs={{0,2},{2,0},{1,3},{3,1},{4,6},{6,4},{5,7},{7,5},{8,10},{10,8},{9,1... | collective-permute-start | bytes 1179656 | tf_op jit(solution)/shard_map/ppermute | solution.py:306
  139.8 18.9 %collective-permute-start.16 = (bf16[256,768]{1,0:T(8,128)(2,1)}, bf16[256,768]{1,0:T(8,128)(2,1)S(1)}, u32[]{:S(2)}, u32[]{:S(2)}) collective-permute-start(bf16[256,768]{1,0:T(8,128)(2,1)} %collective-permute-done.14.refs_1_), channel_id=1, source_target_pairs={{0,4},{4,0},{1,5},{5,1},{2,6},{6,2},{3,7},{7,3},{8,12},{12,8},{9,1... | collective-permute-start | bytes 1179656 | tf_op jit(solution)/shard_map/ppermute | solution.py:308
  142.3 16.9 %collective-permute-start.21 = (bf16[256,768]{1,0:T(8,128)(2,1)S(1)}, bf16[256,768]{1,0:T(8,128)(2,1)S(1)}, u32[]{:S(2)}, u32[]{:S(2)}) collective-permute-start(bf16[256,768]{1,0:T(8,128)(2,1)S(1)} %collective-permute-done.20.refs_3_), channel_id=1, source_target_pairs={{0,2},{2,0},{1,3},{3,1},{4,6},{6,4},{5,7},{7,5},{8,10},{10,8},{9,1... | collective-permute-start | bytes 1179656 | tf_op jit(solution)/shard_map/ppermute | solution.py:306
  153.5 17.6 %collective-permute-start.15 = (bf16[256,768]{1,0:T(8,128)(2,1)}, bf16[256,768]{1,0:T(8,128)(2,1)}, u32[]{:S(2)}, u32[]{:S(2)}) collective-permute-start(bf16[256,768]{1,0:T(8,128)(2,1)} %collective-permute-done.14.refs_1_), channel_id=1, source_target_pairs={{0,2},{2,0},{1,3},{3,1},{4,6},{6,4},{5,7},{7,5},{8,10},{10,8},{9,1... | collective-permute-start | bytes 1179656 | tf_op jit(solution)/shard_map/ppermute | solution.py:306
  158.7 23.5 %collective-permute-start.3 = (bf16[256,768]{1,0:T(8,128)(2,1)S(1)}, bf16[256,768]{1,0:T(8,128)(2,1)S(1)}, u32[]{:S(2)}, u32[]{:S(2)}) collective-permute-start(bf16[256,768]{1,0:T(8,128)(2,1)S(1)} %collective-permute-done.2.refs_3_), channel_id=1, source_target_pairs={{0,2},{2,0},{1,3},{3,1},{4,6},{6,4},{5,7},{7,5},{8,10},{10,8},{9,1... | collective-permute-start | bytes 1179656 | tf_op jit(solution)/shard_map/ppermute | solution.py:306
  244.3 22.8 %collective-permute-start.25 = (bf16[256,192]{1,0:T(8,128)(2,1)S(1)}, bf16[256,192]{1,0:T(8,128)(2,1)S(1)}, u32[]{:S(2)}, u32[]{:S(2)}) collective-permute-start(bf16[256,192]{1,0:T(8,128)(2,1)S(1)} %bitcast.328), channel_id=1, source_target_pairs={{0,2},{2,0},{1,3},{3,1},{4,6},{6,4},{5,7},{7,5},{8,10},{10,8},{9,1... | collective-permute-start | bytes 294920 | tf_op jit(solution)/shard_map/ppermute | solution.py:306
  244.4 22.7 %collective-permute-start.26 = (bf16[256,192]{1,0:T(8,128)(2,1)S(1)}, bf16[256,192]{1,0:T(8,128)(2,1)S(1)}, u32[]{:S(2)}, u32[]{:S(2)}) collective-permute-start(bf16[256,192]{1,0:T(8,128)(2,1)S(1)} %bitcast.329), channel_id=1, source_target_pairs={{0,4},{4,0},{1,5},{5,1},{2,6},{6,2},{3,7},{7,3},{8,12},{12,8},{9,1... | collective-permute-start | bytes 294920 | tf_op jit(solution)/shard_map/ppermute | solution.py:308
  245.5 21.7 %collective-permute-start.27 = (bf16[256,192]{1,0:T(8,128)(2,1)S(1)}, bf16[256,192]{1,0:T(8,128)(2,1)S(1)}, u32[]{:S(2)}, u32[]{:S(2)}) collective-permute-start(bf16[256,192]{1,0:T(8,128)(2,1)S(1)} %bitcast.330), channel_id=1, source_target_pairs={{0,6},{6,0},{2,4},{4,2},{1,7},{7,1},{3,5},{5,3},{8,14},{14,8},{10,... | collective-permute-start | bytes 294920 | tf_op jit(solution)/shard_map/ppermute | solution.py:309
  316.1 88.2 %collective-permute-start.34 = (bf16[2,256,768]{2,1,0:T(8,128)(2,1)S(1)}, bf16[2,256,768]{2,1,0:T(8,128)(2,1)}, u32[]{:S(2)}, u32[]{:S(2)}) collective-permute-start(bf16[2,256,768]{2,1,0:T(8,128)(2,1)S(1)} %slice_bitcast_fusion.4), channel_id=1, source_target_pairs={{0,2},{2,0},{1,3},{3,1},{4,6},{6,4},{5,7},{7,5},{8,10},{10,8},{9,1... | collective-permute-start | bytes 2359304 | tf_op jit(solution)/shard_map/ppermute | solution.py:306
  367.5 20.7 %collective-permute-start.39 = (bf16[4,4,24,576]{3,2,1,0:T(8,128)(2,1)S(1)}, bf16[4,4,24,576]{3,2,1,0:T(8,128)(2,1)S(1)}, u32[]{:S(2)}, u32[]{:S(2)}) collective-permute-start(bf16[4,4,24,576]{3,2,1,0:T(8,128)(2,1)S(1)} %fusion.51), channel_id=1, source_target_pairs={{1,0},{0,1},{3,2},{2,3},{5,4},{4,5},{7,6},{6,7},{9,8},{8,9},{11,10... | collective-permute-start | bytes 1327112 | tf_op jit(solution)/shard_map/ppermute | solution.py:299
  372.6 33.4 %collective-permute-start.31 = (bf16[2,256,768]{2,1,0:T(8,128)(2,1)S(1)}, bf16[2,256,768]{2,1,0:T(8,128)(2,1)S(1)}, u32[]{:S(2)}, u32[]{:S(2)}) collective-permute-start(bf16[2,256,768]{2,1,0:T(8,128)(2,1)S(1)} %slice_bitcast_fusion.7), channel_id=1, source_target_pairs={{0,2},{2,0},{1,3},{3,1},{4,6},{6,4},{5,7},{7,5},{8,10},{10,8},{9,1... | collective-permute-start | bytes 2359304 | tf_op jit(solution)/shard_map/ppermute | solution.py:306
  375.0 14.7 %collective-permute-start.51 = (f32[288]{0:T(512)S(1)}, f32[288]{0:T(512)S(1)}, u32[]{:S(2)}, u32[]{:S(2)}) collective-permute-start(f32[288]{0:T(512)S(1)} %get-tuple-element.89), channel_id=1, source_target_pairs={{0,4},{4,0},{1,5},{5,1},{2,6},{6,2},{3,7},{7,3},{8,12},{12,8},{9,1... | collective-permute-start | bytes 3464 | tf_op jit(solution)/shard_map/ppermute | solution.py:308
  402.5 37.7 %collective-permute-start.45 = (f32[24,576]{1,0:T(8,128)S(1)}, f32[24,576]{1,0:T(8,128)S(1)}, u32[]{:S(2)}, u32[]{:S(2)}) collective-permute-start(f32[24,576]{1,0:T(8,128)S(1)} %get-tuple-element.137), channel_id=1, source_target_pairs={{0,6},{6,0},{2,4},{4,2},{1,7},{7,1},{3,5},{5,3},{8,14},{14,8},{10,... | collective-permute-start | bytes 165896 | tf_op jit(solution)/shard_map/ppermute | solution.py:309
  404.3 36.4 %collective-permute-start.44 = (f32[24,576]{1,0:T(8,128)S(1)}, f32[24,576]{1,0:T(8,128)S(1)}, u32[]{:S(2)}, u32[]{:S(2)}) collective-permute-start(f32[24,576]{1,0:T(8,128)S(1)} %get-tuple-element.138), channel_id=1, source_target_pairs={{0,4},{4,0},{1,5},{5,1},{2,6},{6,2},{3,7},{7,3},{8,12},{12,8},{9,1... | collective-permute-start | bytes 165896 | tf_op jit(solution)/shard_map/ppermute | solution.py:308
  406.0 37.9 %collective-permute-start.43 = (f32[24,576]{1,0:T(8,128)S(1)}, f32[24,576]{1,0:T(8,128)S(1)}, u32[]{:S(2)}, u32[]{:S(2)}) collective-permute-start(f32[24,576]{1,0:T(8,128)S(1)} %get-tuple-element.139), channel_id=1, source_target_pairs={{0,2},{2,0},{1,3},{3,1},{4,6},{6,4},{5,7},{7,5},{8,10},{10,8},{9,1... | collective-permute-start | bytes 165896 | tf_op jit(solution)/shard_map/ppermute | solution.py:306
  408.3 20.0 %collective-permute-start.32 = (bf16[256,768]{1,0:T(8,128)(2,1)S(1)}, bf16[256,768]{1,0:T(8,128)(2,1)S(1)}, u32[]{:S(2)}, u32[]{:S(2)}) collective-permute-start(bf16[256,768]{1,0:T(8,128)(2,1)S(1)} %fusion.54), channel_id=1, source_target_pairs={{0,4},{4,0},{1,5},{5,1},{2,6},{6,2},{3,7},{7,3},{8,12},{12,8},{9,1... | collective-permute-start | bytes 1179656 | tf_op jit(solution)/shard_map/ppermute | solution.py:308
  419.9 16.9 %collective-permute-start.29 = (bf16[256,768]{1,0:T(8,128)(2,1)S(1)}, bf16[256,768]{1,0:T(8,128)(2,1)S(1)}, u32[]{:S(2)}, u32[]{:S(2)}) collective-permute-start(bf16[256,768]{1,0:T(8,128)(2,1)S(1)} %fusion.53), channel_id=1, source_target_pairs={{0,4},{4,0},{1,5},{5,1},{2,6},{6,2},{3,7},{7,3},{8,12},{12,8},{9,1... | collective-permute-start | bytes 1179656 | tf_op jit(solution)/shard_map/ppermute | solution.py:308
  428.3 17.0 %collective-permute-start.38 = (bf16[256,768]{1,0:T(8,128)(2,1)}, bf16[256,768]{1,0:T(8,128)(2,1)}, u32[]{:S(2)}, u32[]{:S(2)}) collective-permute-start(bf16[256,768]{1,0:T(8,128)(2,1)} %fusion.57), channel_id=1, source_target_pairs={{0,4},{4,0},{1,5},{5,1},{2,6},{6,2},{3,7},{7,3},{8,12},{12,8},{9,1... | collective-permute-start | bytes 1179656 | tf_op jit(solution)/shard_map/ppermute | solution.py:308
  440.2 34.2 %collective-permute-start.33 = (bf16[256,768]{1,0:T(8,128)(2,1)}, bf16[256,768]{1,0:T(8,128)(2,1)}, u32[]{:S(2)}, u32[]{:S(2)}) collective-permute-start(bf16[256,768]{1,0:T(8,128)(2,1)} %fusion.40), channel_id=1, source_target_pairs={{16,0},{24,8},{0,16},{8,24},{17,1},{25,9},{1,17},{9,25},{18,2},{26... | collective-permute-start | bytes 1179656 | tf_op jit(solution)/shard_map/ppermute | solution.py:299
  440.7 33.7 %collective-permute-start.30 = (bf16[256,768]{1,0:T(8,128)(2,1)}, bf16[256,768]{1,0:T(8,128)(2,1)}, u32[]{:S(2)}, u32[]{:S(2)}) collective-permute-start(bf16[256,768]{1,0:T(8,128)(2,1)} %fusion.42), channel_id=1, source_target_pairs={{24,0},{0,8},{8,16},{16,24},{25,1},{1,9},{9,17},{17,25},{26,2},{2,... | collective-permute-start | bytes 1179656 | tf_op jit(solution)/shard_map/ppermute | solution.py:299
  (63 other events, 439.2 us)
Sparse Core Ops, SparseCore 0:
  11.5 131.4 all-gather.2
  267.2 155.7 reduce-scatter.1

commit v2 on v1

v2 whole, which is shorter than its diff:
```python
from functools import partial
import math

import jax
import jax.numpy as jnp
from jax import lax
from jax.experimental import pallas as pl
from jax.experimental.pallas import tpu as pltpu
from jax.sharding import Mesh, PartitionSpec as P

HEADS = 12
HEAD_DIM = 64
GROUPS = 4
OWN_HEADS = HEADS // GROUPS
OWN_WIDTH = OWN_HEADS * HEAD_DIM
LANES = 128
WIDE = 640
VECTORS = 3 * OWN_WIDTH

bf16 = jnp.bfloat16
f32 = jnp.float32
masked_score = -1e30
norm_eps = 1e-12
log2_e = 1.4426950408889634
CONTRACT_LAST = (((1,), (1,)), ((), ()))
VMEM_BYTES = 60 * 1024 * 1024
AXES = ("q", "x", "c", "b")


def split_three(value):
    high = value.astype(bf16).astype(f32)
    rest = value - high
    mid = rest.astype(bf16).astype(f32)
    low = (rest - mid).astype(bf16).astype(f32)
    return high, mid, low


def low_half(tile, lane, from_high):
    turned = pltpu.roll(tile, HEAD_DIM, 1)
    low = lane < HEAD_DIM
    return jnp.where(low, turned, tile) if from_high else jnp.where(low, tile, turned)


def place_of(kind, h):
    slot = kind * OWN_HEADS + h
    return slot // 2, slot % 2


def forward_kernel(first, last, block_q, block_k, *refs):
    refs = list(refs)
    where_ref = refs.pop(0)
    pieces = [refs.pop(0) for _ in range(4)]
    w_ref, bias_ref = [refs.pop(0) for _ in range(2)]
    if not first:
        qx_ref, peak_in, sum_in = [refs.pop(0) for _ in range(3)]
    kx_ref, vx_ref = [refs.pop(0) for _ in range(2)]
    if first:
        qx_ref, qp_ref = [refs.pop(0) for _ in range(2)]
    if last:
        att_refs = [refs.pop(0) for _ in range(4)]
        attx_ref, qx2_ref = [refs.pop(0) for _ in range(2)]
    else:
        peak_out, sum_out = [refs.pop(0) for _ in range(2)]
    (vt_ref,) = refs
    piece_rows = pieces[0].shape[0]
    rows_in = 4 * piece_rows
    lane = lax.broadcasted_iota(jnp.int32, (piece_rows, LANES), 1)
    row = lax.broadcasted_iota(jnp.int32, (piece_rows, LANES), 0)
    low = lane < HEAD_DIM
    length = where_ref[4]
    three = (lane >= HEAD_DIM) & (lane < HEAD_DIM + 3)
    skip = 0 if first else LANES
    for p in range(4):
        rows = slice(p * piece_rows, (p + 1) * piece_rows)
        joint = jnp.dot(pieces[p][...], w_ref[:, skip:], preferred_element_type=f32)
        joint = joint + bias_ref[:, skip:]
        bias = jnp.where(where_ref[p] + row < length, 0.0, masked_score)
        key_extra = jnp.where(three, 1.0, jnp.where(lane == HEAD_DIM + 3, bias, 0.0))

        def head_of(kind, h):
            tile, high = place_of(kind, h)
            return low_half(joint[:, tile * LANES - skip : (tile + 1) * LANES - skip], lane, high)

        for h in range(OWN_HEADS):
            k = head_of(1, h)
            kx_ref[h, rows, :LANES] = k.astype(bf16)
            kx_ref[h, rows, LANES:] = jnp.where(low, k, key_extra).astype(bf16)
            v = jnp.where(low, head_of(2, h), 0.0)
            vx_ref[h, rows, :] = jnp.where(three, -1.0, v).astype(bf16)
            vt = jnp.where(lane == HEAD_DIM, 1.0, v).T
            vt_ref[h, :, rows] = vt[:80].astype(bf16)
            if first:
                q = head_of(0, h).astype(bf16).astype(f32)
                qp_ref[h, rows, :] = jnp.where(low, q, 0.0).astype(bf16)
                high, mid, rest = split_three(q * (HEAD_DIM**-0.5 * log2_e))
                qx_ref[h, rows, :LANES] = jnp.where(low, high, mid).astype(bf16)
                one = jnp.where(lane == HEAD_DIM + 3, 1.0, 0.0)
                qx_ref[h, rows, LANES:] = jnp.where(low, rest, one).astype(bf16)
    for h in range(OWN_HEADS):
        for i in range(rows_in // block_q):
            cols = slice(i * block_q, (i + 1) * block_q)
            q = qx_ref[h, cols, :]
            if first:
                peak = jnp.full((1, block_q), masked_score, f32)
                total = jnp.zeros((80, block_q), f32)
            else:
                peak = peak_in[h, :1, cols]
                total = sum_in[h, :, cols]
            for j in range(rows_in // block_k):
                ks = slice(j * block_k, (j + 1) * block_k)
                s = lax.dot_general(kx_ref[h, ks, :], q, CONTRACT_LAST, preferred_element_type=f32)
                new_peak = jnp.maximum(peak, jnp.max(s, axis=0, keepdims=True))
                prob = jnp.exp2(s - new_peak).astype(bf16)
                total = total * jnp.exp2(peak - new_peak) + jnp.dot(
                    vt_ref[h, :, ks], prob, preferred_element_type=f32
                )
                peak = new_peak
            if last:
                denom = total[HEAD_DIM : HEAD_DIM + 1]
                n_high, n_mid, n_low = split_three(-(peak + jnp.log2(denom)))
                tall = jnp.concatenate(
                    [
                        total[:HEAD_DIM] / denom,
                        n_high,
                        n_mid,
                        n_low,
                        jnp.zeros((HEAD_DIM - 3, block_q), f32),
                    ],
                    axis=0,
                )
                attx_ref[h, cols, :] = tall.T
            else:
                peak_out[h, :, cols] = jnp.broadcast_to(peak, (8, block_q))
                sum_out[h, :, cols] = total
    if last:
        for p in range(4):
            rows = slice(p * piece_rows, (p + 1) * piece_rows)
            heads = [attx_ref[h, rows, :] for h in range(OWN_HEADS)]
            pair = jnp.where(low, heads[0], pltpu.roll(heads[1], HEAD_DIM, 1))
            att_refs[p][:, :LANES] = pair.astype(bf16)
            att_refs[p][:, LANES:] = heads[2][:, :HEAD_DIM].astype(bf16)
            for h in range(OWN_HEADS):
                qx2_ref[h, rows, :LANES] = qx_ref[h, rows, :LANES]
                old = qx_ref[h, rows, LANES:].astype(f32)
                qx2_ref[h, rows, LANES:] = jnp.where(three, heads[h], old).astype(bf16)


def vmem_specs(n):
    return [pl.BlockSpec(memory_space=pltpu.VMEM) for _ in range(n)]


def attend_chunk(first, last, where, pieces, weights, carry):
    piece_rows = pieces[0].shape[0]
    rows = 4 * piece_rows
    operands = [where, *pieces, *weights]
    operands += [] if first else list(carry)
    wide_keys = jax.ShapeDtypeStruct((OWN_HEADS, rows, 2 * LANES), bf16)
    out_shape = [wide_keys, jax.ShapeDtypeStruct((OWN_HEADS, rows, LANES), bf16)]
    if first:
        out_shape += [wide_keys, jax.ShapeDtypeStruct((OWN_HEADS, rows, LANES), bf16)]
    if last:
        out_shape += [jax.ShapeDtypeStruct((piece_rows, OWN_WIDTH), bf16)] * 4
        out_shape += [jax.ShapeDtypeStruct((OWN_HEADS, rows, LANES), f32), wide_keys]
    else:
        out_shape += [
            jax.ShapeDtypeStruct((OWN_HEADS, 8, rows), f32),
            jax.ShapeDtypeStruct((OWN_HEADS, 80, rows), f32),
        ]
    return pl.pallas_call(
        partial(forward_kernel, first, last, min(512, rows), min(1024, rows)),
        out_shape=out_shape,
        in_specs=[pl.BlockSpec(memory_space=pltpu.SMEM)] + vmem_specs(len(operands) - 1),
        out_specs=vmem_specs(len(out_shape)),
        scratch_shapes=[pltpu.VMEM((OWN_HEADS, 80, rows), bf16)],
        compiler_params=pltpu.CompilerParams(vmem_limit_bytes=VMEM_BYTES),
        cost_estimate=pl.CostEstimate(
            flops=int(8e9), transcendentals=OWN_HEADS * rows * rows, bytes_accessed=int(1e7)
        ),
        name="attend_forward",
    )(*operands)


def backward_kernel(first, last, block_q, block_k, *refs):
    refs = list(refs)
    kx_ref, vx_ref, qx_ref, qp_ref, w_ref = [refs.pop(0) for _ in range(5)]
    pieces = [refs.pop(0) for _ in range(4)]
    if first:
        grads = [refs.pop(0) for _ in range(4)]
        attx_ref = refs.pop(0)
    else:
        dox_ref, dqt_in, dw_in, col_in = [refs.pop(0) for _ in range(4)]
    keep_ref, send_ref = [refs.pop(0) for _ in range(2)]
    if first:
        dox_ref = refs.pop(0)
    if last:
        dw_out, col_out = [refs.pop(0) for _ in range(2)]
        dqt_ref = refs.pop()
    else:
        dqt_ref, dw_out, col_out = [refs.pop(0) for _ in range(3)]
    kt_ref, all_ref = refs
    rows_in = kx_ref.shape[1]
    piece_rows = rows_in // 4
    scale = HEAD_DIM**-0.5
    lane = lax.broadcasted_iota(jnp.int32, (piece_rows, LANES), 1)
    if first:
        for p in range(4):
            rows = slice(p * piece_rows, (p + 1) * piece_rows)
            left = grads[p][:, :LANES].astype(f32)
            right = grads[p][:, LANES:].astype(f32)
            right = jnp.concatenate([right, jnp.zeros_like(right)], axis=1)
            for h, wide in enumerate((left, pltpu.roll(left, HEAD_DIM, 1), right)):
                grad = jnp.where(lane < HEAD_DIM, wide, 0.0)
                delta = jnp.sum(grad * attx_ref[h, rows, :], axis=1, keepdims=True)
                d_high, d_mid, d_low = split_three(delta)
                grad = jnp.where(lane == HEAD_DIM, d_high, grad)
                grad = jnp.where(lane == HEAD_DIM + 1, d_mid, grad)
                grad = jnp.where(lane == HEAD_DIM + 2, d_low, grad)
                dox_ref[h, rows, :] = grad.astype(bf16)
        dqt_ref[...] = jnp.zeros_like(dqt_ref)
    else:
        dqt_ref[...] = dqt_in[...]
    for h in range(OWN_HEADS):
        kt_ref[h] = kx_ref[h, :, LANES:].astype(f32).T[:HEAD_DIM].astype(bf16)
    lane_k = lax.broadcasted_iota(jnp.int32, (block_k, LANES), 1)
    low_k = lane_k < HEAD_DIM
    for j in range(rows_in // block_k):
        ks = slice(j * block_k, (j + 1) * block_k)
        parts = {}
        for h in range(OWN_HEADS):
            k = kx_ref[h, ks, :]
            v = vx_ref[h, ks, :]
            kt = kt_ref[h, :, ks]
            dk = jnp.zeros((block_k, LANES), f32)
            dv = jnp.zeros((block_k, LANES), f32)
            for i in range(rows_in // block_q):
                qs = slice(i * block_q, (i + 1) * block_q)
                s = lax.dot_general(k, qx_ref[h, qs, :], CONTRACT_LAST, preferred_element_type=f32)
                prob = jnp.exp2(s)
                do = dox_ref[h, qs, :]
                dp = lax.dot_general(v, do, CONTRACT_LAST, preferred_element_type=f32)
                ds = (prob * dp).astype(bf16)
                dv = dv + jnp.dot(prob.astype(bf16), do, preferred_element_type=f32)
                dk = dk + jnp.dot(ds, qp_ref[h, qs, :], preferred_element_type=f32)
                dqt_ref[h, :, qs] += jnp.dot(kt, ds, preferred_element_type=f32)
            parts[OWN_HEADS + h] = dk * scale
            parts[2 * OWN_HEADS + h] = dv
        for tile in range(1, WIDE // LANES):
            left, right = parts.get(2 * tile), parts.get(2 * tile + 1)
            left = jnp.zeros((block_k, LANES), f32) if left is None else left
            right = 0.0 if right is None else pltpu.roll(right, HEAD_DIM, 1)
            both = jnp.where(low_k, left, right).astype(bf16)
            all_ref[ks, tile * LANES : (tile + 1) * LANES] = both
    if last:
        tall = jnp.concatenate([dqt_ref[0], dqt_ref[1]], axis=0) * scale
        all_ref[:, :LANES] = tall.T.astype(bf16)
        tall = dqt_ref[2] * scale
        tall = jnp.concatenate([tall, jnp.zeros_like(tall)], axis=0).T
        lane_all = lax.broadcasted_iota(jnp.int32, (rows_in, LANES), 1)
        old = all_ref[:, LANES : 2 * LANES].astype(f32)
        all_ref[:, LANES : 2 * LANES] = jnp.where(lane_all < HEAD_DIM, tall, old).astype(bf16)
    skip = 0 if last else LANES
    d_weight = [None, None]
    for p in range(4):
        rows = slice(p * piece_rows, (p + 1) * piece_rows)
        own = all_ref[rows, skip:]
        dx = lax.dot_general(own, w_ref[:, skip:], CONTRACT_LAST, preferred_element_type=f32)
        out_ref = keep_ref if p % 2 == 0 else send_ref
        out_ref[p // 2] = dx.astype(bf16)
        piece = lax.dot_general(
            pieces[p][...], own, (((0,), (0,)), ((), ())), preferred_element_type=f32
        )
        d_weight[0] = piece if p == 0 else d_weight[0] + piece
        col = jnp.sum(own.astype(f32), axis=0, keepdims=True)
        d_weight[1] = col if p == 0 else d_weight[1] + col
    grad, col = d_weight
    if last:
        dw_out[:, :LANES] = grad[:, :LANES].astype(bf16)
        dw_out[:, LANES:] = (grad[:, LANES:] + dw_in[...]).astype(bf16)
        col_out[:, :LANES] = jnp.broadcast_to(col[:, :LANES], (8, LANES))
        col_out[:, LANES:] = col[:, LANES:] + col_in[...]
    elif first:
        dw_out[...] = grad
        col_out[...] = jnp.broadcast_to(col, col_out.shape)
    else:
        dw_out[...] = grad + dw_in[...]
        col_out[...] = col + col_in[...]


def attend_back_chunk(first, last, chunk, pieces, shared, carry):
    kx, vx = chunk
    qx2, qp, w, grads, attx = shared
    rows, width = kx.shape[1], w.shape[0]
    operands = [kx, vx, qx2, qp, w, *pieces]
    operands += [*grads, attx] if first else list(carry)
    half = jax.ShapeDtypeStruct((2, rows // 4, width), bf16)
    out_shape = [half, half]
    scratch = [
        pltpu.VMEM((OWN_HEADS, HEAD_DIM, rows), bf16),
        pltpu.VMEM((rows, WIDE), bf16),
    ]
    if first:
        out_shape.append(jax.ShapeDtypeStruct((OWN_HEADS, rows, LANES), bf16))
    if last:
        out_shape.append(jax.ShapeDtypeStruct((width, WIDE), bf16))
        out_shape.append(jax.ShapeDtypeStruct((8, WIDE), f32))
        scratch.append(pltpu.VMEM((OWN_HEADS, HEAD_DIM, rows), f32))
    else:
        out_shape.append(jax.ShapeDtypeStruct((OWN_HEADS, HEAD_DIM, rows), f32))
        out_shape.append(jax.ShapeDtypeStruct((width, WIDE - LANES), f32))
        out_shape.append(jax.ShapeDtypeStruct((8, WIDE - LANES), f32))
    return pl.pallas_call(
        partial(backward_kernel, first, last, min(512, rows), min(512, rows)),
        out_shape=out_shape,
        in_specs=vmem_specs(len(operands)),
        out_specs=vmem_specs(len(out_shape)),
        scratch_shapes=scratch,
        compiler_params=pltpu.CompilerParams(vmem_limit_bytes=VMEM_BYTES),
        cost_estimate=pl.CostEstimate(
            flops=int(1.5e10), transcendentals=OWN_HEADS * rows * rows, bytes_accessed=int(1e7)
        ),
        name="attend_backward",
    )(*operands)


def norm_forward(value, gain, shift):
    center = value - jnp.mean(value, axis=-1, keepdims=True)
    spread = jnp.mean(center * center, axis=-1, keepdims=True)
    inverse = lax.rsqrt(spread + norm_eps)
    normal = center * inverse
    return normal * gain + shift, normal, inverse


def norm_backward(grad, gain, normal, inverse):
    inner = grad * gain
    mean = jnp.mean(inner, axis=-1, keepdims=True)
    along = jnp.mean(inner * normal, axis=-1, keepdims=True)
    return inverse * (inner - mean - normal * along)


CONTRACT_FIRST = (((0,), (0,)), ((), ()))


def ffn_kernel(layout, *refs):
    n_q, n_b, own_rows, fold, aligned = layout
    refs = list(refs)
    where_ref = refs.pop(0)
    att_refs = [refs.pop(0) for _ in range(4)]
    x_ref, cot_ref, vec_ref, eb_ref, packed = [refs.pop(0) for _ in range(5)]
    out_ref, resid_ref = [refs.pop(0) for _ in range(2)]
    da_refs = [refs.pop(0) for _ in range(4)]
    vec_out = refs.pop(0)
    targets = [refs.pop(0) for _ in range(4 if aligned else 2)]
    wo, w1, w2, go, g1, g2, act, slope, in_sem, out_sem = refs
    group, zi, xi, ci, bi, start, length = [where_ref[i] for i in range(7)]
    rows, width = x_ref.shape

    def lanes(i):
        return slice(i * width, (i + 1) * width)

    loads = [pltpu.make_async_copy(packed.at[:, lanes(0)], wo, in_sem.at[0])]
    for k in range(fold):
        loads.append(pltpu.make_async_copy(packed.at[:, lanes(1 + k)], w1.at[k], in_sem.at[1 + k]))
    for k in range(fold):
        sem = in_sem.at[1 + fold + k]
        loads.append(pltpu.make_async_copy(packed.at[:, lanes(1 + fold + k)], w2.at[k], sem))
    for load in loads:
        load.start()

    def group_rows(r):
        other = (2 * (xi ^ (r // 2))) + (ci ^ (r % 2))
        return pl.ds(pl.multiple_of(other * OWN_WIDTH, HEAD_DIM), OWN_WIDTH)

    obias, gain1, shift1, sbias, gain2, shift2 = [vec_ref[i : i + 1, :] for i in range(2, 8)]
    loads[0].wait()
    branch = obias + jnp.zeros((rows, width), f32)
    for r in range(4):
        branch += jnp.dot(att_refs[r][...], wo[group_rows(r), :], preferred_element_type=f32)
    hidden, normal1, inverse1 = norm_forward(x_ref[...].astype(f32) + branch, gain1, shift1)
    hidden_low = hidden.astype(bf16)
    shrunk = sbias + hidden
    for k in range(fold):
        loads[1 + k].wait()
        expanded = jnp.dot(hidden_low, w1[k], preferred_element_type=f32) + eb_ref[k : k + 1, :]
        cdf = 0.5 * (1.0 + lax.erf(expanded * (2.0**-0.5)))
        pdf = jnp.exp(-0.5 * expanded * expanded) * ((2.0 * math.pi) ** -0.5)
        act[k] = (expanded * cdf).astype(bf16)
        slope[k] = cdf + expanded * pdf
        loads[1 + fold + k].wait()
        shrunk += jnp.dot(act[k], w2[k], preferred_element_type=f32)
    result, normal2, inverse2 = norm_forward(shrunk, gain2, shift2)
    out_ref[...] = result.astype(bf16)
    row = lax.broadcasted_iota(jnp.int32, (rows, width), 0)
    seed = jnp.where(start + row < length, cot_ref[...].astype(f32), 0.0)
    vec_out[4:5, :] = jnp.sum(seed * normal2, axis=0, keepdims=True)
    vec_out[5:6, :] = jnp.sum(seed, axis=0, keepdims=True)
    resid2 = norm_backward(seed, gain2, normal2, inverse2)
    shrunk_low = resid2.astype(bf16)
    vec_out[3:4, :] = jnp.sum(shrunk_low.astype(f32), axis=0, keepdims=True)
    hidden_grad = resid2
    for k in range(fold):
        active_grad = lax.dot_general(
            shrunk_low, w2[k], CONTRACT_LAST, preferred_element_type=f32
        )
        expanded_low = (active_grad * slope[k]).astype(bf16)
        vec_out[8 + k : 9 + k, :] = jnp.sum(expanded_low.astype(f32), axis=0, keepdims=True)
        hidden_grad += lax.dot_general(
            expanded_low, w1[k], CONTRACT_LAST, preferred_element_type=f32
        )
        g2[k] = lax.dot_general(
            act[k], shrunk_low, CONTRACT_FIRST, preferred_element_type=f32
        ).astype(bf16)
        g1[k] = lax.dot_general(
            hidden_low, expanded_low, CONTRACT_FIRST, preferred_element_type=f32
        ).astype(bf16)
    vec_out[1:2, :] = jnp.sum(hidden_grad * normal1, axis=0, keepdims=True)
    vec_out[2:3, :] = jnp.sum(hidden_grad, axis=0, keepdims=True)
    resid1 = norm_backward(hidden_grad, gain1, normal1, inverse1)
    resid_ref[...] = resid1
    branch_low = resid1.astype(bf16)
    vec_out[0:1, :] = jnp.sum(branch_low.astype(f32), axis=0, keepdims=True)
    vec_out[6:8, :] = jnp.zeros((2, width), f32)
    vec_out[8 + fold :, :] = jnp.zeros((vec_out.shape[0] - 8 - fold, width), f32)
    for r in range(4):
        da_refs[r][...] = lax.dot_general(
            branch_low, wo[group_rows(r), :], CONTRACT_LAST, preferred_element_type=f32
        ).astype(bf16)
        go[group_rows(r), :] = lax.dot_general(
            att_refs[r][...], branch_low, CONTRACT_FIRST, preferred_element_type=f32
        ).astype(bf16)
    block = n_b * own_rows
    for dc in range(2 if aligned else 1):
        to_one, to_two = targets[2 * dc : 2 * dc + 2]
        if not aligned:
            for k, src in enumerate([go] + [g1.at[k] for k in range(fold)]):
                pltpu.make_async_copy(src, to_one.at[:, lanes(k)], out_sem.at[0]).start()
            for k in range(fold):
                pltpu.make_async_copy(g2.at[k], to_two.at[:, lanes(k)], out_sem.at[1]).start()
            continue
        for dx in range(2):
            for jz in range(n_q):
                m = (lax.rem(zi + jz, n_q) * 2 + (xi ^ dx)) * 2 + (ci ^ dc)
                at = pl.ds(pl.multiple_of(m * block, 16), block)
                for k, src in enumerate([go] + [g1.at[k] for k in range(fold)]):
                    dst = to_one.at[dx, jz, :, lanes(k)]
                    pltpu.make_async_copy(src.at[at], dst, out_sem.at[2 * dc]).start()
                for k in range(fold):
                    dst = to_two.at[dx, jz, :, lanes(k)]
                    pltpu.make_async_copy(g2.at[k, at], dst, out_sem.at[2 * dc + 1]).start()
    for i, dst in enumerate(targets):
        pltpu.make_async_copy(dst, dst, out_sem.at[i]).wait()


def ffn_block(layout, where, att, x, cot, vectors, ebias, packed):
    n_q, n_b, own_rows, fold, aligned = layout
    rows, width = x.shape
    ff = fold * width
    operands = [where, *att, x, cot, vectors, ebias, packed]
    in_specs = [pl.BlockSpec(memory_space=pltpu.SMEM)] + vmem_specs(8)
    in_specs += [pl.BlockSpec(memory_space=pl.ANY)]
    out_shape = [
        jax.ShapeDtypeStruct((rows, width), bf16),
        jax.ShapeDtypeStruct((rows, width), f32),
        *[jax.ShapeDtypeStruct((rows, OWN_WIDTH), bf16)] * 4,
        jax.ShapeDtypeStruct((16, width), f32),
    ]
    lead = (2, n_q, n_b * own_rows) if aligned else (width,)
    pair = [jax.ShapeDtypeStruct((*lead, width + ff), bf16), jax.ShapeDtypeStruct((*lead, ff), bf16)]
    targets = pair + pair if aligned else pair
    weight_scratch = [
        pltpu.VMEM((width, width), bf16),
        pltpu.VMEM((fold, width, width), bf16),
        pltpu.VMEM((fold, width, width), bf16),
    ]
    return pl.pallas_call(
        partial(ffn_kernel, layout),
        out_shape=out_shape + targets,
        in_specs=in_specs,
        out_specs=vmem_specs(len(out_shape)) + [pl.BlockSpec(memory_space=pl.ANY)] * len(targets),
        scratch_shapes=weight_scratch
        + weight_scratch
        + [
            pltpu.VMEM((fold, rows, width), bf16),
            pltpu.VMEM((fold, rows, width), f32),
            pltpu.SemaphoreType.DMA((1 + 2 * fold,)),
            pltpu.SemaphoreType.DMA((4,)),
        ],
        compiler_params=pltpu.CompilerParams(vmem_limit_bytes=VMEM_BYTES),
        cost_estimate=pl.CostEstimate(
            flops=int(2e10), transcendentals=2 * rows * ff, bytes_accessed=int(3e7)
        ),
        name="feed_forward",
    )(*operands)


def from_shift(value, axis, count, step):
    return lax.ppermute(value, axis, [((i + step) % count, i) for i in range(count)])


def square_swap(value, r):
    if r == 0:
        return value
    if r == 1:
        return lax.ppermute(value, "c", [(0, 1), (1, 0)])
    if r == 2:
        return lax.ppermute(value, "x", [(0, 1), (1, 0)])
    return lax.ppermute(value, ("x", "c"), [(0, 3), (3, 0), (1, 2), (2, 1)])


def pick(stacked, index, dim=0):
    return lax.dynamic_index_in_dim(stacked, index, dim, keepdims=False)


def after(value, *others):
    return lax.optimization_barrier((value, *others))[0]


def sum_to_owner(keep, send, n_q, n_b, bi):
    total = keep.astype(f32) + square_swap(send, 1).astype(f32)
    total = total.reshape(2, n_q, n_b, -1, keep.shape[-1])
    own = pick(total, bi, 2)
    for j in range(1, n_b):
        away = pick(total, (bi + j) % n_b, 2).astype(bf16)
        own = own + from_shift(away, "b", n_b, n_b - j).astype(f32)
    for axis, count in (("x", 2), ("q", n_q)):
        total = own
        own = total[0]
        for j in range(1, count):
            own = own + from_shift(total[j].astype(bf16), axis, count, count - j).astype(f32)
    return own


def deinterleave(fold):
    size = fold * LANES
    lane = jnp.arange(size)
    return (lane[:, None] // fold + (lane[:, None] % fold) * LANES == lane[None, :]).astype(bf16)


def per_device(
    n_q,
    n_b,
    inputs,
    lengths,
    cotangent,
    triple_weight,
    query_bias,
    value_bias,
    output_weight,
    output_bias,
    first_gain,
    first_shift,
    expand_weight,
    expand_bias,
    shrink_weight,
    shrink_bias,
    second_gain,
    second_shift,
):
    zi, xi, ci, bi = [lax.axis_index(a) for a in AXES]
    group = 2 * xi + ci
    _, seq_rows, width = inputs.shape
    own_rows = triple_weight.shape[0]
    ff = expand_weight.shape[1]
    fold = ff // width
    aligned = n_b * own_rows % 16 == 0
    x_own = inputs[0]

    turn = deinterleave(fold)
    expand_own = expand_weight.astype(bf16).reshape(own_rows, -1, fold * LANES)
    expand_own = jnp.einsum("rbs,st->rbt", expand_own, turn, preferred_element_type=f32)
    expand_own = expand_own.astype(bf16).reshape(own_rows, -1, fold, LANES).transpose(0, 2, 1, 3)
    packed = jnp.concatenate(
        [
            output_weight.astype(bf16),
            expand_own.reshape(own_rows, ff),
            shrink_weight.astype(bf16).reshape(own_rows, ff),
        ],
        axis=1,
    )
    gathered_ffn = lax.all_gather(packed, AXES, axis=0, tiled=True)

    names = [query_bias, value_bias, output_bias, first_gain, first_shift]
    names += [shrink_bias, second_gain, second_shift]
    vectors = jnp.stack(names, axis=1)
    vectors = jnp.concatenate([vectors, expand_bias.reshape(own_rows, fold)], axis=1).astype(bf16)
    n_vec = vectors.shape[1]
    vectors = jnp.pad(vectors, ((0, 0), (0, WIDE - VECTORS - n_vec)))
    thirds = triple_weight.astype(bf16).reshape(own_rows, 3, GROUPS, OWN_WIDTH)

    def columns_of(g):
        mine = [pick(thirds[:, t], g, 1) for t in range(3)]
        return jnp.concatenate(mine + [vectors], axis=1)

    square = jnp.stack([square_swap(columns_of(group ^ r), r) for r in range(4)])
    rows_q = jnp.stack([square] + [from_shift(square, "q", n_q, j) for j in range(1, n_q)])
    rows_b = jnp.stack([rows_q] + [from_shift(rows_q, "b", n_b, j) for j in range(1, n_b)])
    ordered = jnp.stack([pick(rows_b, (i - bi) % n_b) for i in range(n_b)], axis=3)
    ordered = jnp.stack([pick(ordered, group ^ g, 1) for g in range(4)], axis=1)
    ordered = jnp.stack([pick(ordered, (i - zi) % n_q) for i in range(n_q)])
    w_own = ordered.transpose(0, 1, 3, 2, 4).reshape(width, WIDE)
    turned = w_own[:, VECTORS : VECTORS + n_vec].astype(f32)
    turned = turned.T
    ebias = turned[8:]
    turned = turned[:8]
    own_bias = lax.dynamic_slice_in_dim(turned, group * OWN_WIDTH, OWN_WIDTH, 1)
    zero = jnp.zeros((1, OWN_WIDTH), f32)
    bias_row = jnp.concatenate(
        [own_bias[:1], zero, own_bias[1:2], jnp.zeros((1, WIDE - VECTORS), f32)], axis=1
    )

    chunk_x = {}
    tie = []
    for j in [0] + [k for pair in zip(range(1, n_q), range(n_q - 1, 0, -1)) for k in pair]:
        if j in chunk_x:
            continue
        own = x_own if j == 0 else from_shift(after(x_own, *tie), "q", n_q, j)
        tie = [] if j == 0 else [own]
        chunk_x[j] = [own, None, square_swap(own, 2), None]
    for j, piece in chunk_x.items():
        halves = square_swap(jnp.stack([piece[0], piece[2]]), 1)
        piece[1], piece[3] = halves[0], halves[1]
    arrival = list(chunk_x)

    def where_of(j):
        zj = (zi + j) % n_q
        spots = [(zj * 4 + (group ^ r)) * seq_rows for r in range(4)]
        return jnp.stack(spots + [lengths[0]]).astype(jnp.int32)

    weights = (w_own, bias_row)
    kept = {}
    carry = None
    for step, j in enumerate(arrival):
        first, last = step == 0, step == n_q - 1
        outs = attend_chunk(first, last, where_of(j), chunk_x[j], weights, carry)
        kept[j] = (outs[0], outs[1])
        outs = outs[2:]
        if first:
            qx, qp = outs[:2]
            outs = outs[2:]
        carry = (qx, *outs)
    att, attx, qx2 = carry[1:5], carry[5], carry[6]

    att = [square_swap(att[r], r) for r in range(4)]
    start = (zi * 4 + group) * seq_rows
    where = jnp.stack([group, zi, xi, ci, bi, start, lengths[0]]).astype(jnp.int32)
    layout = (n_q, n_b, own_rows, fold, aligned)
    outs = ffn_block(layout, where, att, x_own, cotangent[0], turned, ebias, gathered_ffn)
    output, resid_first_grad = outs[:2]
    att_grads, vec_grads, summands = outs[2:6], outs[6], outs[7:]
    grads = [square_swap(att_grads[r], r) for r in range(4)]

    if aligned:
        one_keep, two_keep, one_send, two_send = summands
        summed_two = sum_to_owner(two_keep, two_send, n_q, n_b, bi)
        summed_one = sum_to_owner(one_keep, one_send, n_q, n_b, bi)
    else:
        summed = lax.psum_scatter(
            jnp.concatenate(summands, axis=1), AXES, scatter_dimension=0, tiled=True
        ).astype(f32)
        summed_one, summed_two = summed[:, : width + ff], summed[:, width + ff :]

    shared = (qx2, qp, w_own, grads, attx)
    carry = None
    token_grad = resid_first_grad
    for step, j in enumerate(reversed(arrival)):
        first, last = step == 0, step == n_q - 1
        outs = attend_back_chunk(first, last, kept[j], chunk_x[j], shared, carry)
        keep, send = outs[:2]
        outs = outs[2:]
        if first:
            dox = outs[0]
            outs = outs[1:]
        carry = (dox, *outs)
        dx = keep.astype(f32) + square_swap(send, 1).astype(f32)
        dx = dx[0] + square_swap(dx[1].astype(bf16), 2).astype(f32)
        if j:
            dx = from_shift(dx.astype(bf16), "q", n_q, n_q - j).astype(f32)
        token_grad = token_grad + dx
    input_grad = token_grad.astype(bf16)
    grad_joint, col = carry[1:]

    own_bias = jnp.stack([col[0, :OWN_WIDTH], col[0, 2 * OWN_WIDTH : 3 * OWN_WIDTH]])
    bias_grads = lax.dynamic_update_slice(
        jnp.zeros((2, width), f32), own_bias, (0, group * OWN_WIDTH)
    )
    tall = jnp.concatenate([bias_grads, vec_grads[:6], vec_grads[8 : 8 + fold]], axis=0).T
    tall_high = tall.astype(bf16)
    tall_low = (tall - tall_high.astype(f32)).astype(bf16)
    room = jnp.zeros((width, WIDE - VECTORS - 2 * n_vec), bf16)
    blocks = jnp.concatenate([grad_joint[:, :VECTORS], tall_high, tall_low, room], axis=1)
    total = blocks.reshape(n_q, 4, n_b, own_rows, WIDE)
    total = jnp.stack([pick(total, (bi + j) % n_b, 2) for j in range(n_b)])
    for axis, count, index in (("b", n_b, bi), ("q", n_q, zi)):
        if axis == "q":
            total = jnp.stack([pick(total, (zi + j) % n_q) for j in range(n_q)])
        own = total[0].astype(f32)
        for j in range(1, count):
            own = own + from_shift(total[j].astype(bf16), axis, count, count - j).astype(f32)
        total = own
    total = total.astype(bf16)
    parts = jnp.stack([square_swap(pick(total, group ^ r), r) for r in range(4)])
    parts = jnp.stack([pick(parts, group ^ g) for g in range(4)])
    grad_triple = parts[:, :, :VECTORS].reshape(GROUPS, own_rows, 3, OWN_WIDTH)
    grad_triple = grad_triple.transpose(1, 2, 0, 3).reshape(own_rows, -1).astype(f32)
    small = jnp.sum(parts[:, :, VECTORS : VECTORS + 2 * n_vec].astype(f32), axis=0)
    small = small[:, :n_vec] + small[:, n_vec:]
    grad_expand = summed_one[:, width:].reshape(own_rows, fold, -1, LANES).transpose(0, 2, 1, 3)
    grad_expand = jnp.einsum(
        "rbs,ts->rbt",
        grad_expand.reshape(own_rows, -1, fold * LANES),
        turn.astype(f32),
        precision=lax.Precision.HIGHEST,
        preferred_element_type=f32,
    ).reshape(own_rows, ff)
    return (
        output[None],
        input_grad[None],
        grad_triple,
        small[:, 0],
        small[:, 1],
        summed_one[:, :width],
        small[:, 2],
        small[:, 3],
        small[:, 4],
        grad_expand,
        small[:, 8:].reshape(-1),
        summed_two.reshape(-1, width),
        small[:, 5],
        small[:, 6],
        small[:, 7],
    )


def solution(mesh):
    n_seq, n_b = mesh.shape["seq"], mesh.shape["batch"]
    n_q = n_seq // GROUPS
    fine = Mesh(mesh.devices.reshape(n_q, 2, 2, n_b), AXES)
    tokens = P("b", ("q", "x", "c"), None)
    matrix = P(AXES, None)
    vector = P(AXES)
    in_specs = (
        tokens,
        P("b"),
        tokens,
        matrix,
        vector,
        vector,
        matrix,
        vector,
        vector,
        vector,
        matrix,
        vector,
        matrix,
        vector,
        vector,
        vector,
    )
    out_specs = (
        tokens,
        tokens,
        matrix,
        vector,
        vector,
        matrix,
        vector,
        vector,
        vector,
        matrix,
        vector,
        matrix,
        vector,
        vector,
        vector,
    )
    return jax.shard_map(
        partial(per_device, n_q, n_b),
        mesh=fine,
        in_specs=in_specs,
        out_specs=out_specs,
        check_vma=False,
    )
```

time: 495 us -> 457 us (0.923)
  local copies, waits for them, and re-layouts: 66.9 us -> 24.3 us
  waiting for transfers between devices: 157 us -> 195 us
  matrix products: 36.3 us -> 1.18 us
  Pallas kernels: 111 us -> 128 us
  other arithmetic: 33.6 us -> 22.6 us
    dot_general x14 -> x2, matrix products: 36.3 us -> 1.18 us  [the longest x1 0.8 us: per_device(): jnp.einsum('rbs,ts->rbt', grad_expand.reshape(own_rows, -1, fold * LANES)...]
    ppermute x18 -> x24, waiting for transfers between devices: 118 us -> 145 us  [from_shift(): lax.ppermute(value, axis, [((i + step) % count, i) for i in range(count)])]
    pallas_call x0 -> x1, Pallas kernels: none -> 20.3 us  [ffn_block(): pl.pallas_call(partial(ffn_kernel, layout), out_shape=out_shape + targets...]
    reshape x16 -> x10, local copies, waits for them, and re-layouts: 16.5 us -> 2.9 us  [the longest x1 0.8 us: per_device(): summed_two.reshape(-1, width)]
    unnamed x90 -> x72, local copies, waits for them, and re-layouts: 10.9 us -> 2.24 us
    another operation x10 -> x9, local copies, waits for them, and re-layouts: 8.7 us -> 1.38 us  [the longest x8 0.78 us: per_device(): vectors = jnp.stack(names, axis=1)]
    reduce_sum x12 -> x1, other arithmetic: 7.27 us -> 0.08 us  [per_device(): jnp.sum(parts[:, :, VECTORS:VECTORS + 2 * n_vec].astype(f32), axis=0)]
    transpose x5 -> x1, local copies, waits for them, and re-layouts: 7.18 us -> 0.08 us  [per_device(): summed_one[:, width:].reshape(own_rows, fold, -1, LANES)]
  transfers between devices with their start and end apart: 55 -> 55, of which waited for: 21 -> 31; matrix products, arithmetic and copies ran while one was open for 18% -> 9% of each run, Pallas kernels for 23% -> 9%
where the time goes in v2:
time: 457 us; the launch traced here: 453 us
  waiting for transfers between devices  195 us (43%)
  Pallas kernels  128 us (28%)
  starting transfers between devices  65.2 us (14%)
  local copies, waits for them, and re-layouts  24.3 us (5%)
  other arithmetic  22.6 us (5%)
  between operations  16.2 us (4%)
    ppermute x24, waiting for transfers between devices, from_shift(): lax.ppermute(value, axis, [((i + step) % count, i) for i in range(count)])  145 us
    pallas_call x4, Pallas kernels, attend_back_chunk(): pl.pallas_call(partial(backward_kernel, first, last, min(512, rows), min(...  64.8 us
    ppermute x24, starting transfers between devices, from_shift(): lax.ppermute(value, axis, [((i + step) % count, i) for i in range(count)])  49 us
    pallas_call x4, Pallas kernels, attend_chunk(): pl.pallas_call(partial(forward_kernel, first, last, min(512, rows), min(1...  42.9 us
    ppermute x12, waiting for transfers between devices, square_swap(): return lax.ppermute(value, 'x', [(0, 1), (1, 0)])  40.5 us
    pallas_call x1, Pallas kernels, ffn_block(): pl.pallas_call(partial(ffn_kernel, layout), out_shape=out_shape + targets...  20.3 us
    ppermute x12, starting transfers between devices, square_swap(): return lax.ppermute(value, 'x', [(0, 1), (1, 0)])  10.3 us
  transfers between devices with their start and end apart: 55, of which 31 were waited for; matrix products, arithmetic and copies ran while one was open for 9% of the time, Pallas kernels for 9%

profile of v2, /device:TPU:0, one launch (start us, length us, event | category | flops | bytes accessed | tf_op | source)
XLA Modules:
  0.0 452.6 jit_solution(13553222940418300009)
XLA Ops:
  18.5 3.7 collective-permute-start.8
  24.0 4.2 collective-permute-done.8
  28.2 10.5 %collective-permute-done.9 = bf16[4,24,640]{2,1,0:T(8,128)(2,1)S(1)} collective-permute-done((bf16[4,24,640]{2,1,0:T(8,128)(2,1)S(1)}, bf16[4,24,640]{2,1,0:T(8,128)(2,1)S(1)}, u32[]{:S(2)}, u32[]{:S(2)}) %collective-permute-start.9) | collective-permute-done | bytes 122912 | tf_op jit(solution)/shard_map/ppermute | solution.py:496
  53.8 12.6 %collective-permute-done.1.refs_1_.refs_5_ = bf16[256,768]{1,0:T(8,128)(2,1)} collective-permute-done((bf16[256,768]{1,0:T(8,128)(2,1)}, bf16[256,768]{1,0:T(8,128)(2,1)}, u32[]{:S(2)}, u32[]{:S(2)}) %collective-permute-start.1) | collective-permute-done | bytes 393248 | tf_op jit(solution)/shard_map/ppermute | solution.py:496
  66.5 10.2 %collective-permute-start.2 = (bf16[256,768]{1,0:T(8,128)(2,1)}, bf16[256,768]{1,0:T(8,128)(2,1)}, u32[]{:S(2)}, u32[]{:S(2)}) collective-permute-start(bf16[256,768]{1,0:T(8,128)(2,1)} %bitcast.10.refs_1_.refs_5_), channel_id=1, source_target_pairs={{16,0},{24,8},{0,16},{8,24},{17,1},{25,9},{1,17},{9,25},{18,2},{26... | collective-permute-start | bytes 1179656 | tf_op jit(solution)/shard_map/ppermute | solution.py:496
  82.3 10.0 %collective-permute-done.2.refs_1_.refs_5_ = bf16[256,768]{1,0:T(8,128)(2,1)} collective-permute-done((bf16[256,768]{1,0:T(8,128)(2,1)}, bf16[256,768]{1,0:T(8,128)(2,1)}, u32[]{:S(2)}, u32[]{:S(2)}) %collective-permute-start.2) | collective-permute-done | bytes 393248 | tf_op jit(solution)/shard_map/ppermute | solution.py:496
  93.7 10.3 %attend_forward.4 = (bf16[3,1024,256]{2,1,0:T(8,128)(2,1)}, bf16[3,1024,128]{2,1,0:T(8,128)(2,1)}, bf16[3,1024,256]{2,1,0:T(8,128)(2,1)}, bf16[3,1024,128]{2,1,0...) custom-call(s32[5]{0:T(128)} %stack.276.refs_0_, bf16[256,768]{1,0:T(8,128)(2,1)} %bitcast.10.refs_1_.refs_5_, ...), custom_call_target="tpu_custom_call" | custom-call | flops 8000000000 | bytes 10000000 | tf_op jit(solution)/shard_map/attend_forward/pallas_call | solution.py:169
  104.1 6.2 %collective-permute-done.3.refs_3_.refs_7_ = bf16[256,768]{1,0:T(8,128)(2,1)S(1)} collective-permute-done((bf16[256,768]{1,0:T(8,128)(2,1)}, bf16[256,768]{1,0:T(8,128)(2,1)S(1)}, u32[]{:S(2)}, u32[]{:S(2)}) %collective-permute-start.3) | collective-permute-done | bytes 393248 | tf_op jit(solution)/shard_map/ppermute | solution.py:505
  113.7 10.4 %attend_forward.5 = (bf16[3,1024,256]{2,1,0:T(8,128)(2,1)}, bf16[3,1024,128]{2,1,0:T(8,128)(2,1)}, f32[3,8,1024]{2,1,0:T(8,128)}, f32[3,80,1024]{2,1,0:T(8,128)}) custom-call(s32[5]{0:T(128)} %stack.291.refs_0_, bf16[256,768]{1,0:T(8,128)(2,1)} %collective-permute-done.refs_1_.refs_5_, bf16[256,768]{1,0:T(8,128)(2,1)} %get-tuple-element.153.refs_2_.refs_6_, ...), custom_call_target="tpu_custom_call" | custom-call | flops 8000000000 | bytes 10000000 | tf_op jit(solution)/shard_map/attend_forward/pallas_call | solution.py:169
  126.1 10.3 %attend_forward.6 = (bf16[3,1024,256]{2,1,0:T(8,128)(2,1)}, bf16[3,1024,128]{2,1,0:T(8,128)(2,1)}, f32[3,8,1024]{2,1,0:T(8,128)}, f32[3,80,1024]{2,1,0:T(8,128)}) custom-call(s32[5]{0:T(128)} %stack.283.refs_0_, bf16[256,768]{1,0:T(8,128)(2,1)} %collective-permute-done.1.refs_1_.refs_5_, bf16[256,768]{1,0:T(8,128)(2,1)} %get-tuple-element.155.refs_2_.refs_6_, ...), custom_call_target="tpu_custom_call" | custom-call | flops 8000000000 | bytes 10000000 | tf_op jit(solution)/shard_map/attend_forward/pallas_call | solution.py:169
  137.4 11.9 %attend_forward.7 = (bf16[3,1024,256]{2,1,0:T(8,128)(2,1)}, bf16[3,1024,128]{2,1,0:T(8,128)(2,1)}, bf16[256,192]{1,0:T(8,128)(2,1)}, bf16[256,192]{1,0:T(8,128)(...) custom-call(s32[5]{0:T(128)} %stack.242.refs_0_, ...), custom_call_target="tpu_custom_call" | custom-call | flops 8000000000 | bytes 10000000 | tf_op jit(solution)/shard_map/attend_forward/pallas_call | solution.py:169
  158.0 20.3 %feed_forward.1 = (bf16[256,768]{1,0:T(8,128)(2,1)}, f32[256,768]{1,0:T(8,128)}, bf16[256,192]{1,0:T(8,128)(2,1)}, bf16[256,192]{1,0:T(8,128)(2,1)}, bf16[256,19...) custom-call(s32[7]{0:T(128)} %stack.237.refs_0_, ...), custom_call_target="tpu_custom_call" | custom-call | flops 20000000000 | bytes 30000000 | tf_op jit(solution)/shard_map/feed_forward/pallas_call | solution.py:474
  182.1 3.6 collective-permute-done.22.refs_11_
  187.4 15.9 %attend_backward.4 = (bf16[2,256,768]{2,1,0:T(8,128)(2,1)}, bf16[2,256,768]{2,1,0:T(8,128)(2,1)}, bf16[3,1024,128]{2,1,0:T(8,128)(2,1)}, f32[3,64,1024]{2,1,0:T(...) custom-call(bf16[3,1024,256]{2,1,0:T(8,128)(2,1)} %get-tuple-element.85.refs_0_, ...), custom_call_target="tpu_custom_call" | custom-call | flops 15000000512 | bytes 10000000 | tf_op jit(solution)/shard_map/attend_backward/pallas_call | solution.py:311
  203.3 15.9 %attend_backward.5 = (bf16[2,256,768]{2,1,0:T(8,128)(2,1)}, bf16[2,256,768]{2,1,0:T(8,128)(2,1)}, f32[3,64,1024]{2,1,0:T(8,128)}, f32[768,512]{1,0:T(8,128)}, f32[8,512]{1,0:T(8,128)}) custom-call(bf16[3,1024,256]{2,1,0:T(8,128)(2,1)} %get-tuple-element.96.refs_0_, bf16[3,1024,128]{2,1,0:T(8,128)(2,1)} %get-tuple-element.97.refs_1_, ...), custom_call_target="tpu_custom_call" | custom-call | flops 15000000512 | bytes 10000000 | tf_op jit(solution)/shard_map/attend_backward/pallas_call | solution.py:311
  219.2 16.2 %attend_backward.6 = (bf16[2,256,768]{2,1,0:T(8,128)(2,1)}, bf16[2,256,768]{2,1,0:T(8,128)(2,1)}, f32[3,64,1024]{2,1,0:T(8,128)}, f32[768,512]{1,0:T(8,128)}, f32[8,512]{1,0:T(8,128)}) custom-call(bf16[3,1024,256]{2,1,0:T(8,128)(2,1)} %get-tuple-element.104.refs_0_, bf16[3,1024,128]{2,1,0:T(8,128)(2,1)} %get-tuple-element.105.refs_1_, ...), custom_call_target="tpu_custom_call" | custom-call | flops 15000000512 | bytes 10000000 | tf_op jit(solution)/shard_map/attend_backward/pallas_call | solution.py:311
  235.4 16.8 %attend_backward.7 = (bf16[2,256,768]{2,1,0:T(8,128)(2,1)}, bf16[2,256,768]{2,1,0:T(8,128)(2,1)}, bf16[768,640]{1,0:T(8,128)(2,1)}, f32[8,640]{1,0:T(8,128)}) custom-call(bf16[3,1024,256]{2,1,0:T(8,128)(2,1)} %get-tuple-element.111.refs_0_, bf16[3,1024,128]{2,1,0:T(8,128)(2,1)} %get-tuple-element.112.refs_1_, ...), custom_call_target="tpu_custom_call" | custom-call | flops 15000000512 | bytes 10000000 | tf_op jit(solution)/shard_map/attend_backward/pallas_call | solution.py:311
  254.0 13.9 %collective-permute-done.35 = bf16[4,4,24,640]{3,2,1,0:T(8,128)(2,1)S(1)} collective-permute-done((bf16[4,4,24,640]{3,2,1,0:T(8,128)(2,1)S(1)}, bf16[4,4,24,640]{3,2,1,0:T(8,128)(2,1)S(1)}, u32[]{:S(2)}, u32[]{:S(2)}) %collective-permute-start.35) | collective-permute-done | bytes 491552 | tf_op jit(solution)/shard_map/ppermute | solution.py:496
  268.2 3.7 collective-permute-start.38
  271.9 4.2 collective-permute-done.36
  276.2 4.3 collective-permute-done.37
  295.0 6.4 %collective-permute-done.25 = bf16[256,768]{1,0:T(8,128)(2,1)S(1)} collective-permute-done((bf16[256,768]{1,0:T(8,128)(2,1)S(1)}, bf16[256,768]{1,0:T(8,128)(2,1)S(1)}, u32[]{:S(2)}, u32[]{:S(2)}) %collective-permute-start.25) | collective-permute-done | bytes 393248 | tf_op jit(solution)/shard_map/ppermute | solution.py:505
  303.1 6.8 %collective-permute-done.28 = bf16[256,768]{1,0:T(8,128)(2,1)S(1)} collective-permute-done((bf16[256,768]{1,0:T(8,128)(2,1)S(1)}, bf16[256,768]{1,0:T(8,128)(2,1)S(1)}, u32[]{:S(2)}, u32[]{:S(2)}) %collective-permute-start.28) | collective-permute-done | bytes 393248 | tf_op jit(solution)/shard_map/ppermute | solution.py:505
  312.0 6.3 %collective-permute-done.31 = bf16[256,768]{1,0:T(8,128)(2,1)S(1)} collective-permute-done((bf16[256,768]{1,0:T(8,128)(2,1)S(1)}, bf16[256,768]{1,0:T(8,128)(2,1)S(1)}, u32[]{:S(2)}, u32[]{:S(2)}) %collective-permute-start.31) | collective-permute-done | bytes 393248 | tf_op jit(solution)/shard_map/ppermute | solution.py:505
  321.4 4.7 %collective-permute-done.34 = bf16[256,768]{1,0:T(8,128)(2,1)S(1)} collective-permute-done((bf16[256,768]{1,0:T(8,128)(2,1)S(1)}, bf16[256,768]{1,0:T(8,128)(2,1)S(1)}, u32[]{:S(2)}, u32[]{:S(2)}) %collective-permute-start.34) | collective-permute-done | bytes 393248 | tf_op jit(solution)/shard_map/ppermute | solution.py:505
  331.2 8.6 %collective-permute-done.26 = bf16[256,768]{1,0:T(8,128)(2,1)} collective-permute-done((bf16[256,768]{1,0:T(8,128)(2,1)}, bf16[256,768]{1,0:T(8,128)(2,1)}, u32[]{:S(2)}, u32[]{:S(2)}) %collective-permute-start.26) | collective-permute-done | bytes 393248 | tf_op jit(solution)/shard_map/ppermute | solution.py:496
  339.9 4.4 collective-permute-done.29
  354.3 24.2 %collective-permute-done.49 = bf16[2,4,24,3072]{3,2,1,0:T(8,128)(2,1)S(1)} collective-permute-done((bf16[2,4,24,3072]{3,2,1,0:T(8,128)(2,1)S(1)}, bf16[2,4,24,3072]{3,2,1,0:T(8,128)(2,1)S(1)}, u32[]{:S(2)}, u32[]{:S(2)}) %collective-permute-start.49) | collective-permute-done | bytes 1179680 | tf_op jit(solution)/shard_map/ppermute | solution.py:496
  379.7 28.5 %collective-permute-done.43 = bf16[2,4,24,3840]{3,2,1,0:T(8,128)(2,1)S(1)} collective-permute-done((bf16[2,4,24,3840]{3,2,1,0:T(8,128)(2,1)S(1)}, bf16[2,4,24,3840]{3,2,1,0:T(8,128)(2,1)S(1)}, u32[]{:S(2)}, u32[]{:S(2)}) %collective-permute-start.43) | collective-permute-done | bytes 1474592 | tf_op jit(solution)/shard_map/ppermute | solution.py:496
  416.9 8.3 %collective-permute-done.44 = bf16[4,24,3840]{2,1,0:T(8,128)(2,1)S(1)} collective-permute-done((bf16[4,24,3840]{2,1,0:T(8,128)(2,1)S(1)}, bf16[4,24,3840]{2,1,0:T(8,128)(2,1)S(1)}, u32[]{:S(2)}, u32[]{:S(2)}) %collective-permute-start.44) | collective-permute-done | bytes 737312 | tf_op jit(solution)/shard_map/ppermute | solution.py:496
  427.5 4.7 %collective-permute-start.46 = (bf16[24,3840]{1,0:T(8,128)(2,1)S(1)}, bf16[24,3840]{1,0:T(8,128)(2,1)S(1)}, u32[]{:S(2)}, u32[]{:S(2)}) collective-permute-start(bf16[24,3840]{1,0:T(8,128)(2,1)S(1)} %get-tuple-element.162), channel_id=1, source_target_pairs={{16,0},{24,8},{0,16},{8,24},{17,1},{25,9},{1,17},{9,25},{18,2},{26... | collective-permute-start | bytes 552968 | tf_op jit(solution)/shard_map/ppermute | solution.py:496
  437.2 5.4 %collective-permute-done.46 = bf16[24,3840]{1,0:T(8,128)(2,1)S(1)} collective-permute-done((bf16[24,3840]{1,0:T(8,128)(2,1)S(1)}, bf16[24,3840]{1,0:T(8,128)(2,1)S(1)}, u32[]{:S(2)}, u32[]{:S(2)}) %collective-permute-start.46) | collective-permute-done | bytes 184352 | tf_op jit(solution)/shard_map/ppermute | solution.py:496
  (290 shorter events, 113.2 us)
Async XLA Ops:
  7.2 150.2 %all-gather.2.cloned.1.call-start = ((), (), s32[]{:S(2)}) async-start(), calls=%async_computation | async-start | bytes 10948608 | tf_op jit(solution)/shard_map/all_gather | solution.py:579
  22.1 16.5 %collective-permute-start.9 = (bf16[4,24,640]{2,1,0:T(8,128)(2,1)S(1)}, bf16[4,24,640]{2,1,0:T(8,128)(2,1)S(1)}, u32[]{:S(2)}, u32[]{:S(2)}) collective-permute-start(bf16[4,24,640]{2,1,0:T(8,128)(2,1)S(1)} %get-tuple-element.182), channel_id=1, source_target_pairs={{16,0},{24,8},{0,16},{8,24},{17,1},{25,9},{1,17},{9,25},{18,2},{26... | collective-permute-start | bytes 368648 | tf_op jit(solution)/shard_map/ppermute | solution.py:496
  22.1 16.5 %collective-permute-start.10 = (bf16[4,24,640]{2,1,0:T(8,128)(2,1)S(1)}, bf16[4,24,640]{2,1,0:T(8,128)(2,1)S(1)}, u32[]{:S(2)}, u32[]{:S(2)}) collective-permute-start(bf16[4,24,640]{2,1,0:T(8,128)(2,1)S(1)} %get-tuple-element.182), channel_id=1, source_target_pairs={{24,0},{0,8},{8,16},{16,24},{25,1},{1,9},{9,17},{17,25},{26,2},{2,... | collective-permute-start | bytes 368648 | tf_op jit(solution)/shard_map/ppermute | solution.py:496
  23.1 21.3 %collective-permute-start.12 = (bf16[256,768]{1,0:T(8,128)(2,1)}, bf16[256,768]{1,0:T(8,128)(2,1)S(1)}, u32[]{:S(2)}, u32[]{:S(2)}) collective-permute-start(bf16[256,768]{1,0:T(8,128)(2,1)} %bitcast.10.refs_1_.refs_5_), channel_id=1, source_target_pairs={{0,4},{4,0},{1,5},{5,1},{2,6},{6,2},{3,7},{7,3},{8,12},{12,8},{9,1... | collective-permute-start | bytes 1179656 | tf_op jit(solution)/shard_map/ppermute | solution.py:505
  38.8 14.0 %collective-permute-start.11 = (bf16[4,4,24,640]{3,2,1,0:T(8,128)(2,1)S(1)}, bf16[4,4,24,640]{3,2,1,0:T(8,128)(2,1)S(1)}, u32[]{:S(2)}, u32[]{:S(2)}) collective-permute-start(bf16[4,4,24,640]{3,2,1,0:T(8,128)(2,1)S(1)} %get-tuple-element.166), channel_id=1, source_target_pairs={{1,0},{0,1},{3,2},{2,3},{5,4},{4,5},{7,6},{6,7},{9,8},{8,9},{11,10... | collective-permute-start | bytes 1474568 | tf_op jit(solution)/shard_map/ppermute | solution.py:496
  46.3 46.5 %collective-permute-start.13 = (bf16[2,256,768]{2,1,0:T(8,128)(2,1)S(1)}, bf16[2,256,768]{2,1,0:T(8,128)(2,1)S(1)}, u32[]{:S(2)}, u32[]{:S(2)}) collective-permute-start(bf16[2,256,768]{2,1,0:T(8,128)(2,1)S(1)} %pad_maximum_fusion.3), channel_id=1, source_target_pairs={{0,2},{2,0},{1,3},{3,1},{4,6},{6,4},{5,7},{7,5},{8,10},{10,8},{9,1... | collective-permute-start | bytes 2359304 | tf_op jit(solution)/shard_map/ppermute | solution.py:503
  49.5 16.8 %collective-permute-start.1 = (bf16[256,768]{1,0:T(8,128)(2,1)}, bf16[256,768]{1,0:T(8,128)(2,1)}, u32[]{:S(2)}, u32[]{:S(2)}) collective-permute-start(bf16[256,768]{1,0:T(8,128)(2,1)} %bitcast.10.refs_1_.refs_5_), channel_id=1, source_target_pairs={{24,0},{0,8},{8,16},{16,24},{25,1},{1,9},{9,17},{17,25},{26,2},{2,... | collective-permute-start | bytes 1179656 | tf_op jit(solution)/shard_map/ppermute | solution.py:496
  52.0 25.5 %collective-permute-start.16 = (bf16[256,768]{1,0:T(8,128)(2,1)}, bf16[256,768]{1,0:T(8,128)(2,1)}, u32[]{:S(2)}, u32[]{:S(2)}) collective-permute-start(bf16[256,768]{1,0:T(8,128)(2,1)} %collective-permute-done.refs_1_.refs_5_), channel_id=1, source_target_pairs={{0,4},{4,0},{1,5},{5,1},{2,6},{6,2},{3,7},{7,3},{8,12},{12,8},{9,1... | collective-permute-start | bytes 1179656 | tf_op jit(solution)/shard_map/ppermute | solution.py:505
  66.4 13.3 %collective-permute-start.14 = (bf16[256,768]{1,0:T(8,128)(2,1)}, bf16[256,768]{1,0:T(8,128)(2,1)}, u32[]{:S(2)}, u32[]{:S(2)}) collective-permute-start(bf16[256,768]{1,0:T(8,128)(2,1)} %collective-permute-done.1.refs_1_.refs_5_), channel_id=1, source_target_pairs={{0,4},{4,0},{1,5},{5,1},{2,6},{6,2},{3,7},{7,3},{8,12},{12,8},{9,1... | collective-permute-start | bytes 1179656 | tf_op jit(solution)/shard_map/ppermute | solution.py:505
  66.5 25.7 %collective-permute-start.2 = (bf16[256,768]{1,0:T(8,128)(2,1)}, bf16[256,768]{1,0:T(8,128)(2,1)}, u32[]{:S(2)}, u32[]{:S(2)}) collective-permute-start(bf16[256,768]{1,0:T(8,128)(2,1)} %bitcast.10.refs_1_.refs_5_), channel_id=1, source_target_pairs={{16,0},{24,8},{0,16},{8,24},{17,1},{25,9},{1,17},{9,25},{18,2},{26... | collective-permute-start | bytes 1179656 | tf_op jit(solution)/shard_map/ppermute | solution.py:496
  79.7 31.9 %collective-permute-start.17 = (bf16[2,256,768]{2,1,0:T(8,128)(2,1)}, bf16[2,256,768]{2,1,0:T(8,128)(2,1)}, u32[]{:S(2)}, u32[]{:S(2)}) collective-permute-start(bf16[2,256,768]{2,1,0:T(8,128)(2,1)} %pad_maximum_fusion.5), channel_id=1, source_target_pairs={{0,2},{2,0},{1,3},{3,1},{4,6},{6,4},{5,7},{7,5},{8,10},{10,8},{9,1... | collective-permute-start | bytes 2359304 | tf_op jit(solution)/shard_map/ppermute | solution.py:503
  81.8 42.3 %collective-permute-start.15 = (bf16[2,256,768]{2,1,0:T(8,128)(2,1)}, bf16[2,256,768]{2,1,0:T(8,128)(2,1)}, u32[]{:S(2)}, u32[]{:S(2)}) collective-permute-start(bf16[2,256,768]{2,1,0:T(8,128)(2,1)} %pad_maximum_fusion.4), channel_id=1, source_target_pairs={{0,2},{2,0},{1,3},{3,1},{4,6},{6,4},{5,7},{7,5},{8,10},{10,8},{9,1... | collective-permute-start | bytes 2359304 | tf_op jit(solution)/shard_map/ppermute | solution.py:503
  92.2 18.1 %collective-permute-start.3 = (bf16[256,768]{1,0:T(8,128)(2,1)}, bf16[256,768]{1,0:T(8,128)(2,1)S(1)}, u32[]{:S(2)}, u32[]{:S(2)}) collective-permute-start(bf16[256,768]{1,0:T(8,128)(2,1)} %collective-permute-done.2.refs_1_.refs_5_), channel_id=1, source_target_pairs={{0,4},{4,0},{1,5},{5,1},{2,6},{6,2},{3,7},{7,3},{8,12},{12,8},{9,1... | collective-permute-start | bytes 1179656 | tf_op jit(solution)/shard_map/ppermute | solution.py:505
  111.5 24.9 %collective-permute-start.4 = (bf16[2,256,768]{2,1,0:T(8,128)(2,1)S(1)}, bf16[2,256,768]{2,1,0:T(8,128)(2,1)S(1)}, u32[]{:S(2)}, u32[]{:S(2)}) collective-permute-start(bf16[2,256,768]{2,1,0:T(8,128)(2,1)S(1)} %pad_maximum_fusion.2), channel_id=1, source_target_pairs={{0,2},{2,0},{1,3},{3,1},{4,6},{6,4},{5,7},{7,5},{8,10},{10,8},{9,1... | collective-permute-start | bytes 2359304 | tf_op jit(solution)/shard_map/ppermute | solution.py:503
  253.9 14.0 %collective-permute-start.35 = (bf16[4,4,24,640]{3,2,1,0:T(8,128)(2,1)S(1)}, bf16[4,4,24,640]{3,2,1,0:T(8,128)(2,1)S(1)}, u32[]{:S(2)}, u32[]{:S(2)}) collective-permute-start(bf16[4,4,24,640]{3,2,1,0:T(8,128)(2,1)S(1)} %dynamic-slice_bitcast_fusion), channel_id=1, source_target_pairs={{1,0},{0,1},{3,2},{2,3},{5,4},{4,5},{7,6},{6,7},{9,8},{8,9},{11,10... | collective-permute-start | bytes 1474568 | tf_op jit(solution)/shard_map/ppermute | solution.py:496
  271.9 13.5 %collective-permute-start.24 = (bf16[2,256,768]{2,1,0:T(8,128)(2,1)}, bf16[2,256,768]{2,1,0:T(8,128)(2,1)S(1)}, u32[]{:S(2)}, u32[]{:S(2)}) collective-permute-start(bf16[2,256,768]{2,1,0:T(8,128)(2,1)} %get-tuple-element.95), channel_id=1, source_target_pairs={{0,2},{2,0},{1,3},{3,1},{4,6},{6,4},{5,7},{7,5},{8,10},{10,8},{9,1... | collective-permute-start | bytes 2359304 | tf_op jit(solution)/shard_map/ppermute | solution.py:503
  282.5 64.2 %collective-permute-start.48 = (bf16[2,4,48,3072]{3,2,1,0:T(8,128)(2,1)}, bf16[2,4,48,3072]{3,2,1,0:T(8,128)(2,1)}, u32[]{:S(2)}, u32[]{:S(2)}) collective-permute-start(bf16[2,4,48,3072]{3,2,1,0:T(8,128)(2,1)} %get-tuple-element.124), channel_id=1, source_target_pairs={{0,2},{2,0},{1,3},{3,1},{4,6},{6,4},{5,7},{7,5},{8,10},{10,8},{9,1... | collective-permute-start | bytes 7077896 | tf_op jit(solution)/shard_map/ppermute | solution.py:503
  282.8 67.0 %collective-permute-start.42 = (bf16[2,4,48,3840]{3,2,1,0:T(8,128)(2,1)}, bf16[2,4,48,3840]{3,2,1,0:T(8,128)(2,1)}, u32[]{:S(2)}, u32[]{:S(2)}) collective-permute-start(bf16[2,4,48,3840]{3,2,1,0:T(8,128)(2,1)} %get-tuple-element.122), channel_id=1, source_target_pairs={{0,2},{2,0},{1,3},{3,1},{4,6},{6,4},{5,7},{7,5},{8,10},{10,8},{9,1... | collective-permute-start | bytes 8847368 | tf_op jit(solution)/shard_map/ppermute | solution.py:503
  291.7 18.1 %collective-permute-start.28 = (bf16[256,768]{1,0:T(8,128)(2,1)S(1)}, bf16[256,768]{1,0:T(8,128)(2,1)S(1)}, u32[]{:S(2)}, u32[]{:S(2)}) collective-permute-start(bf16[256,768]{1,0:T(8,128)(2,1)S(1)} %fusion.26), channel_id=1, source_target_pairs={{0,4},{4,0},{1,5},{5,1},{2,6},{6,2},{3,7},{7,3},{8,12},{12,8},{9,1... | collective-permute-start | bytes 1179656 | tf_op jit(solution)/shard_map/ppermute | solution.py:505
  294.0 24.3 %collective-permute-start.31 = (bf16[256,768]{1,0:T(8,128)(2,1)S(1)}, bf16[256,768]{1,0:T(8,128)(2,1)S(1)}, u32[]{:S(2)}, u32[]{:S(2)}) collective-permute-start(bf16[256,768]{1,0:T(8,128)(2,1)S(1)} %fusion.27), channel_id=1, source_target_pairs={{0,4},{4,0},{1,5},{5,1},{2,6},{6,2},{3,7},{7,3},{8,12},{12,8},{9,1... | collective-permute-start | bytes 1179656 | tf_op jit(solution)/shard_map/ppermute | solution.py:505
  301.4 24.7 %collective-permute-start.34 = (bf16[256,768]{1,0:T(8,128)(2,1)S(1)}, bf16[256,768]{1,0:T(8,128)(2,1)S(1)}, u32[]{:S(2)}, u32[]{:S(2)}) collective-permute-start(bf16[256,768]{1,0:T(8,128)(2,1)S(1)} %fusion.29), channel_id=1, source_target_pairs={{0,4},{4,0},{1,5},{5,1},{2,6},{6,2},{3,7},{7,3},{8,12},{12,8},{9,1... | collective-permute-start | bytes 1179656 | tf_op jit(solution)/shard_map/ppermute | solution.py:505
  309.8 30.0 %collective-permute-start.26 = (bf16[256,768]{1,0:T(8,128)(2,1)}, bf16[256,768]{1,0:T(8,128)(2,1)}, u32[]{:S(2)}, u32[]{:S(2)}) collective-permute-start(bf16[256,768]{1,0:T(8,128)(2,1)} %fusion.16), channel_id=1, source_target_pairs={{16,0},{24,8},{0,16},{8,24},{17,1},{25,9},{1,17},{9,25},{18,2},{26... | collective-permute-start | bytes 1179656 | tf_op jit(solution)/shard_map/ppermute | solution.py:496
  318.3 26.0 %collective-permute-start.29 = (bf16[256,768]{1,0:T(8,128)(2,1)}, bf16[256,768]{1,0:T(8,128)(2,1)}, u32[]{:S(2)}, u32[]{:S(2)}) collective-permute-start(bf16[256,768]{1,0:T(8,128)(2,1)} %fusion.14), channel_id=1, source_target_pairs={{8,0},{16,8},{24,16},{0,24},{9,1},{17,9},{25,17},{1,25},{10,2},{18... | collective-permute-start | bytes 1179656 | tf_op jit(solution)/shard_map/ppermute | solution.py:496
  326.1 18.1 %collective-permute-start.32 = (bf16[256,768]{1,0:T(8,128)(2,1)}, bf16[256,768]{1,0:T(8,128)(2,1)}, u32[]{:S(2)}, u32[]{:S(2)}) collective-permute-start(bf16[256,768]{1,0:T(8,128)(2,1)} %fusion.12), channel_id=1, source_target_pairs={{24,0},{0,8},{8,16},{16,24},{25,1},{1,9},{9,17},{17,25},{26,2},{2,... | collective-permute-start | bytes 1179656 | tf_op jit(solution)/shard_map/ppermute | solution.py:496
  349.6 29.0 %collective-permute-start.49 = (bf16[2,4,24,3072]{3,2,1,0:T(8,128)(2,1)S(1)}, bf16[2,4,24,3072]{3,2,1,0:T(8,128)(2,1)S(1)}, u32[]{:S(2)}, u32[]{:S(2)}) collective-permute-start(bf16[2,4,24,3072]{3,2,1,0:T(8,128)(2,1)S(1)} %fusion.2), channel_id=1, source_target_pairs={{1,0},{0,1},{3,2},{2,3},{5,4},{4,5},{7,6},{6,7},{9,8},{8,9},{11,10... | collective-permute-start | bytes 3538952 | tf_op jit(solution)/shard_map/ppermute | solution.py:496
  352.5 55.7 %collective-permute-start.43 = (bf16[2,4,24,3840]{3,2,1,0:T(8,128)(2,1)S(1)}, bf16[2,4,24,3840]{3,2,1,0:T(8,128)(2,1)S(1)}, u32[]{:S(2)}, u32[]{:S(2)}) collective-permute-start(bf16[2,4,24,3840]{3,2,1,0:T(8,128)(2,1)S(1)} %fusion), channel_id=1, source_target_pairs={{1,0},{0,1},{3,2},{2,3},{5,4},{4,5},{7,6},{6,7},{9,8},{8,9},{11,10... | collective-permute-start | bytes 4423688 | tf_op jit(solution)/shard_map/ppermute | solution.py:496
  378.9 30.5 %collective-permute-start.50 = (bf16[4,24,3072]{2,1,0:T(8,128)(2,1)S(1)}, bf16[4,24,3072]{2,1,0:T(8,128)(2,1)S(1)}, u32[]{:S(2)}, u32[]{:S(2)}) collective-permute-start(bf16[4,24,3072]{2,1,0:T(8,128)(2,1)S(1)} %fusion.18), channel_id=1, source_target_pairs={{4,0},{0,4},{5,1},{1,5},{6,2},{2,6},{7,3},{3,7},{12,8},{8,12},{13,... | collective-permute-start | bytes 1769480 | tf_op jit(solution)/shard_map/ppermute | solution.py:496
  408.5 16.6 %collective-permute-start.44 = (bf16[4,24,3840]{2,1,0:T(8,128)(2,1)S(1)}, bf16[4,24,3840]{2,1,0:T(8,128)(2,1)S(1)}, u32[]{:S(2)}, u32[]{:S(2)}) collective-permute-start(bf16[4,24,3840]{2,1,0:T(8,128)(2,1)S(1)} %fusion.17), channel_id=1, source_target_pairs={{4,0},{0,4},{5,1},{1,5},{6,2},{2,6},{7,3},{3,7},{12,8},{8,12},{13,... | collective-permute-start | bytes 2211848 | tf_op jit(solution)/shard_map/ppermute | solution.py:496
  409.6 22.5 %collective-permute-start.51 = (bf16[24,3072]{1,0:T(8,128)(2,1)S(1)}, bf16[24,3072]{1,0:T(8,128)(2,1)S(1)}, u32[]{:S(2)}, u32[]{:S(2)}) collective-permute-start(bf16[24,3072]{1,0:T(8,128)(2,1)S(1)} %get-tuple-element.163), channel_id=1, source_target_pairs={{24,0},{0,8},{8,16},{16,24},{25,1},{1,9},{9,17},{17,25},{26,2},{2,... | collective-permute-start | bytes 442376 | tf_op jit(solution)/shard_map/ppermute | solution.py:496
  412.0 21.6 %collective-permute-start.52 = (bf16[24,3072]{1,0:T(8,128)(2,1)S(1)}, bf16[24,3072]{1,0:T(8,128)(2,1)S(1)}, u32[]{:S(2)}, u32[]{:S(2)}) collective-permute-start(bf16[24,3072]{1,0:T(8,128)(2,1)S(1)} %get-tuple-element.165), channel_id=1, source_target_pairs={{16,0},{24,8},{0,16},{8,24},{17,1},{25,9},{1,17},{9,25},{18,2},{26... | collective-permute-start | bytes 442376 | tf_op jit(solution)/shard_map/ppermute | solution.py:496
  415.4 18.3 %collective-permute-start.53 = (bf16[24,3072]{1,0:T(8,128)(2,1)S(1)}, bf16[24,3072]{1,0:T(8,128)(2,1)S(1)}, u32[]{:S(2)}, u32[]{:S(2)}) collective-permute-start(bf16[24,3072]{1,0:T(8,128)(2,1)S(1)} %get-tuple-element.164), channel_id=1, source_target_pairs={{8,0},{16,8},{24,16},{0,24},{9,1},{17,9},{25,17},{1,25},{10,2},{18... | collective-permute-start | bytes 442376 | tf_op jit(solution)/shard_map/ppermute | solution.py:496
  427.5 15.1 %collective-permute-start.46 = (bf16[24,3840]{1,0:T(8,128)(2,1)S(1)}, bf16[24,3840]{1,0:T(8,128)(2,1)S(1)}, u32[]{:S(2)}, u32[]{:S(2)}) collective-permute-start(bf16[24,3840]{1,0:T(8,128)(2,1)S(1)} %get-tuple-element.162), channel_id=1, source_target_pairs={{16,0},{24,8},{0,16},{8,24},{17,1},{25,9},{1,17},{9,25},{18,2},{26... | collective-permute-start | bytes 552968 | tf_op jit(solution)/shard_map/ppermute | solution.py:496
  (54 other events, 286.7 us)
Sparse Core Ops, SparseCore 0:
  11.5 121.1 all-gather.1

commit v3 on v2

--- a/solution.py
+++ b/solution.py
@@ -349,7 +349,7 @@
     out_ref, resid_ref = [refs.pop(0) for _ in range(2)]
     da_refs = [refs.pop(0) for _ in range(4)]
     vec_out = refs.pop(0)
-    targets = [refs.pop(0) for _ in range(4 if aligned else 2)]
+    targets = [refs.pop(0) for _ in range(6 if aligned else 1)]
     wo, w1, w2, go, g1, g2, act, slope, in_sem, out_sem = refs
     group, zi, xi, ci, bi, start, length = [where_ref[i] for i in range(7)]
     rows, width = x_ref.shape
@@ -427,27 +427,30 @@
         go[group_rows(r), :] = lax.dot_general(
             att_refs[r][...], branch_low, CONTRACT_FIRST, preferred_element_type=f32
         ).astype(bf16)
-    block = n_b * own_rows
-    for dc in range(2 if aligned else 1):
-        to_one, to_two = targets[2 * dc : 2 * dc + 2]
-        if not aligned:
-            for k, src in enumerate([go] + [g1.at[k] for k in range(fold)]):
-                pltpu.make_async_copy(src, to_one.at[:, lanes(k)], out_sem.at[0]).start()
-            for k in range(fold):
-                pltpu.make_async_copy(g2.at[k], to_two.at[:, lanes(k)], out_sem.at[1]).start()
-            continue
-        for dx in range(2):
-            for jz in range(n_q):
-                m = (lax.rem(zi + jz, n_q) * 2 + (xi ^ dx)) * 2 + (ci ^ dc)
-                at = pl.ds(pl.multiple_of(m * block, 16), block)
-                for k, src in enumerate([go] + [g1.at[k] for k in range(fold)]):
-                    dst = to_one.at[dx, jz, :, lanes(k)]
-                    pltpu.make_async_copy(src.at[at], dst, out_sem.at[2 * dc]).start()
-                for k in range(fold):
-                    dst = to_two.at[dx, jz, :, lanes(k)]
-                    pltpu.make_async_copy(g2.at[k, at], dst, out_sem.at[2 * dc + 1]).start()
+    units = [g2.at[k] for k in range(fold)] + [g1.at[k] for k in range(fold)] + [go]
+    if aligned:
+        block = n_b * own_rows
+        for i, part in enumerate(unit_parts(fold)):
+            for dc in range(2):
+                target, sem = targets[2 * i + dc], out_sem.at[2 * i + dc]
+                for dx in range(2):
+                    for jz in range(n_q):
+                        m = (lax.rem(zi + jz, n_q) * 2 + (xi ^ dx)) * 2 + (ci ^ dc)
+                        at = pl.ds(pl.multiple_of(m * block, 16), block)
+                        for place, unit in enumerate(part):
+                            dst = target.at[dx, jz, :, lanes(place)]
+                            pltpu.make_async_copy(units[unit].at[at], dst, sem).start()
+    else:
+        for i, unit in enumerate(units):
+            pltpu.make_async_copy(unit, targets[0].at[:, lanes(i)], out_sem.at[0]).start()
     for i, dst in enumerate(targets):
         pltpu.make_async_copy(dst, dst, out_sem.at[i]).wait()
+
+
+def unit_parts(fold):
+    count = 1 + 2 * fold
+    edges = [count * i // 3 for i in range(4)]
+    return [range(edges[i], edges[i + 1]) for i in range(3)]
 
 
 def ffn_block(layout, where, att, x, cot, vectors, ebias, packed):
@@ -463,9 +466,12 @@
         *[jax.ShapeDtypeStruct((rows, OWN_WIDTH), bf16)] * 4,
         jax.ShapeDtypeStruct((16, width), f32),
     ]
-    lead = (2, n_q, n_b * own_rows) if aligned else (width,)
-    pair = [jax.ShapeDtypeStruct((*lead, width + ff), bf16), jax.ShapeDtypeStruct((*lead, ff), bf16)]
-    targets = pair + pair if aligned else pair
+    if aligned:
+        lead = (2, n_q, n_b * own_rows)
+        sizes = [len(part) * width for part in unit_parts(fold)]
+        targets = [jax.ShapeDtypeStruct((*lead, size), bf16) for size in sizes for _ in range(2)]
+    else:
+        targets = [jax.ShapeDtypeStruct((width, width + 2 * ff), bf16)]
     weight_scratch = [
         pltpu.VMEM((width, width), bf16),
         pltpu.VMEM((fold, width, width), bf16),
@@ -482,7 +488,7 @@
             pltpu.VMEM((fold, rows, width), bf16),
             pltpu.VMEM((fold, rows, width), f32),
             pltpu.SemaphoreType.DMA((1 + 2 * fold,)),
-            pltpu.SemaphoreType.DMA((4,)),
+            pltpu.SemaphoreType.DMA((6,)),
         ],
         compiler_params=pltpu.CompilerParams(vmem_limit_bytes=VMEM_BYTES),
         cost_estimate=pl.CostEstimate(
@@ -490,6 +496,31 @@
         ),
         name="feed_forward",
     )(*operands)
+
+
+def order_kernel(n_q, n_b, where_ref, blocks_ref, out_ref):
+    group, zi, bi = [where_ref[i] for i in range(3)]
+    rows = blocks_ref.shape[3]
+    for m in range(4 * n_q):
+        q, g = m // 4, m % 4
+        far, r = lax.rem(q + n_q - zi, n_q), g ^ group
+        both = [
+            blocks_ref[lax.rem(b + n_b - bi, n_b), far, r].astype(f32) for b in range(n_b)
+        ]
+        at = slice(m * n_b * rows, (m + 1) * n_b * rows)
+        out_ref[at, :] = jnp.concatenate(both, axis=0).astype(bf16)
+
+
+def order_rows(n_q, n_b, where, blocks):
+    rows, lanes = blocks.shape[3:]
+    return pl.pallas_call(
+        partial(order_kernel, n_q, n_b),
+        out_shape=jax.ShapeDtypeStruct((4 * n_q * n_b * rows, lanes), bf16),
+        in_specs=[pl.BlockSpec(memory_space=pltpu.SMEM)] + vmem_specs(1),
+        out_specs=vmem_specs(1)[0],
+        compiler_params=pltpu.CompilerParams(vmem_limit_bytes=VMEM_BYTES),
+        name="order_rows",
+    )(where, blocks)
 
 
 def from_shift(value, axis, count, step):
@@ -510,23 +541,66 @@
     return lax.dynamic_index_in_dim(stacked, index, dim, keepdims=False)
 
 
-def after(value, *others):
-    return lax.optimization_barrier((value, *others))[0]
-
-
-def sum_to_owner(keep, send, n_q, n_b, bi):
-    total = keep.astype(f32) + square_swap(send, 1).astype(f32)
-    total = total.reshape(2, n_q, n_b, -1, keep.shape[-1])
-    own = pick(total, bi, 2)
-    for j in range(1, n_b):
-        away = pick(total, (bi + j) % n_b, 2).astype(bf16)
-        own = own + from_shift(away, "b", n_b, n_b - j).astype(f32)
-    for axis, count in (("x", 2), ("q", n_q)):
-        total = own
-        own = total[0]
-        for j in range(1, count):
-            own = own + from_shift(total[j].astype(bf16), axis, count, count - j).astype(f32)
-    return own
+class Chain:
+    def __init__(self, state, *steps):
+        self.state, self.steps = tuple(state), list(steps)
+
+
+def run_stage(chains, outs=()):
+    for chain in chains:
+        chain.state = tuple(chain.steps.pop(0)(*chain.state))
+    outs, states = lax.optimization_barrier((tuple(outs), [c.state for c in chains]))
+    for chain, state in zip(chains, states):
+        chain.state = tuple(state)
+    return outs
+
+
+def away_sum(total, axis, count):
+    parts = [total[j].astype(bf16) for j in range(1, count)]
+    return [from_shift(part, axis, count, count - j - 1) for j, part in enumerate(parts)]
+
+
+def weight_sum(keep, send, n_q, n_b, bi):
+    def own_b(keep, got, j):
+        shape = (2, n_q, n_b, -1, keep.shape[-1])
+        both = [pick(v.reshape(shape), (bi + j) % n_b, 2).astype(f32) for v in (keep, got)]
+        return both[0] + both[1]
+
+    def over_core(keep, send):
+        return keep, square_swap(send, 1)
+
+    def over_b(keep, got):
+        away = [own_b(keep, got, j).astype(bf16) for j in range(1, n_b)]
+        return keep, got, *[from_shift(v, "b", n_b, n_b - 1 - j) for j, v in enumerate(away)]
+
+    def over_x(keep, got, *more):
+        total = own_b(keep, got, 0) + sum(v.astype(f32) for v in more)
+        return total[0], *away_sum(total, "x", 2)
+
+    def over_q(own, *more):
+        total = own + sum(v.astype(f32) for v in more)
+        return total[0], *away_sum(total, "q", n_q)
+
+    return Chain((keep, send), over_core, over_b, over_x, over_q)
+
+
+def token_sum(keep, send, n_q, j):
+    def over_core(keep, send):
+        return keep, square_swap(send, 1)
+
+    def over_x(keep, got):
+        total = keep.astype(f32) + got.astype(f32)
+        return total[0], square_swap(total[1].astype(bf16), 2)
+
+    def over_q(own, got):
+        total = own + got.astype(f32)
+        return (from_shift(total.astype(bf16), "q", n_q, n_q - j),)
+
+    return Chain((keep, send), over_core, over_x, *([over_q] if j else []))
+
+
+def chain_sum(chain):
+    return sum(v.astype(f32) for v in chain.state)
 
 
 def deinterleave(fold):
@@ -590,13 +664,52 @@
         mine = [pick(thirds[:, t], g, 1) for t in range(3)]
         return jnp.concatenate(mine + [vectors], axis=1)
 
-    square = jnp.stack([square_swap(columns_of(group ^ r), r) for r in range(4)])
-    rows_q = jnp.stack([square] + [from_shift(square, "q", n_q, j) for j in range(1, n_q)])
-    rows_b = jnp.stack([rows_q] + [from_shift(rows_q, "b", n_b, j) for j in range(1, n_b)])
-    ordered = jnp.stack([pick(rows_b, (i - bi) % n_b) for i in range(n_b)], axis=3)
-    ordered = jnp.stack([pick(ordered, group ^ g, 1) for g in range(4)], axis=1)
-    ordered = jnp.stack([pick(ordered, (i - zi) % n_q) for i in range(n_q)])
-    w_own = ordered.transpose(0, 1, 3, 2, 4).reshape(width, WIDE)
+    def rows_square(*blocks):
+        return [square_swap(block, r) for r, block in enumerate(blocks)]
+
+    def rows_q(*blocks):
+        square = jnp.stack(blocks)
+        return [square] + [from_shift(square, "q", n_q, j) for j in range(1, n_q)]
+
+    def rows_b(*blocks):
+        both = jnp.stack(blocks)
+        return [both] + [from_shift(both, "b", n_b, j) for j in range(1, n_b)]
+
+    weight_rows = Chain([columns_of(group ^ r) for r in range(4)], rows_square, rows_q, rows_b)
+
+    def token_chunk(j):
+        def over_q(own):
+            return (from_shift(own, "q", n_q, j),)
+
+        def over_x(own):
+            return own, square_swap(own, 2)
+
+        def over_core(own, other):
+            halves = square_swap(jnp.stack([own, other]), 1)
+            return own, halves[0], other, halves[1]
+
+        return Chain((x_own,), *([over_q] if j else []), over_x, over_core)
+
+    arrival = []
+    for j in [k for pair in zip(range(1, n_q), range(n_q - 1, 0, -1)) for k in pair]:
+        arrival += [] if j in arrival else [j]
+    arrival = [0] + arrival
+    chunks = {j: token_chunk(j) for j in arrival}
+    line = [chunks[j] for j in arrival]
+    for step in range(3):
+        ready = [c for i, c in enumerate(line) if i <= step + 1 and c.steps and (i or step < 2)]
+        run_stage([weight_rows] + ready)
+    chunk_x = {}
+
+    by_distance = jnp.stack(weight_rows.state)
+    if aligned:
+        spot = jnp.stack([group, zi, bi]).astype(jnp.int32)
+        w_own = order_rows(n_q, n_b, spot, by_distance)
+    else:
+        ordered = jnp.stack([pick(by_distance, (i - bi) % n_b) for i in range(n_b)], axis=3)
+        ordered = jnp.stack([pick(ordered, group ^ g, 1) for g in range(4)], axis=1)
+        ordered = jnp.stack([pick(ordered, (i - zi) % n_q) for i in range(n_q)])
+        w_own = ordered.transpose(0, 1, 3, 2, 4).reshape(width, WIDE)
     turned = w_own[:, VECTORS : VECTORS + n_vec].astype(f32)
     turned = turned.T
     ebias = turned[8:]
@@ -607,19 +720,6 @@
         [own_bias[:1], zero, own_bias[1:2], jnp.zeros((1, WIDE - VECTORS), f32)], axis=1
     )
 
-    chunk_x = {}
-    tie = []
-    for j in [0] + [k for pair in zip(range(1, n_q), range(n_q - 1, 0, -1)) for k in pair]:
-        if j in chunk_x:
-            continue
-        own = x_own if j == 0 else from_shift(after(x_own, *tie), "q", n_q, j)
-        tie = [] if j == 0 else [own]
-        chunk_x[j] = [own, None, square_swap(own, 2), None]
-    for j, piece in chunk_x.items():
-        halves = square_swap(jnp.stack([piece[0], piece[2]]), 1)
-        piece[1], piece[3] = halves[0], halves[1]
-    arrival = list(chunk_x)
-
     def where_of(j):
         zj = (zi + j) % n_q
         spots = [(zj * 4 + (group ^ r)) * seq_rows for r in range(4)]
@@ -630,7 +730,11 @@
     carry = None
     for step, j in enumerate(arrival):
         first, last = step == 0, step == n_q - 1
+        while chunks[j].steps:
+            run_stage([c for c in line[step:] if c.steps])
+        chunk_x[j] = chunks[j].state
         outs = attend_chunk(first, last, where_of(j), chunk_x[j], weights, carry)
+        outs = run_stage([c for c in line[step + 1 :] if c.steps], outs)
         kept[j] = (outs[0], outs[1])
         outs = outs[2:]
         if first:
@@ -646,36 +750,32 @@
     outs = ffn_block(layout, where, att, x_own, cotangent[0], turned, ebias, gathered_ffn)
     output, resid_first_grad = outs[:2]
     att_grads, vec_grads, summands = outs[2:6], outs[6], outs[7:]
-    grads = [square_swap(att_grads[r], r) for r in range(4)]
-
+    square = Chain(att_grads, lambda *parts: [square_swap(v, r) for r, v in enumerate(parts)])
+
+    sums = []
     if aligned:
-        one_keep, two_keep, one_send, two_send = summands
-        summed_two = sum_to_owner(two_keep, two_send, n_q, n_b, bi)
-        summed_one = sum_to_owner(one_keep, one_send, n_q, n_b, bi)
-    else:
-        summed = lax.psum_scatter(
-            jnp.concatenate(summands, axis=1), AXES, scatter_dimension=0, tiled=True
-        ).astype(f32)
-        summed_one, summed_two = summed[:, : width + ff], summed[:, width + ff :]
-
-    shared = (qx2, qp, w_own, grads, attx)
+        for i in range(3):
+            sums.append(weight_sum(summands[2 * i], summands[2 * i + 1], n_q, n_b, bi))
+    else:
+        summed = lax.psum_scatter(summands[0], AXES, scatter_dimension=0, tiled=True).astype(f32)
+    run_stage([square] + sums[:1])
+    shared = (qx2, qp, w_own, square.state, attx)
     carry = None
-    token_grad = resid_first_grad
+    moving = []
     for step, j in enumerate(reversed(arrival)):
         first, last = step == 0, step == n_q - 1
         outs = attend_back_chunk(first, last, kept[j], chunk_x[j], shared, carry)
+        begun = [c for c in sums[: step + 2] if c.steps]
+        outs = run_stage(begun + [c for c in moving if c.steps], outs)
         keep, send = outs[:2]
+        moving.append(token_sum(keep, send, n_q, j))
         outs = outs[2:]
         if first:
             dox = outs[0]
             outs = outs[1:]
         carry = (dox, *outs)
-        dx = keep.astype(f32) + square_swap(send, 1).astype(f32)
-        dx = dx[0] + square_swap(dx[1].astype(bf16), 2).astype(f32)
-        if j:
-            dx = from_shift(dx.astype(bf16), "q", n_q, n_q - j).astype(f32)
-        token_grad = token_grad + dx
-    input_grad = token_grad.astype(bf16)
+        if not last:
+            carry = run_stage(moving[-1:], carry)
     grad_joint, col = carry[1:]
 
     own_bias = jnp.stack([col[0, :OWN_WIDTH], col[0, 2 * OWN_WIDTH : 3 * OWN_WIDTH]])
@@ -688,22 +788,36 @@
     room = jnp.zeros((width, WIDE - VECTORS - 2 * n_vec), bf16)
     blocks = jnp.concatenate([grad_joint[:, :VECTORS], tall_high, tall_low, room], axis=1)
     total = blocks.reshape(n_q, 4, n_b, own_rows, WIDE)
-    total = jnp.stack([pick(total, (bi + j) % n_b, 2) for j in range(n_b)])
-    for axis, count, index in (("b", n_b, bi), ("q", n_q, zi)):
-        if axis == "q":
-            total = jnp.stack([pick(total, (zi + j) % n_q) for j in range(n_q)])
-        own = total[0].astype(f32)
-        for j in range(1, count):
-            own = own + from_shift(total[j].astype(bf16), axis, count, count - j).astype(f32)
-        total = own
-    total = total.astype(bf16)
-    parts = jnp.stack([square_swap(pick(total, group ^ r), r) for r in range(4)])
+
+    def rows_over_b(total):
+        parts = [pick(total, (bi + j) % n_b, 2) for j in range(n_b)]
+        return parts[0], *away_sum(parts, "b", n_b)
+
+    def rows_over_q(*parts):
+        total = sum(v.astype(f32) for v in parts)
+        parts = [pick(total, (zi + j) % n_q) for j in range(n_q)]
+        return parts[0], *away_sum(parts, "q", n_q)
+
+    def rows_over_square(*parts):
+        total = sum(v.astype(f32) for v in parts).astype(bf16)
+        return [square_swap(pick(total, group ^ r), r) for r in range(4)]
+
+    rows = Chain((total,), rows_over_b, rows_over_q, rows_over_square)
+    while any(c.steps for c in [rows, *sums, *moving]):
+        run_stage([c for c in [rows, *sums, *moving] if c.steps])
+    token_grad = resid_first_grad
+    for chain in moving:
+        token_grad = token_grad + chain_sum(chain)
+    input_grad = token_grad.astype(bf16)
+    if aligned:
+        summed = jnp.concatenate([chain_sum(c) for c in sums], axis=1)
+    parts = jnp.stack(rows.state)
     parts = jnp.stack([pick(parts, group ^ g) for g in range(4)])
     grad_triple = parts[:, :, :VECTORS].reshape(GROUPS, own_rows, 3, OWN_WIDTH)
     grad_triple = grad_triple.transpose(1, 2, 0, 3).reshape(own_rows, -1).astype(f32)
     small = jnp.sum(parts[:, :, VECTORS : VECTORS + 2 * n_vec].astype(f32), axis=0)
     small = small[:, :n_vec] + small[:, n_vec:]
-    grad_expand = summed_one[:, width:].reshape(own_rows, fold, -1, LANES).transpose(0, 2, 1, 3)
+    grad_expand = summed[:, ff : 2 * ff].reshape(own_rows, fold, -1, LANES).transpose(0, 2, 1, 3)
     grad_expand = jnp.einsum(
         "rbs,ts->rbt",
         grad_expand.reshape(own_rows, -1, fold * LANES),
@@ -717,13 +831,13 @@
         grad_triple,
         small[:, 0],
         small[:, 1],
-        summed_one[:, :width],
+        summed[:, 2 * ff :],
         small[:, 2],
         small[:, 3],
         small[:, 4],
         grad_expand,
         small[:, 8:].reshape(-1),
-        summed_two.reshape(-1, width),
+        summed[:, :ff].reshape(-1, width),
         small[:, 5],
         small[:, 6],
         small[:, 7],

time: 457 us -> 383 us (0.84)
  waiting for transfers between devices: 195 us -> 106 us
  other arithmetic: 22.6 us -> 35.2 us
    ppermute x24 -> x29, waiting for transfers between devices: 145 us -> 86.5 us  [from_shift(): lax.ppermute(value, axis, [((i + step) % count, i) for i in range(count)])]
    ppermute x12, waiting for transfers between devices: 40.5 us -> 16.2 us  [square_swap(): return lax.ppermute(value, 'x', [(0, 1), (1, 0)])]
    convert_element_type x4 -> x7, other arithmetic: 2.62 us -> 11.8 us  [the longest x3 7.07 us: over_b(): away = [own_b(keep, got, j).astype(bf16) for j in range(1, n_b)]]
    ppermute x14 -> x15, waiting for transfers between devices: 6.04 us -> 0.04 us  [square_swap(): return lax.ppermute(value, 'c', [(0, 1), (1, 0)])]
    ppermute x24 -> x29, starting transfers between devices: 49 us -> 43.2 us  [from_shift(): lax.ppermute(value, axis, [((i + step) % count, i) for i in range(count)])]
  transfers between devices with their start and end apart: 55 -> 61, of which waited for: 31 -> 23; matrix products, arithmetic and copies ran while one was open for 9% -> 13% of each run, Pallas kernels for 9% -> 29%
where the time goes in v3:
time: 383 us; the launch traced here: 379 us
  Pallas kernels  130 us (34%)
  waiting for transfers between devices  106 us (28%)
  starting transfers between devices  61.4 us (16%)
  other arithmetic  35.2 us (9%)
  local copies, waits for them, and re-layouts  28.7 us (7%)
  between operations  16.6 us (4%)
    ppermute x29, waiting for transfers between devices, from_shift(): lax.ppermute(value, axis, [((i + step) % count, i) for i in range(count)])  86.5 us
    pallas_call x4, Pallas kernels, attend_back_chunk(): pl.pallas_call(partial(backward_kernel, first, last, min(512, rows), min(...  64.5 us
    pallas_call x4, Pallas kernels, attend_chunk(): pl.pallas_call(partial(forward_kernel, first, last, min(512, rows), min(1...  43.3 us
    ppermute x29, starting transfers between devices, from_shift(): lax.ppermute(value, axis, [((i + step) % count, i) for i in range(count)])  43.2 us
    pallas_call x1, Pallas kernels, ffn_block(): pl.pallas_call(partial(ffn_kernel, layout), out_shape=out_shape + targets...  20.3 us
    ppermute x12, waiting for transfers between devices, square_swap(): return lax.ppermute(value, 'x', [(0, 1), (1, 0)])  16.2 us
    ppermute x12, starting transfers between devices, square_swap(): return lax.ppermute(value, 'x', [(0, 1), (1, 0)])  11.2 us
  transfers between devices with their start and end apart: 61, of which 23 were waited for; matrix products, arithmetic and copies ran while one was open for 13% of the time, Pallas kernels for 29%

profile of v3, /device:TPU:0, one launch (start us, length us, event | category | flops | bytes accessed | tf_op | source)
XLA Modules:
  0.0 379.3 jit_solution(227216463973904646)
XLA Ops:
  10.1 3.0 collective-permute-start.3
  13.1 3.6 collective-permute-start.4
  20.7 2.4 collective-permute-done.1
  23.3 3.8 %collective-permute-done.4.refs_1_.refs_5_ = bf16[256,768]{1,0:T(8,128)(2,1)S(1)} collective-permute-done((bf16[256,768]{1,0:T(8,128)(2,1)S(1)}, bf16[256,768]{1,0:T(8,128)(2,1)S(1)}, u32[]{:S(2)}, u32[]{:S(2)}) %collective-permute-start.4) | collective-permute-done | bytes 393248 | tf_op jit(solution)/shard_map/ppermute | solution.py:527
  27.4 4.3 %collective-permute-start.5 = (bf16[4,24,640]{2,1,0:T(8,128)(2,1)S(1)}, bf16[4,24,640]{2,1,0:T(8,128)(2,1)S(1)}, u32[]{:S(2)}, u32[]{:S(2)}) collective-permute-start(bf16[4,24,640]{2,1,0:T(8,128)(2,1)S(1)} %pad_maximum_fusion.9), channel_id=1, source_target_pairs={{8,0},{16,8},{24,16},{0,24},{9,1},{17,9},{25,17},{1,25},{10,2},{18... | collective-permute-start | bytes 368648 | tf_op jit(solution)/shard_map/ppermute | solution.py:527
  32.3 2.5 collective-permute-start.7
  35.7 9.0 %collective-permute-done.10.refs_1_.refs_5_ = bf16[256,768]{1,0:T(8,128)(2,1)} collective-permute-done((bf16[256,768]{1,0:T(8,128)(2,1)S(1)}, bf16[256,768]{1,0:T(8,128)(2,1)}, u32[]{:S(2)}, u32[]{:S(2)}) %collective-permute-start.10) | collective-permute-done | bytes 393248 | tf_op jit(solution)/shard_map/ppermute | solution.py:527
  45.8 14.1 %collective-permute-done.6 = bf16[4,24,640]{2,1,0:T(8,128)(2,1)S(1)} collective-permute-done((bf16[4,24,640]{2,1,0:T(8,128)(2,1)S(1)}, bf16[4,24,640]{2,1,0:T(8,128)(2,1)S(1)}, u32[]{:S(2)}, u32[]{:S(2)}) %collective-permute-start.6) | collective-permute-done | bytes 122912 | tf_op jit(solution)/shard_map/ppermute | solution.py:527
  64.8 20.9 %collective-permute-done.14.refs_1_.refs_5_ = bf16[256,768]{1,0:T(8,128)(2,1)} collective-permute-done((bf16[256,768]{1,0:T(8,128)(2,1)S(1)}, bf16[256,768]{1,0:T(8,128)(2,1)}, u32[]{:S(2)}, u32[]{:S(2)}) %collective-permute-start.14) | collective-permute-done | bytes 393248 | tf_op jit(solution)/shard_map/ppermute | solution.py:527
  93.1 10.4 %attend_forward.4 = (bf16[3,1024,256]{2,1,0:T(8,128)(2,1)}, bf16[3,1024,128]{2,1,0:T(8,128)(2,1)}, bf16[3,1024,256]{2,1,0:T(8,128)(2,1)}, bf16[3,1024,128]{2,1,0...) custom-call(s32[5]{0:T(128)} %stack.268.refs_0_, bf16[256,768]{1,0:T(8,128)(2,1)} %bitcast.282, ...), custom_call_target="tpu_custom_call" | custom-call | flops 8000000000 | bytes 10000000 | tf_op jit(solution)/shard_map/attend_forward/pallas_call | solution.py:169
  104.5 7.7 %collective-permute-done.16.refs_3_.refs_7_ = bf16[256,768]{1,0:T(8,128)(2,1)S(1)} collective-permute-done((bf16[256,768]{1,0:T(8,128)(2,1)}, bf16[256,768]{1,0:T(8,128)(2,1)S(1)}, u32[]{:S(2)}, u32[]{:S(2)}) %collective-permute-start.16) | collective-permute-done | bytes 393248 | tf_op jit(solution)/shard_map/ppermute | solution.py:536
  115.4 10.5 %attend_forward.5 = (bf16[3,1024,256]{2,1,0:T(8,128)(2,1)}, bf16[3,1024,128]{2,1,0:T(8,128)(2,1)}, f32[3,8,1024]{2,1,0:T(8,128)}, f32[3,80,1024]{2,1,0:T(8,128)}) custom-call(s32[5]{0:T(128)} %stack.235.refs_0_, bf16[256,768]{1,0:T(8,128)(2,1)} %copy-done.22, bf16[256,768]{1,0:T(8,128)(2,1)} %get-tuple-element.230.refs_2_.refs_6_, ...), custom_call_target="tpu_custom_call" | custom-call | flops 8000000000 | bytes 10000000 | tf_op jit(solution)/shard_map/attend_forward/pallas_call | solution.py:169
  126.9 10.4 %attend_forward.6 = (bf16[3,1024,256]{2,1,0:T(8,128)(2,1)}, bf16[3,1024,128]{2,1,0:T(8,128)(2,1)}, f32[3,8,1024]{2,1,0:T(8,128)}, f32[3,80,1024]{2,1,0:T(8,128)}) custom-call(s32[5]{0:T(128)} %stack.279.refs_0_, bf16[256,768]{1,0:T(8,128)(2,1)} %collective-permute-done.10.refs_1_.refs_5_, bf16[256,768]{1,0:T(8,128)(2,1)} %get-tuple-element.262.refs_2_.refs_6_, ...), custom_call_target="tpu_custom_call" | custom-call | flops 8000000000 | bytes 10000000 | tf_op jit(solution)/shard_map/attend_forward/pallas_call | solution.py:169
  137.3 12.0 %attend_forward.7 = (bf16[3,1024,256]{2,1,0:T(8,128)(2,1)}, bf16[3,1024,128]{2,1,0:T(8,128)(2,1)}, bf16[256,192]{1,0:T(8,128)(2,1)}, bf16[256,192]{1,0:T(8,128)(...) custom-call(s32[5]{0:T(128)} %stack.230.refs_0_, ...), custom_call_target="tpu_custom_call" | custom-call | flops 8000000000 | bytes 10000000 | tf_op jit(solution)/shard_map/attend_forward/pallas_call | solution.py:169
  152.4 3.9 %collective-permute-done.19.refs_3_ = bf16[256,192]{1,0:T(8,128)(2,1)S(1)} collective-permute-done((bf16[256,192]{1,0:T(8,128)(2,1)}, bf16[256,192]{1,0:T(8,128)(2,1)S(1)}, u32[]{:S(2)}, u32[]{:S(2)}) %collective-permute-start.19) | collective-permute-done | bytes 98336 | tf_op jit(solution)/shard_map/ppermute | solution.py:536
  158.0 20.3 %feed_forward.1 = (bf16[256,768]{1,0:T(8,128)(2,1)}, f32[256,768]{1,0:T(8,128)}, bf16[256,192]{1,0:T(8,128)(2,1)}, bf16[256,192]{1,0:T(8,128)(2,1)}, bf16[256,19...) custom-call(s32[7]{0:T(128)} %stack.225.refs_0_, ...), custom_call_target="tpu_custom_call" | custom-call | flops 20000000000 | bytes 30000000 | tf_op jit(solution)/shard_map/feed_forward/pallas_call | solution.py:480
  187.7 2.4 fusion.4
  191.4 16.0 %attend_backward.4 = (bf16[2,256,768]{2,1,0:T(8,128)(2,1)}, bf16[2,256,768]{2,1,0:T(8,128)(2,1)}, bf16[3,1024,128]{2,1,0:T(8,128)(2,1)}, f32[3,64,1024]{2,1,0:T(...) custom-call(bf16[3,1024,256]{2,1,0:T(8,128)(2,1)} %get-tuple-element.279.refs_0_, ...), custom_call_target="tpu_custom_call" | custom-call | flops 15000000512 | bytes 10000000 | tf_op jit(solution)/shard_map/attend_backward/pallas_call | solution.py:311
  207.4 4.8 %collective-permute-done.25 = bf16[2,4,24,2304]{3,2,1,0:T(8,128)(2,1)} collective-permute-done((bf16[2,4,24,2304]{3,2,1,0:T(8,128)(2,1)}, bf16[2,4,24,2304]{3,2,1,0:T(8,128)(2,1)}, u32[]{:S(2)}, u32[]{:S(2)}) %collective-permute-start.25) | collective-permute-done | bytes 884768 | tf_op jit(solution)/shard_map/ppermute | solution.py:527
  220.0 16.0 %attend_backward.5 = (bf16[2,256,768]{2,1,0:T(8,128)(2,1)}, bf16[2,256,768]{2,1,0:T(8,128)(2,1)}, f32[3,64,1024]{2,1,0:T(8,128)}, f32[768,512]{1,0:T(8,128)}, f32[8,512]{1,0:T(8,128)}) custom-call(bf16[3,1024,256]{2,1,0:T(8,128)(2,1)} %get-tuple-element.303.refs_0_, bf16[3,1024,128]{2,1,0:T(8,128)(2,1)} %get-tuple-element.304.refs_1_, ...), custom_call_target="tpu_custom_call" | custom-call | flops 15000000512 | bytes 10000000 | tf_op jit(solution)/shard_map/attend_backward/pallas_call | solution.py:311
  250.0 3.3 collective-permute-done.33
  254.8 16.0 %attend_backward.6 = (bf16[2,256,768]{2,1,0:T(8,128)(2,1)}, bf16[2,256,768]{2,1,0:T(8,128)(2,1)}, f32[3,64,1024]{2,1,0:T(8,128)}, f32[768,512]{1,0:T(8,128)}, f32[8,512]{1,0:T(8,128)}) custom-call(bf16[3,1024,256]{2,1,0:T(8,128)(2,1)} %get-tuple-element.275.refs_0_, bf16[3,1024,128]{2,1,0:T(8,128)(2,1)} %get-tuple-element.276.refs_1_, ...), custom_call_target="tpu_custom_call" | custom-call | flops 15000000512 | bytes 10000000 | tf_op jit(solution)/shard_map/attend_backward/pallas_call | solution.py:311
  273.1 9.6 %collective-permute-done.35 = bf16[24,2304]{1,0:T(8,128)(2,1)S(1)} collective-permute-done((bf16[24,2304]{1,0:T(8,128)(2,1)}, bf16[24,2304]{1,0:T(8,128)(2,1)S(1)}, u32[]{:S(2)}, u32[]{:S(2)}) %collective-permute-start.35) | collective-permute-done | bytes 110624 | tf_op jit(solution)/shard_map/ppermute | solution.py:527
  284.6 3.2 collective-permute-start.45
  293.1 2.9 collective-permute-start.42
  299.2 16.5 %attend_backward.7 = (bf16[2,256,768]{2,1,0:T(8,128)(2,1)}, bf16[2,256,768]{2,1,0:T(8,128)(2,1)}, bf16[768,640]{1,0:T(8,128)(2,1)}, f32[8,640]{1,0:T(8,128)}) custom-call(bf16[3,1024,256]{2,1,0:T(8,128)(2,1)} %get-tuple-element.354.refs_0_, bf16[3,1024,128]{2,1,0:T(8,128)(2,1)} %get-tuple-element.355.refs_1_, ...), custom_call_target="tpu_custom_call" | custom-call | flops 15000000512 | bytes 10000000 | tf_op jit(solution)/shard_map/attend_backward/pallas_call | solution.py:311
  316.8 3.9 %collective-permute-done.43 = bf16[24,2304]{1,0:T(8,128)(2,1)S(1)} collective-permute-done((bf16[24,2304]{1,0:T(8,128)(2,1)}, bf16[24,2304]{1,0:T(8,128)(2,1)S(1)}, u32[]{:S(2)}, u32[]{:S(2)}) %collective-permute-start.43) | collective-permute-done | bytes 110624 | tf_op jit(solution)/shard_map/ppermute | solution.py:527
  325.9 2.8 collective-permute-start.49
  333.6 4.6 %collective-permute-done.48 = bf16[24,2304]{1,0:T(8,128)(2,1)} collective-permute-done((bf16[24,2304]{1,0:T(8,128)(2,1)}, bf16[24,2304]{1,0:T(8,128)(2,1)}, u32[]{:S(2)}, u32[]{:S(2)}) %collective-permute-start.48) | collective-permute-done | bytes 110624 | tf_op jit(solution)/shard_map/ppermute | solution.py:527
  340.6 6.7 %collective-permute-done.47 = bf16[4,4,24,640]{3,2,1,0:T(8,128)(2,1)S(1)} collective-permute-done((bf16[4,4,24,640]{3,2,1,0:T(8,128)(2,1)S(1)}, bf16[4,4,24,640]{3,2,1,0:T(8,128)(2,1)S(1)}, u32[]{:S(2)}, u32[]{:S(2)}) %collective-permute-start.47) | collective-permute-done | bytes 491552 | tf_op jit(solution)/shard_map/ppermute | solution.py:527
  355.9 2.6 collective-permute-start.55
  366.5 2.4 fusion.12
  (360 shorter events, 110.0 us)
Async XLA Ops:
  7.2 150.2 %all-gather.2.cloned.1.call-start = ((), (), s32[]{:S(2)}) async-start(), calls=%async_computation | async-start | bytes 10948608 | tf_op jit(solution)/shard_map/all_gather | solution.py:653
  13.1 14.0 %collective-permute-start.4 = (bf16[256,768]{1,0:T(8,128)(2,1)S(1)}, bf16[256,768]{1,0:T(8,128)(2,1)S(1)}, u32[]{:S(2)}, u32[]{:S(2)}) collective-permute-start(bf16[256,768]{1,0:T(8,128)(2,1)S(1)} %bitcast.286), channel_id=1, source_target_pairs={{8,0},{16,8},{24,16},{0,24},{9,1},{17,9},{25,17},{1,25},{10,2},{18... | collective-permute-start | bytes 1179656 | tf_op jit(solution)/shard_map/ppermute | solution.py:527
  27.3 17.4 %collective-permute-start.10 = (bf16[256,768]{1,0:T(8,128)(2,1)S(1)}, bf16[256,768]{1,0:T(8,128)(2,1)}, u32[]{:S(2)}, u32[]{:S(2)}) collective-permute-start(bf16[256,768]{1,0:T(8,128)(2,1)S(1)} %bitcast.287), channel_id=1, source_target_pairs={{24,0},{0,8},{8,16},{16,24},{25,1},{1,9},{9,17},{17,25},{26,2},{2,... | collective-permute-start | bytes 1179656 | tf_op jit(solution)/shard_map/ppermute | solution.py:527
  27.3 32.6 %collective-permute-start.9 = (bf16[256,768]{1,0:T(8,128)(2,1)S(1)}, bf16[256,768]{1,0:T(8,128)(2,1)S(1)}, u32[]{:S(2)}, u32[]{:S(2)}) collective-permute-start(bf16[256,768]{1,0:T(8,128)(2,1)S(1)} %collective-permute-done.4.refs_1_.refs_5_), channel_id=1, source_target_pairs={{0,4},{4,0},{1,5},{5,1},{2,6},{6,2},{3,7},{7,3},{8,12},{12,8},{9,1... | collective-permute-start | bytes 1179656 | tf_op jit(solution)/shard_map/ppermute | solution.py:536
  27.4 18.3 %collective-permute-start.5 = (bf16[4,24,640]{2,1,0:T(8,128)(2,1)S(1)}, bf16[4,24,640]{2,1,0:T(8,128)(2,1)S(1)}, u32[]{:S(2)}, u32[]{:S(2)}) collective-permute-start(bf16[4,24,640]{2,1,0:T(8,128)(2,1)S(1)} %pad_maximum_fusion.9), channel_id=1, source_target_pairs={{8,0},{16,8},{24,16},{0,24},{9,1},{17,9},{25,17},{1,25},{10,2},{18... | collective-permute-start | bytes 368648 | tf_op jit(solution)/shard_map/ppermute | solution.py:527
  31.8 28.1 %collective-permute-start.6 = (bf16[4,24,640]{2,1,0:T(8,128)(2,1)S(1)}, bf16[4,24,640]{2,1,0:T(8,128)(2,1)S(1)}, u32[]{:S(2)}, u32[]{:S(2)}) collective-permute-start(bf16[4,24,640]{2,1,0:T(8,128)(2,1)S(1)} %pad_maximum_fusion.9), channel_id=1, source_target_pairs={{16,0},{24,8},{0,16},{8,24},{17,1},{25,9},{1,17},{9,25},{18,2},{26... | collective-permute-start | bytes 368648 | tf_op jit(solution)/shard_map/ppermute | solution.py:527
  32.3 27.6 %collective-permute-start.7 = (bf16[4,24,640]{2,1,0:T(8,128)(2,1)S(1)}, bf16[4,24,640]{2,1,0:T(8,128)(2,1)S(1)}, u32[]{:S(2)}, u32[]{:S(2)}) collective-permute-start(bf16[4,24,640]{2,1,0:T(8,128)(2,1)S(1)} %pad_maximum_fusion.9), channel_id=1, source_target_pairs={{24,0},{0,8},{8,16},{16,24},{25,1},{1,9},{9,17},{17,25},{26,2},{2,... | collective-permute-start | bytes 368648 | tf_op jit(solution)/shard_map/ppermute | solution.py:527
  60.2 25.5 %collective-permute-start.11 = (bf16[4,4,24,640]{3,2,1,0:T(8,128)(2,1)S(1)}, bf16[4,4,24,640]{3,2,1,0:T(8,128)(2,1)S(1)}, u32[]{:S(2)}, u32[]{:S(2)}) collective-permute-start(bf16[4,4,24,640]{3,2,1,0:T(8,128)(2,1)S(1)} %pad_maximum_fusion.5), channel_id=1, source_target_pairs={{1,0},{0,1},{3,2},{2,3},{5,4},{4,5},{7,6},{6,7},{9,8},{8,9},{11,10... | collective-permute-start | bytes 1474568 | tf_op jit(solution)/shard_map/ppermute | solution.py:527
  61.8 23.9 %collective-permute-start.14 = (bf16[256,768]{1,0:T(8,128)(2,1)S(1)}, bf16[256,768]{1,0:T(8,128)(2,1)}, u32[]{:S(2)}, u32[]{:S(2)}) collective-permute-start(bf16[256,768]{1,0:T(8,128)(2,1)S(1)} %bitcast.288), channel_id=1, source_target_pairs={{16,0},{24,8},{0,16},{8,24},{17,1},{25,9},{1,17},{9,25},{18,2},{26... | collective-permute-start | bytes 1179656 | tf_op jit(solution)/shard_map/ppermute | solution.py:527
  61.8 23.9 %collective-permute-start.13 = (bf16[256,768]{1,0:T(8,128)(2,1)}, bf16[256,768]{1,0:T(8,128)(2,1)S(1)}, u32[]{:S(2)}, u32[]{:S(2)}) collective-permute-start(bf16[256,768]{1,0:T(8,128)(2,1)} %collective-permute-done.10.refs_1_.refs_5_), channel_id=1, source_target_pairs={{0,4},{4,0},{1,5},{5,1},{2,6},{6,2},{3,7},{7,3},{8,12},{12,8},{9,1... | collective-permute-start | bytes 1179656 | tf_op jit(solution)/shard_map/ppermute | solution.py:536
  87.0 16.5 %collective-permute-start.15 = (bf16[2,256,768]{2,1,0:T(8,128)(2,1)S(1)}, bf16[2,256,768]{2,1,0:T(8,128)(2,1)S(1)}, u32[]{:S(2)}, u32[]{:S(2)}) collective-permute-start(bf16[2,256,768]{2,1,0:T(8,128)(2,1)S(1)} %pad_maximum_fusion.3), channel_id=1, source_target_pairs={{0,2},{2,0},{1,3},{3,1},{4,6},{6,4},{5,7},{7,5},{8,10},{10,8},{9,1... | collective-permute-start | bytes 2359304 | tf_op jit(solution)/shard_map/ppermute | solution.py:534
  91.7 20.5 %collective-permute-start.16 = (bf16[256,768]{1,0:T(8,128)(2,1)}, bf16[256,768]{1,0:T(8,128)(2,1)S(1)}, u32[]{:S(2)}, u32[]{:S(2)}) collective-permute-start(bf16[256,768]{1,0:T(8,128)(2,1)} %collective-permute-done.14.refs_1_.refs_5_), channel_id=1, source_target_pairs={{0,4},{4,0},{1,5},{5,1},{2,6},{6,2},{3,7},{7,3},{8,12},{12,8},{9,1... | collective-permute-start | bytes 1179656 | tf_op jit(solution)/shard_map/ppermute | solution.py:536
  184.4 23.0 %collective-permute-start.26 = (bf16[2,4,48,2304]{3,2,1,0:T(8,128)(2,1)}, bf16[2,4,48,2304]{3,2,1,0:T(8,128)(2,1)}, u32[]{:S(2)}, u32[]{:S(2)}) collective-permute-start(bf16[2,4,48,2304]{3,2,1,0:T(8,128)(2,1)} %get-tuple-element.301), channel_id=1, source_target_pairs={{0,2},{2,0},{1,3},{3,1},{4,6},{6,4},{5,7},{7,5},{8,10},{10,8},{9,1... | collective-permute-start | bytes 5308424 | tf_op jit(solution)/shard_map/ppermute | solution.py:534
  184.7 51.3 %collective-permute-start.30 = (bf16[2,4,48,2304]{3,2,1,0:T(8,128)(2,1)}, bf16[2,4,48,2304]{3,2,1,0:T(8,128)(2,1)}, u32[]{:S(2)}, u32[]{:S(2)}) collective-permute-start(bf16[2,4,48,2304]{3,2,1,0:T(8,128)(2,1)} %get-tuple-element.325), channel_id=1, source_target_pairs={{0,2},{2,0},{1,3},{3,1},{4,6},{6,4},{5,7},{7,5},{8,10},{10,8},{9,1... | collective-permute-start | bytes 5308424 | tf_op jit(solution)/shard_map/ppermute | solution.py:534
  190.1 22.1 %collective-permute-start.25 = (bf16[2,4,24,2304]{3,2,1,0:T(8,128)(2,1)}, bf16[2,4,24,2304]{3,2,1,0:T(8,128)(2,1)}, u32[]{:S(2)}, u32[]{:S(2)}) collective-permute-start(bf16[2,4,24,2304]{3,2,1,0:T(8,128)(2,1)} %fusion.4), channel_id=1, source_target_pairs={{1,0},{0,1},{3,2},{2,3},{5,4},{4,5},{7,6},{6,7},{9,8},{8,9},{11,10... | collective-permute-start | bytes 2654216 | tf_op jit(solution)/shard_map/ppermute | solution.py:527
  214.7 22.3 %collective-permute-start.29 = (bf16[2,4,24,2304]{3,2,1,0:T(8,128)(2,1)}, bf16[2,4,24,2304]{3,2,1,0:T(8,128)(2,1)}, u32[]{:S(2)}, u32[]{:S(2)}) collective-permute-start(bf16[2,4,24,2304]{3,2,1,0:T(8,128)(2,1)} %fusion.5), channel_id=1, source_target_pairs={{1,0},{0,1},{3,2},{2,3},{5,4},{4,5},{7,6},{6,7},{9,8},{8,9},{11,10... | collective-permute-start | bytes 2654216 | tf_op jit(solution)/shard_map/ppermute | solution.py:527
  217.6 18.5 %collective-permute-start.28 = (bf16[4,24,2304]{2,1,0:T(8,128)(2,1)S(1)}, bf16[4,24,2304]{2,1,0:T(8,128)(2,1)S(1)}, u32[]{:S(2)}, u32[]{:S(2)}) collective-permute-start(bf16[4,24,2304]{2,1,0:T(8,128)(2,1)S(1)} %fusion.9), channel_id=1, source_target_pairs={{4,0},{0,4},{5,1},{1,5},{6,2},{2,6},{7,3},{3,7},{12,8},{8,12},{13,... | collective-permute-start | bytes 1327112 | tf_op jit(solution)/shard_map/ppermute | solution.py:527
  218.9 19.4 %collective-permute-start.31 = (bf16[256,768]{1,0:T(8,128)(2,1)S(1)}, bf16[256,768]{1,0:T(8,128)(2,1)S(1)}, u32[]{:S(2)}, u32[]{:S(2)}) collective-permute-start(bf16[256,768]{1,0:T(8,128)(2,1)S(1)} %fusion.13), channel_id=1, source_target_pairs={{0,4},{4,0},{1,5},{5,1},{2,6},{6,2},{3,7},{7,3},{8,12},{12,8},{9,1... | collective-permute-start | bytes 1179656 | tf_op jit(solution)/shard_map/ppermute | solution.py:536
  239.1 43.6 %collective-permute-start.38 = (bf16[256,768]{1,0:T(8,128)(2,1)}, bf16[256,768]{1,0:T(8,128)(2,1)}, u32[]{:S(2)}, u32[]{:S(2)}) collective-permute-start(bf16[256,768]{1,0:T(8,128)(2,1)} %add_convert_fusion.6), channel_id=1, source_target_pairs={{16,0},{24,8},{0,16},{8,24},{17,1},{25,9},{1,17},{9,25},{18,2},{26... | collective-permute-start | bytes 1179656 | tf_op jit(solution)/shard_map/ppermute | solution.py:527
  241.5 41.2 %collective-permute-start.37 = (bf16[2,4,24,2304]{3,2,1,0:T(8,128)(2,1)}, bf16[2,4,24,2304]{3,2,1,0:T(8,128)(2,1)S(1)}, u32[]{:S(2)}, u32[]{:S(2)}) collective-permute-start(bf16[2,4,24,2304]{3,2,1,0:T(8,128)(2,1)} %fusion.6), channel_id=1, source_target_pairs={{1,0},{0,1},{3,2},{2,3},{5,4},{4,5},{7,6},{6,7},{9,8},{8,9},{11,10... | collective-permute-start | bytes 2654216 | tf_op jit(solution)/shard_map/ppermute | solution.py:527
  244.2 38.6 %collective-permute-start.36 = (bf16[4,24,2304]{2,1,0:T(8,128)(2,1)S(1)}, bf16[4,24,2304]{2,1,0:T(8,128)(2,1)}, u32[]{:S(2)}, u32[]{:S(2)}) collective-permute-start(bf16[4,24,2304]{2,1,0:T(8,128)(2,1)S(1)} %fusion.10), channel_id=1, source_target_pairs={{4,0},{0,4},{5,1},{1,5},{6,2},{2,6},{7,3},{3,7},{12,8},{8,12},{13,... | collective-permute-start | bytes 1327112 | tf_op jit(solution)/shard_map/ppermute | solution.py:527
  246.8 24.0 %collective-permute-start.34 = (bf16[24,2304]{1,0:T(8,128)(2,1)}, bf16[24,2304]{1,0:T(8,128)(2,1)S(1)}, u32[]{:S(2)}, u32[]{:S(2)}) collective-permute-start(bf16[24,2304]{1,0:T(8,128)(2,1)} %get-tuple-element.451), channel_id=1, source_target_pairs={{16,0},{24,8},{0,16},{8,24},{17,1},{25,9},{1,17},{9,25},{18,2},{26... | collective-permute-start | bytes 331784 | tf_op jit(solution)/shard_map/ppermute | solution.py:527
  253.3 29.4 %collective-permute-start.39 = (bf16[256,768]{1,0:T(8,128)(2,1)}, bf16[256,768]{1,0:T(8,128)(2,1)}, u32[]{:S(2)}, u32[]{:S(2)}) collective-permute-start(bf16[256,768]{1,0:T(8,128)(2,1)} %fusion.14), channel_id=1, source_target_pairs={{0,4},{4,0},{1,5},{5,1},{2,6},{6,2},{3,7},{7,3},{8,12},{12,8},{9,1... | collective-permute-start | bytes 1179656 | tf_op jit(solution)/shard_map/ppermute | solution.py:536
  282.7 15.6 %collective-permute-start.40 = (bf16[2,256,768]{2,1,0:T(8,128)(2,1)}, bf16[2,256,768]{2,1,0:T(8,128)(2,1)S(1)}, u32[]{:S(2)}, u32[]{:S(2)}) collective-permute-start(bf16[2,256,768]{2,1,0:T(8,128)(2,1)} %get-tuple-element.360), channel_id=1, source_target_pairs={{0,2},{2,0},{1,3},{3,1},{4,6},{6,4},{5,7},{7,5},{8,10},{10,8},{9,1... | collective-permute-start | bytes 2359304 | tf_op jit(solution)/shard_map/ppermute | solution.py:534
  284.6 36.1 %collective-permute-start.45 = (bf16[256,768]{1,0:T(8,128)(2,1)}, bf16[256,768]{1,0:T(8,128)(2,1)}, u32[]{:S(2)}, u32[]{:S(2)}) collective-permute-start(bf16[256,768]{1,0:T(8,128)(2,1)} %add_convert_fusion.5), channel_id=1, source_target_pairs={{8,0},{16,8},{24,16},{0,24},{9,1},{17,9},{25,17},{1,25},{10,2},{18... | collective-permute-start | bytes 1179656 | tf_op jit(solution)/shard_map/ppermute | solution.py:527
  289.4 31.3 %collective-permute-start.44 = (bf16[4,24,2304]{2,1,0:T(8,128)(2,1)S(1)}, bf16[4,24,2304]{2,1,0:T(8,128)(2,1)S(1)}, u32[]{:S(2)}, u32[]{:S(2)}) collective-permute-start(bf16[4,24,2304]{2,1,0:T(8,128)(2,1)S(1)} %fusion.11), channel_id=1, source_target_pairs={{4,0},{0,4},{5,1},{1,5},{6,2},{2,6},{7,3},{3,7},{12,8},{8,12},{13,... | collective-permute-start | bytes 1327112 | tf_op jit(solution)/shard_map/ppermute | solution.py:527
  292.8 22.8 %collective-permute-start.41 = (bf16[24,2304]{1,0:T(8,128)(2,1)}, bf16[24,2304]{1,0:T(8,128)(2,1)S(1)}, u32[]{:S(2)}, u32[]{:S(2)}) collective-permute-start(bf16[24,2304]{1,0:T(8,128)(2,1)} %get-tuple-element.449), channel_id=1, source_target_pairs={{24,0},{0,8},{8,16},{16,24},{25,1},{1,9},{9,17},{17,25},{26,2},{2,... | collective-permute-start | bytes 331784 | tf_op jit(solution)/shard_map/ppermute | solution.py:527
  293.1 23.7 %collective-permute-start.42 = (bf16[24,2304]{1,0:T(8,128)(2,1)}, bf16[24,2304]{1,0:T(8,128)(2,1)S(1)}, u32[]{:S(2)}, u32[]{:S(2)}) collective-permute-start(bf16[24,2304]{1,0:T(8,128)(2,1)} %get-tuple-element.448), channel_id=1, source_target_pairs={{16,0},{24,8},{0,16},{8,24},{17,1},{25,9},{1,17},{9,25},{18,2},{26... | collective-permute-start | bytes 331784 | tf_op jit(solution)/shard_map/ppermute | solution.py:527
  298.6 22.1 %collective-permute-start.46 = (bf16[256,768]{1,0:T(8,128)(2,1)S(1)}, bf16[256,768]{1,0:T(8,128)(2,1)}, u32[]{:S(2)}, u32[]{:S(2)}) collective-permute-start(bf16[256,768]{1,0:T(8,128)(2,1)S(1)} %fusion.15), channel_id=1, source_target_pairs={{0,4},{4,0},{1,5},{5,1},{2,6},{6,2},{3,7},{7,3},{8,12},{12,8},{9,1... | collective-permute-start | bytes 1179656 | tf_op jit(solution)/shard_map/ppermute | solution.py:536
  322.5 18.2 %collective-permute-start.51 = (bf16[256,768]{1,0:T(8,128)(2,1)S(1)}, bf16[256,768]{1,0:T(8,128)(2,1)S(1)}, u32[]{:S(2)}, u32[]{:S(2)}) collective-permute-start(bf16[256,768]{1,0:T(8,128)(2,1)S(1)} %add_convert_fusion.4), channel_id=1, source_target_pairs={{24,0},{0,8},{8,16},{16,24},{25,1},{1,9},{9,17},{17,25},{26,2},{2,... | collective-permute-start | bytes 1179656 | tf_op jit(solution)/shard_map/ppermute | solution.py:527
  325.9 14.7 %collective-permute-start.49 = (bf16[24,2304]{1,0:T(8,128)(2,1)}, bf16[24,2304]{1,0:T(8,128)(2,1)}, u32[]{:S(2)}, u32[]{:S(2)}) collective-permute-start(bf16[24,2304]{1,0:T(8,128)(2,1)} %get-tuple-element.445), channel_id=1, source_target_pairs={{16,0},{24,8},{0,16},{8,24},{17,1},{25,9},{1,17},{9,25},{18,2},{26... | collective-permute-start | bytes 331784 | tf_op jit(solution)/shard_map/ppermute | solution.py:527
  332.1 15.3 %collective-permute-start.52 = (bf16[2,256,768]{2,1,0:T(8,128)(2,1)}, bf16[2,256,768]{2,1,0:T(8,128)(2,1)S(1)}, u32[]{:S(2)}, u32[]{:S(2)}) collective-permute-start(bf16[2,256,768]{2,1,0:T(8,128)(2,1)} %get-tuple-element.387), channel_id=1, source_target_pairs={{0,2},{2,0},{1,3},{3,1},{4,6},{6,4},{5,7},{7,5},{8,10},{10,8},{9,1... | collective-permute-start | bytes 2359304 | tf_op jit(solution)/shard_map/ppermute | solution.py:534
  (83 other events, 614.9 us)
Sparse Core Ops, SparseCore 0:
  11.5 119.5 all-gather.1

commit v4 on v3

--- a/solution.py
+++ b/solution.py
@@ -435,7 +435,7 @@
                 target, sem = targets[2 * i + dc], out_sem.at[2 * i + dc]
                 for dx in range(2):
                     for jz in range(n_q):
-                        m = (lax.rem(zi + jz, n_q) * 2 + (xi ^ dx)) * 2 + (ci ^ dc)
+                        m = ((zi ^ jz) * 2 + (xi ^ dx)) * 2 + (ci ^ dc)
                         at = pl.ds(pl.multiple_of(m * block, 16), block)
                         for place, unit in enumerate(part):
                             dst = target.at[dx, jz, :, lanes(place)]
@@ -577,14 +577,23 @@
         total = own_b(keep, got, 0) + sum(v.astype(f32) for v in more)
         return total[0], *away_sum(total, "x", 2)
 
-    def over_q(own, *more):
-        total = own + sum(v.astype(f32) for v in more)
-        return total[0], *away_sum(total, "q", n_q)
-
-    return Chain((keep, send), over_core, over_b, over_x, over_q)
-
-
-def token_sum(keep, send, n_q, j):
+    def halve(half):
+        def over_q(own, got):
+            total = own + got.astype(f32)
+            pairs = [(i, i ^ half) for i in range(n_q)]
+            return total[:half], lax.ppermute(total[half:].astype(bf16), "q", pairs)
+
+        return over_q
+
+    halves = [n_q >> (k + 1) for k in range(n_q.bit_length() - 1)]
+    return Chain((keep, send), over_core, over_b, over_x, *[halve(half) for half in halves])
+
+
+def toward(j, n_q):
+    return (j - 1, n_q - 1) if 2 * j <= n_q else ((j + 1) % n_q, 1)
+
+
+def token_sum(keep, send, n_q, j, farther):
     def over_core(keep, send):
         return keep, square_swap(send, 1)
 
@@ -593,14 +602,14 @@
         return total[0], square_swap(total[1].astype(bf16), 2)
 
     def over_q(own, got):
-        total = own + got.astype(f32)
-        return (from_shift(total.astype(bf16), "q", n_q, n_q - j),)
+        total = own + got.astype(f32) + sum(chain_sum(c) for c in farther)
+        return (from_shift(total.astype(bf16), "q", n_q, toward(j, n_q)[1]),)
 
     return Chain((keep, send), over_core, over_x, *([over_q] if j else []))
 
 
 def chain_sum(chain):
-    return sum(v.astype(f32) for v in chain.state)
+    return sum(v.astype(f32).reshape(chain.state[0].shape) for v in chain.state)
 
 
 def deinterleave(fold):
@@ -635,7 +644,7 @@
     own_rows = triple_weight.shape[0]
     ff = expand_weight.shape[1]
     fold = ff // width
-    aligned = n_b * own_rows % 16 == 0
+    aligned = n_b * own_rows % 16 == 0 and n_q & (n_q - 1) == 0
     x_own = inputs[0]
 
     turn = deinterleave(fold)
@@ -678,8 +687,10 @@
     weight_rows = Chain([columns_of(group ^ r) for r in range(4)], rows_square, rows_q, rows_b)
 
     def token_chunk(j):
-        def over_q(own):
-            return (from_shift(own, "q", n_q, j),)
+        def over_q():
+            source, step = toward(j, n_q)
+            own = chunks[source].state[0] if source else x_own
+            return (from_shift(own, "q", n_q, n_q - step),)
 
         def over_x(own):
             return own, square_swap(own, 2)
@@ -688,7 +699,7 @@
             halves = square_swap(jnp.stack([own, other]), 1)
             return own, halves[0], other, halves[1]
 
-        return Chain((x_own,), *([over_q] if j else []), over_x, over_core)
+        return Chain(() if j else (x_own,), *([over_q] if j else []), over_x, over_core)
 
     arrival = []
     for j in [k for pair in zip(range(1, n_q), range(n_q - 1, 0, -1)) for k in pair]:
@@ -696,9 +707,13 @@
     arrival = [0] + arrival
     chunks = {j: token_chunk(j) for j in arrival}
     line = [chunks[j] for j in arrival]
-    for step in range(3):
-        ready = [c for i, c in enumerate(line) if i <= step + 1 and c.steps and (i or step < 2)]
-        run_stage([weight_rows] + ready)
+
+    def moving_at(slot):
+        begun = [c for i, c in enumerate(line) if slot >= (i if i > 1 else 0)]
+        return [c for c in begun if c.steps]
+
+    for slot in range(3):
+        run_stage([weight_rows] + moving_at(slot))
     chunk_x = {}
 
     by_distance = jnp.stack(weight_rows.state)
@@ -730,11 +745,10 @@
     carry = None
     for step, j in enumerate(arrival):
         first, last = step == 0, step == n_q - 1
-        while chunks[j].steps:
-            run_stage([c for c in line[step:] if c.steps])
+        assert not chunks[j].steps
         chunk_x[j] = chunks[j].state
         outs = attend_chunk(first, last, where_of(j), chunk_x[j], weights, carry)
-        outs = run_stage([c for c in line[step + 1 :] if c.steps], outs)
+        outs = run_stage(moving_at(3 + step), outs)
         kept[j] = (outs[0], outs[1])
         outs = outs[2:]
         if first:
@@ -761,14 +775,16 @@
     run_stage([square] + sums[:1])
     shared = (qx2, qp, w_own, square.state, attx)
     carry = None
-    moving = []
+    moving, moving_to = [], {}
     for step, j in enumerate(reversed(arrival)):
         first, last = step == 0, step == n_q - 1
         outs = attend_back_chunk(first, last, kept[j], chunk_x[j], shared, carry)
         begun = [c for c in sums[: step + 2] if c.steps]
         outs = run_stage(begun + [c for c in moving if c.steps], outs)
         keep, send = outs[:2]
-        moving.append(token_sum(keep, send, n_q, j))
+        farther = [c for k, c in moving_to.items() if k and toward(k, n_q)[0] == j and j]
+        moving_to[j] = token_sum(keep, send, n_q, j, farther)
+        moving.append(moving_to[j])
         outs = outs[2:]
         if first:
             dox = outs[0]
@@ -806,11 +822,12 @@
     while any(c.steps for c in [rows, *sums, *moving]):
         run_stage([c for c in [rows, *sums, *moving] if c.steps])
     token_grad = resid_first_grad
-    for chain in moving:
-        token_grad = token_grad + chain_sum(chain)
+    for j, chain in moving_to.items():
+        if j == 0 or toward(j, n_q)[0] == 0:
+            token_grad = token_grad + chain_sum(chain)
     input_grad = token_grad.astype(bf16)
     if aligned:
-        summed = jnp.concatenate([chain_sum(c) for c in sums], axis=1)
+        summed = jnp.concatenate([chain_sum(c)[0] for c in sums], axis=1)
     parts = jnp.stack(rows.state)
     parts = jnp.stack([pick(parts, group ^ g) for g in range(4)])
     grad_triple = parts[:, :, :VECTORS].reshape(GROUPS, own_rows, 3, OWN_WIDTH)

time: 383 us -> 353 us (0.922)
  waiting for transfers between devices: 106 us -> 78.8 us
    ppermute x29 -> x20, waiting for transfers between devices: 86.5 us -> 50.9 us  [from_shift(): lax.ppermute(value, axis, [((i + step) % count, i) for i in range(count)])]
    ppermute x0 -> x6, waiting for transfers between devices: none -> 14.3 us  [over_q(): return (total[:half], lax.ppermute(total[half:].astype(bf16), 'q', pairs))]
    ppermute x12, waiting for transfers between devices: 16.2 us -> 9.77 us  [square_swap(): return lax.ppermute(value, 'x', [(0, 1), (1, 0)])]
    ppermute x0 -> x6, starting transfers between devices: none -> 5.8 us  [over_q(): return (total[:half], lax.ppermute(total[half:].astype(bf16), 'q', pairs))]
    ppermute x29 -> x20, starting transfers between devices: 43.2 us -> 39.6 us  [from_shift(): lax.ppermute(value, axis, [((i + step) % count, i) for i in range(count)])]
  transfers between devices with their start and end apart: 61 -> 58, of which waited for: 23 -> 21; matrix products, arithmetic and copies ran while one was open for 13% -> 13% of each run, Pallas kernels for 29% -> 31%
where the time goes in v4:
time: 353 us; the launch traced here: 349 us
  Pallas kernels  130 us (37%)
  waiting for transfers between devices  78.8 us (22%)
  starting transfers between devices  63.5 us (18%)
  other arithmetic  32.2 us (9%)
  local copies, waits for them, and re-layouts  26.1 us (7%)
  between operations  16.7 us (5%)
    pallas_call x4, Pallas kernels, attend_back_chunk(): pl.pallas_call(partial(backward_kernel, first, last, min(512, rows), min(...  64.4 us
    ppermute x20, waiting for transfers between devices, from_shift(): lax.ppermute(value, axis, [((i + step) % count, i) for i in range(count)])  50.9 us
    pallas_call x4, Pallas kernels, attend_chunk(): pl.pallas_call(partial(forward_kernel, first, last, min(512, rows), min(1...  42.9 us
    ppermute x20, starting transfers between devices, from_shift(): lax.ppermute(value, axis, [((i + step) % count, i) for i in range(count)])  39.6 us
    pallas_call x1, Pallas kernels, ffn_block(): pl.pallas_call(partial(ffn_kernel, layout), out_shape=out_shape + targets...  20.3 us
    ppermute x6, waiting for transfers between devices, over_q(): return (total[:half], lax.ppermute(total[half:].astype(bf16), 'q', pairs))  14.3 us
    ppermute x12, starting transfers between devices, square_swap(): return lax.ppermute(value, 'x', [(0, 1), (1, 0)])  13.4 us
    ppermute x12, waiting for transfers between devices, square_swap(): return lax.ppermute(value, 'x', [(0, 1), (1, 0)])  9.77 us
  transfers between devices with their start and end apart: 58, of which 21 were waited for; matrix products, arithmetic and copies ran while one was open for 13% of the time, Pallas kernels for 31%

profile of v4, /device:TPU:0, one launch (start us, length us, event | category | flops | bytes accessed | tf_op | source)
XLA Modules:
  0.0 348.5 jit_solution(5981128830332522794)
XLA Ops:
  10.1 3.0 collective-permute-start.3
  13.1 3.6 %collective-permute-start.4 = (bf16[256,768]{1,0:T(8,128)(2,1)S(1)}, bf16[256,768]{1,0:T(8,128)(2,1)S(1)}, u32[]{:S(2)}, u32[]{:S(2)}) collective-permute-start(bf16[256,768]{1,0:T(8,128)(2,1)S(1)} %bitcast.268), channel_id=1, source_target_pairs={{8,0},{16,8},{24,16},{0,24},{9,1},{17,9},{25,17},{1,25},{10,2},{18... | collective-permute-start | bytes 1179656 | tf_op jit(solution)/shard_map/ppermute | solution.py:527
  20.7 2.4 collective-permute-done.1
  23.3 3.8 %collective-permute-done.4.refs_1_.refs_5_ = bf16[256,768]{1,0:T(8,128)(2,1)S(1)} collective-permute-done((bf16[256,768]{1,0:T(8,128)(2,1)S(1)}, bf16[256,768]{1,0:T(8,128)(2,1)S(1)}, u32[]{:S(2)}, u32[]{:S(2)}) %collective-permute-start.4) | collective-permute-done | bytes 393248 | tf_op jit(solution)/shard_map/ppermute | solution.py:527
  27.4 4.4 %collective-permute-start.5 = (bf16[4,24,640]{2,1,0:T(8,128)(2,1)S(1)}, bf16[4,24,640]{2,1,0:T(8,128)(2,1)S(1)}, u32[]{:S(2)}, u32[]{:S(2)}) collective-permute-start(bf16[4,24,640]{2,1,0:T(8,128)(2,1)S(1)} %pad_maximum_fusion.9), channel_id=1, source_target_pairs={{8,0},{16,8},{24,16},{0,24},{9,1},{17,9},{25,17},{1,25},{10,2},{18... | collective-permute-start | bytes 368648 | tf_op jit(solution)/shard_map/ppermute | solution.py:527
  33.4 5.6 %collective-permute-done.5 = bf16[4,24,640]{2,1,0:T(8,128)(2,1)S(1)} collective-permute-done((bf16[4,24,640]{2,1,0:T(8,128)(2,1)S(1)}, bf16[4,24,640]{2,1,0:T(8,128)(2,1)S(1)}, u32[]{:S(2)}, u32[]{:S(2)}) %collective-permute-start.5) | collective-permute-done | bytes 122912 | tf_op jit(solution)/shard_map/ppermute | solution.py:527
  38.9 5.8 %collective-permute-done.6 = bf16[4,24,640]{2,1,0:T(8,128)(2,1)S(1)} collective-permute-done((bf16[4,24,640]{2,1,0:T(8,128)(2,1)S(1)}, bf16[4,24,640]{2,1,0:T(8,128)(2,1)S(1)}, u32[]{:S(2)}, u32[]{:S(2)}) %collective-permute-start.6) | collective-permute-done | bytes 122912 | tf_op jit(solution)/shard_map/ppermute | solution.py:527
  50.2 18.1 %collective-permute-done.12.refs_1_.refs_5_ = bf16[256,768]{1,0:T(8,128)(2,1)S(1)} collective-permute-done((bf16[256,768]{1,0:T(8,128)(2,1)S(1)}, bf16[256,768]{1,0:T(8,128)(2,1)S(1)}, u32[]{:S(2)}, u32[]{:S(2)}) %collective-permute-start.12) | collective-permute-done | bytes 393248 | tf_op jit(solution)/shard_map/ppermute | solution.py:527
  69.5 2.3 order_rows.1.refs_5_.refs_4_
  74.1 6.0 %collective-permute-start.14 = (bf16[256,768]{1,0:T(8,128)(2,1)S(1)}, bf16[256,768]{1,0:T(8,128)(2,1)S(1)}, u32[]{:S(2)}, u32[]{:S(2)}) collective-permute-start(bf16[256,768]{1,0:T(8,128)(2,1)S(1)} %copy-done.19), channel_id=1, source_target_pairs={{8,0},{16,8},{24,16},{0,24},{9,1},{17,9},{25,17},{1,25},{10,2},{18... | collective-permute-start | bytes 1179656 | tf_op jit(solution)/shard_map/ppermute | solution.py:527
  80.8 10.3 %attend_forward.4 = (bf16[3,1024,256]{2,1,0:T(8,128)(2,1)}, bf16[3,1024,128]{2,1,0:T(8,128)(2,1)}, bf16[3,1024,256]{2,1,0:T(8,128)(2,1)}, bf16[3,1024,128]{2,1,0...) custom-call(s32[5]{0:T(128)} %stack.273.refs_0_, bf16[256,768]{1,0:T(8,128)(2,1)} %bitcast.264, ...), custom_call_target="tpu_custom_call" | custom-call | flops 8000000000 | bytes 10000000 | tf_op jit(solution)/shard_map/attend_forward/pallas_call | solution.py:169
  91.1 8.3 %collective-permute-done.14.refs_1_.refs_5_ = bf16[256,768]{1,0:T(8,128)(2,1)S(1)} collective-permute-done((bf16[256,768]{1,0:T(8,128)(2,1)S(1)}, bf16[256,768]{1,0:T(8,128)(2,1)S(1)}, u32[]{:S(2)}, u32[]{:S(2)}) %collective-permute-start.14) | collective-permute-done | bytes 393248 | tf_op jit(solution)/shard_map/ppermute | solution.py:527
  100.2 10.4 %attend_forward.5 = (bf16[3,1024,256]{2,1,0:T(8,128)(2,1)}, bf16[3,1024,128]{2,1,0:T(8,128)(2,1)}, f32[3,8,1024]{2,1,0:T(8,128)}, f32[3,80,1024]{2,1,0:T(8,128)}) custom-call(s32[5]{0:T(128)} %stack.240.refs_0_, bf16[256,768]{1,0:T(8,128)(2,1)} %copy-done.18, bf16[256,768]{1,0:T(8,128)(2,1)} %get-tuple-element.233.refs_2_.refs_6_, ...), custom_call_target="tpu_custom_call" | custom-call | flops 8000000000 | bytes 10000000 | tf_op jit(solution)/shard_map/attend_forward/pallas_call | solution.py:169
  113.5 10.3 %attend_forward.6 = (bf16[3,1024,256]{2,1,0:T(8,128)(2,1)}, bf16[3,1024,128]{2,1,0:T(8,128)(2,1)}, f32[3,8,1024]{2,1,0:T(8,128)}, f32[3,80,1024]{2,1,0:T(8,128)}) custom-call(s32[5]{0:T(128)} %stack.235.refs_0_, bf16[256,768]{1,0:T(8,128)(2,1)} %copy-done.21, bf16[256,768]{1,0:T(8,128)(2,1)} %get-tuple-element.260.refs_2_.refs_6_, ...), custom_call_target="tpu_custom_call" | custom-call | flops 8000000000 | bytes 10000000 | tf_op jit(solution)/shard_map/attend_forward/pallas_call | solution.py:169
  124.7 11.9 %attend_forward.7 = (bf16[3,1024,256]{2,1,0:T(8,128)(2,1)}, bf16[3,1024,128]{2,1,0:T(8,128)(2,1)}, bf16[256,192]{1,0:T(8,128)(2,1)}, bf16[256,192]{1,0:T(8,128)(...) custom-call(s32[5]{0:T(128)} %stack.230.refs_0_, ...), custom_call_target="tpu_custom_call" | custom-call | flops 8000000000 | bytes 10000000 | tf_op jit(solution)/shard_map/attend_forward/pallas_call | solution.py:169
  140.0 3.3 collective-permute-done.19.refs_3_
  146.2 20.3 %feed_forward.1 = (bf16[256,768]{1,0:T(8,128)(2,1)}, f32[256,768]{1,0:T(8,128)}, bf16[256,192]{1,0:T(8,128)(2,1)}, bf16[256,192]{1,0:T(8,128)(2,1)}, bf16[256,19...) custom-call(s32[7]{0:T(128)} %stack.225.refs_0_, ...), custom_call_target="tpu_custom_call" | custom-call | flops 20000000000 | bytes 30000000 | tf_op jit(solution)/shard_map/feed_forward/pallas_call | solution.py:480
  175.0 2.4 fusion.4
  177.4 4.5 %collective-permute-start.25 = (bf16[2,4,24,2304]{3,2,1,0:T(8,128)(2,1)}, bf16[2,4,24,2304]{3,2,1,0:T(8,128)(2,1)}, u32[]{:S(2)}, u32[]{:S(2)}) collective-permute-start(bf16[2,4,24,2304]{3,2,1,0:T(8,128)(2,1)} %fusion.4), channel_id=1, source_target_pairs={{1,0},{0,1},{3,2},{2,3},{5,4},{4,5},{7,6},{6,7},{9,8},{8,9},{11,10... | collective-permute-start | bytes 2654216 | tf_op jit(solution)/shard_map/ppermute | solution.py:527
  181.9 16.0 %attend_backward.4 = (bf16[2,256,768]{2,1,0:T(8,128)(2,1)}, bf16[2,256,768]{2,1,0:T(8,128)(2,1)}, bf16[3,1024,128]{2,1,0:T(8,128)(2,1)}, f32[3,64,1024]{2,1,0:T(...) custom-call(bf16[3,1024,256]{2,1,0:T(8,128)(2,1)} %get-tuple-element.287.refs_0_, ...), custom_call_target="tpu_custom_call" | custom-call | flops 15000000512 | bytes 10000000 | tf_op jit(solution)/shard_map/attend_backward/pallas_call | solution.py:311
  198.0 4.6 %collective-permute-done.25 = bf16[2,4,24,2304]{3,2,1,0:T(8,128)(2,1)} collective-permute-done((bf16[2,4,24,2304]{3,2,1,0:T(8,128)(2,1)}, bf16[2,4,24,2304]{3,2,1,0:T(8,128)(2,1)}, u32[]{:S(2)}, u32[]{:S(2)}) %collective-permute-start.25) | collective-permute-done | bytes 884768 | tf_op jit(solution)/shard_map/ppermute | solution.py:527
  202.5 2.3 fusion.5
  211.4 16.0 %attend_backward.5 = (bf16[2,256,768]{2,1,0:T(8,128)(2,1)}, bf16[2,256,768]{2,1,0:T(8,128)(2,1)}, f32[3,64,1024]{2,1,0:T(8,128)}, f32[768,512]{1,0:T(8,128)}, f32[8,512]{1,0:T(8,128)}) custom-call(bf16[3,1024,256]{2,1,0:T(8,128)(2,1)} %get-tuple-element.313.refs_0_, bf16[3,1024,128]{2,1,0:T(8,128)(2,1)} %get-tuple-element.314.refs_1_, ...), custom_call_target="tpu_custom_call" | custom-call | flops 15000000512 | bytes 10000000 | tf_op jit(solution)/shard_map/attend_backward/pallas_call | solution.py:311
  232.4 2.8 collective-permute-start.36
  235.2 2.3 fusion.6
  242.8 16.0 %attend_backward.6 = (bf16[2,256,768]{2,1,0:T(8,128)(2,1)}, bf16[2,256,768]{2,1,0:T(8,128)(2,1)}, f32[3,64,1024]{2,1,0:T(8,128)}, f32[768,512]{1,0:T(8,128)}, f32[8,512]{1,0:T(8,128)}) custom-call(bf16[3,1024,256]{2,1,0:T(8,128)(2,1)} %get-tuple-element.311.refs_0_, bf16[3,1024,128]{2,1,0:T(8,128)(2,1)} %get-tuple-element.312.refs_1_, ...), custom_call_target="tpu_custom_call" | custom-call | flops 15000000512 | bytes 10000000 | tf_op jit(solution)/shard_map/attend_backward/pallas_call | solution.py:311
  272.6 16.5 %attend_backward.7 = (bf16[2,256,768]{2,1,0:T(8,128)(2,1)}, bf16[2,256,768]{2,1,0:T(8,128)(2,1)}, bf16[768,640]{1,0:T(8,128)(2,1)}, f32[8,640]{1,0:T(8,128)}) custom-call(bf16[3,1024,256]{2,1,0:T(8,128)(2,1)} %get-tuple-element.283.refs_0_, bf16[3,1024,128]{2,1,0:T(8,128)(2,1)} %get-tuple-element.284.refs_1_, ...), custom_call_target="tpu_custom_call" | custom-call | flops 15000000512 | bytes 10000000 | tf_op jit(solution)/shard_map/attend_backward/pallas_call | solution.py:311
  292.4 2.4 collective-permute-start.46
  301.7 5.9 %collective-permute-done.45 = bf16[1,24,2304]{2,1,0:T(8,128)(2,1)} collective-permute-done((bf16[1,24,2304]{2,1,0:T(8,128)(2,1)S(1)}, bf16[1,24,2304]{2,1,0:T(8,128)(2,1)}, u32[]{:S(2)}, u32[]{:S(2)}) %collective-permute-start.45) | collective-permute-done | bytes 110624 | tf_op jit(solution)/shard_map/ppermute | solution.py:584
  307.5 5.6 %collective-permute-done.46 = bf16[2,24,2304]{2,1,0:T(8,128)(2,1)} collective-permute-done((bf16[2,24,2304]{2,1,0:T(8,128)(2,1)S(1)}, bf16[2,24,2304]{2,1,0:T(8,128)(2,1)}, u32[]{:S(2)}, u32[]{:S(2)}) %collective-permute-start.46) | collective-permute-done | bytes 221216 | tf_op jit(solution)/shard_map/ppermute | solution.py:584
  322.0 2.8 collective-permute-done.52
  324.8 4.1 %collective-permute-done.50 = bf16[4,24,640]{2,1,0:T(8,128)(2,1)S(1)} collective-permute-done((bf16[4,24,640]{2,1,0:T(8,128)(2,1)S(1)}, bf16[4,24,640]{2,1,0:T(8,128)(2,1)S(1)}, u32[]{:S(2)}, u32[]{:S(2)}) %collective-permute-start.50) | collective-permute-done | bytes 122912 | tf_op jit(solution)/shard_map/ppermute | solution.py:527
  (366 shorter events, 97.9 us)
Async XLA Ops:
  7.2 138.3 %all-gather.2.cloned.1.call-start = ((), (), s32[]{:S(2)}) async-start(), calls=%async_computation | async-start | bytes 10948608 | tf_op jit(solution)/shard_map/all_gather | solution.py:662
  10.1 13.2 %collective-permute-start.3 = (bf16[256,768]{1,0:T(8,128)(2,1)S(1)}, bf16[256,768]{1,0:T(8,128)(2,1)S(1)}, u32[]{:S(2)}, u32[]{:S(2)}) collective-permute-start(bf16[256,768]{1,0:T(8,128)(2,1)S(1)} %bitcast.267), channel_id=1, source_target_pairs={{0,4},{4,0},{1,5},{5,1},{2,6},{6,2},{3,7},{7,3},{8,12},{12,8},{9,1... | collective-permute-start | bytes 1179656 | tf_op jit(solution)/shard_map/ppermute | solution.py:536
  13.1 14.0 %collective-permute-start.4 = (bf16[256,768]{1,0:T(8,128)(2,1)S(1)}, bf16[256,768]{1,0:T(8,128)(2,1)S(1)}, u32[]{:S(2)}, u32[]{:S(2)}) collective-permute-start(bf16[256,768]{1,0:T(8,128)(2,1)S(1)} %bitcast.268), channel_id=1, source_target_pairs={{8,0},{16,8},{24,16},{0,24},{9,1},{17,9},{25,17},{1,25},{10,2},{18... | collective-permute-start | bytes 1179656 | tf_op jit(solution)/shard_map/ppermute | solution.py:527
  27.3 17.4 %collective-permute-start.9 = (bf16[256,768]{1,0:T(8,128)(2,1)S(1)}, bf16[256,768]{1,0:T(8,128)(2,1)S(1)}, u32[]{:S(2)}, u32[]{:S(2)}) collective-permute-start(bf16[256,768]{1,0:T(8,128)(2,1)S(1)} %collective-permute-done.4.refs_1_.refs_5_), channel_id=1, source_target_pairs={{0,4},{4,0},{1,5},{5,1},{2,6},{6,2},{3,7},{7,3},{8,12},{12,8},{9,1... | collective-permute-start | bytes 1179656 | tf_op jit(solution)/shard_map/ppermute | solution.py:536
  31.8 13.0 %collective-permute-start.6 = (bf16[4,24,640]{2,1,0:T(8,128)(2,1)S(1)}, bf16[4,24,640]{2,1,0:T(8,128)(2,1)S(1)}, u32[]{:S(2)}, u32[]{:S(2)}) collective-permute-start(bf16[4,24,640]{2,1,0:T(8,128)(2,1)S(1)} %pad_maximum_fusion.9), channel_id=1, source_target_pairs={{16,0},{24,8},{0,16},{8,24},{17,1},{25,9},{1,17},{9,25},{18,2},{26... | collective-permute-start | bytes 368648 | tf_op jit(solution)/shard_map/ppermute | solution.py:527
  31.8 13.0 %collective-permute-start.7 = (bf16[4,24,640]{2,1,0:T(8,128)(2,1)S(1)}, bf16[4,24,640]{2,1,0:T(8,128)(2,1)S(1)}, u32[]{:S(2)}, u32[]{:S(2)}) collective-permute-start(bf16[4,24,640]{2,1,0:T(8,128)(2,1)S(1)} %pad_maximum_fusion.9), channel_id=1, source_target_pairs={{24,0},{0,8},{8,16},{16,24},{25,1},{1,9},{9,17},{17,25},{26,2},{2,... | collective-permute-start | bytes 368648 | tf_op jit(solution)/shard_map/ppermute | solution.py:527
  45.5 22.9 %collective-permute-start.10 = (bf16[4,4,24,640]{3,2,1,0:T(8,128)(2,1)S(1)}, bf16[4,4,24,640]{3,2,1,0:T(8,128)(2,1)S(1)}, u32[]{:S(2)}, u32[]{:S(2)}) collective-permute-start(bf16[4,4,24,640]{3,2,1,0:T(8,128)(2,1)S(1)} %pad_maximum_fusion.5), channel_id=1, source_target_pairs={{1,0},{0,1},{3,2},{2,3},{5,4},{4,5},{7,6},{6,7},{9,8},{8,9},{11,10... | collective-permute-start | bytes 1474568 | tf_op jit(solution)/shard_map/ppermute | solution.py:527
  47.0 21.4 %collective-permute-start.12 = (bf16[256,768]{1,0:T(8,128)(2,1)S(1)}, bf16[256,768]{1,0:T(8,128)(2,1)S(1)}, u32[]{:S(2)}, u32[]{:S(2)}) collective-permute-start(bf16[256,768]{1,0:T(8,128)(2,1)S(1)} %bitcast.269), channel_id=1, source_target_pairs={{24,0},{0,8},{8,16},{16,24},{25,1},{1,9},{9,17},{17,25},{26,2},{2,... | collective-permute-start | bytes 1179656 | tf_op jit(solution)/shard_map/ppermute | solution.py:527
  73.1 18.0 %collective-permute-start.13 = (bf16[256,768]{1,0:T(8,128)(2,1)S(1)}, bf16[256,768]{1,0:T(8,128)(2,1)S(1)}, u32[]{:S(2)}, u32[]{:S(2)}) collective-permute-start(bf16[256,768]{1,0:T(8,128)(2,1)S(1)} %collective-permute-done.12.refs_1_.refs_5_), channel_id=1, source_target_pairs={{0,4},{4,0},{1,5},{5,1},{2,6},{6,2},{3,7},{7,3},{8,12},{12,8},{9,1... | collective-permute-start | bytes 1179656 | tf_op jit(solution)/shard_map/ppermute | solution.py:536
  74.1 25.2 %collective-permute-start.14 = (bf16[256,768]{1,0:T(8,128)(2,1)S(1)}, bf16[256,768]{1,0:T(8,128)(2,1)S(1)}, u32[]{:S(2)}, u32[]{:S(2)}) collective-permute-start(bf16[256,768]{1,0:T(8,128)(2,1)S(1)} %copy-done.19), channel_id=1, source_target_pairs={{8,0},{16,8},{24,16},{0,24},{9,1},{17,9},{25,17},{1,25},{10,2},{18... | collective-permute-start | bytes 1179656 | tf_op jit(solution)/shard_map/ppermute | solution.py:527
  111.7 12.0 %collective-permute-start.17 = (bf16[2,256,768]{2,1,0:T(8,128)(2,1)S(1)}, bf16[2,256,768]{2,1,0:T(8,128)(2,1)S(1)}, u32[]{:S(2)}, u32[]{:S(2)}) collective-permute-start(bf16[2,256,768]{2,1,0:T(8,128)(2,1)S(1)} %pad_maximum_fusion.4), channel_id=1, source_target_pairs={{0,2},{2,0},{1,3},{3,1},{4,6},{6,4},{5,7},{7,5},{8,10},{10,8},{9,1... | collective-permute-start | bytes 2359304 | tf_op jit(solution)/shard_map/ppermute | solution.py:534
  171.4 26.5 %collective-permute-start.26 = (bf16[2,4,48,2304]{3,2,1,0:T(8,128)(2,1)}, bf16[2,4,48,2304]{3,2,1,0:T(8,128)(2,1)}, u32[]{:S(2)}, u32[]{:S(2)}) collective-permute-start(bf16[2,4,48,2304]{3,2,1,0:T(8,128)(2,1)} %get-tuple-element.309), channel_id=1, source_target_pairs={{0,2},{2,0},{1,3},{3,1},{4,6},{6,4},{5,7},{7,5},{8,10},{10,8},{9,1... | collective-permute-start | bytes 5308424 | tf_op jit(solution)/shard_map/ppermute | solution.py:534
  172.0 55.4 %collective-permute-start.30 = (bf16[2,4,48,2304]{3,2,1,0:T(8,128)(2,1)}, bf16[2,4,48,2304]{3,2,1,0:T(8,128)(2,1)}, u32[]{:S(2)}, u32[]{:S(2)}) collective-permute-start(bf16[2,4,48,2304]{3,2,1,0:T(8,128)(2,1)} %get-tuple-element.335), channel_id=1, source_target_pairs={{0,2},{2,0},{1,3},{3,1},{4,6},{6,4},{5,7},{7,5},{8,10},{10,8},{9,1... | collective-permute-start | bytes 5308424 | tf_op jit(solution)/shard_map/ppermute | solution.py:534
  177.4 25.1 %collective-permute-start.25 = (bf16[2,4,24,2304]{3,2,1,0:T(8,128)(2,1)}, bf16[2,4,24,2304]{3,2,1,0:T(8,128)(2,1)}, u32[]{:S(2)}, u32[]{:S(2)}) collective-permute-start(bf16[2,4,24,2304]{3,2,1,0:T(8,128)(2,1)} %fusion.4), channel_id=1, source_target_pairs={{1,0},{0,1},{3,2},{2,3},{5,4},{4,5},{7,6},{6,7},{9,8},{8,9},{11,10... | collective-permute-start | bytes 2654216 | tf_op jit(solution)/shard_map/ppermute | solution.py:527
  204.9 22.6 %collective-permute-start.29 = (bf16[2,4,24,2304]{3,2,1,0:T(8,128)(2,1)}, bf16[2,4,24,2304]{3,2,1,0:T(8,128)(2,1)}, u32[]{:S(2)}, u32[]{:S(2)}) collective-permute-start(bf16[2,4,24,2304]{3,2,1,0:T(8,128)(2,1)} %fusion.5), channel_id=1, source_target_pairs={{1,0},{0,1},{3,2},{2,3},{5,4},{4,5},{7,6},{6,7},{9,8},{8,9},{11,10... | collective-permute-start | bytes 2654216 | tf_op jit(solution)/shard_map/ppermute | solution.py:527
  208.1 19.3 %collective-permute-start.28 = (bf16[4,24,2304]{2,1,0:T(8,128)(2,1)S(1)}, bf16[4,24,2304]{2,1,0:T(8,128)(2,1)S(1)}, u32[]{:S(2)}, u32[]{:S(2)}) collective-permute-start(bf16[4,24,2304]{2,1,0:T(8,128)(2,1)S(1)} %fusion.9), channel_id=1, source_target_pairs={{4,0},{0,4},{5,1},{1,5},{6,2},{2,6},{7,3},{3,7},{12,8},{8,12},{13,... | collective-permute-start | bytes 1327112 | tf_op jit(solution)/shard_map/ppermute | solution.py:527
  210.2 18.8 %collective-permute-start.31 = (bf16[256,768]{1,0:T(8,128)(2,1)S(1)}, bf16[256,768]{1,0:T(8,128)(2,1)}, u32[]{:S(2)}, u32[]{:S(2)}) collective-permute-start(bf16[256,768]{1,0:T(8,128)(2,1)S(1)} %fusion.13), channel_id=1, source_target_pairs={{0,4},{4,0},{1,5},{5,1},{2,6},{6,2},{3,7},{7,3},{8,12},{12,8},{9,1... | collective-permute-start | bytes 1179656 | tf_op jit(solution)/shard_map/ppermute | solution.py:536
  232.4 26.4 %collective-permute-start.36 = (bf16[256,768]{1,0:T(8,128)(2,1)}, bf16[256,768]{1,0:T(8,128)(2,1)}, u32[]{:S(2)}, u32[]{:S(2)}) collective-permute-start(bf16[256,768]{1,0:T(8,128)(2,1)} %add_convert_fusion.6), channel_id=1, source_target_pairs={{24,0},{0,8},{8,16},{16,24},{25,1},{1,9},{9,17},{17,25},{26,2},{2,... | collective-permute-start | bytes 1179656 | tf_op jit(solution)/shard_map/ppermute | solution.py:527
  237.5 22.0 %collective-permute-start.35 = (bf16[2,4,24,2304]{3,2,1,0:T(8,128)(2,1)}, bf16[2,4,24,2304]{3,2,1,0:T(8,128)(2,1)}, u32[]{:S(2)}, u32[]{:S(2)}) collective-permute-start(bf16[2,4,24,2304]{3,2,1,0:T(8,128)(2,1)} %fusion.6), channel_id=1, source_target_pairs={{1,0},{0,1},{3,2},{2,3},{5,4},{4,5},{7,6},{6,7},{9,8},{8,9},{11,10... | collective-permute-start | bytes 2654216 | tf_op jit(solution)/shard_map/ppermute | solution.py:527
  239.7 19.1 %collective-permute-start.34 = (bf16[4,24,2304]{2,1,0:T(8,128)(2,1)S(1)}, bf16[4,24,2304]{2,1,0:T(8,128)(2,1)S(1)}, u32[]{:S(2)}, u32[]{:S(2)}) collective-permute-start(bf16[4,24,2304]{2,1,0:T(8,128)(2,1)S(1)} %fusion.10), channel_id=1, source_target_pairs={{4,0},{0,4},{5,1},{1,5},{6,2},{2,6},{7,3},{3,7},{12,8},{8,12},{13,... | collective-permute-start | bytes 1327112 | tf_op jit(solution)/shard_map/ppermute | solution.py:527
  241.5 17.3 %collective-permute-start.33 = (bf16[2,24,2304]{2,1,0:T(8,128)(2,1)S(1)}, bf16[2,24,2304]{2,1,0:T(8,128)(2,1)}, u32[]{:S(2)}, u32[]{:S(2)}) collective-permute-start(bf16[2,24,2304]{2,1,0:T(8,128)(2,1)S(1)} %slice.384), channel_id=1, source_target_pairs={{0,16},{8,24},{16,0},{24,8},{1,17},{9,25},{17,1},{25,9},{2,18},{10... | collective-permute-start | bytes 663560 | tf_op jit(solution)/shard_map/ppermute | solution.py:584
  241.8 18.4 %collective-permute-start.37 = (bf16[256,768]{1,0:T(8,128)(2,1)S(1)}, bf16[256,768]{1,0:T(8,128)(2,1)}, u32[]{:S(2)}, u32[]{:S(2)}) collective-permute-start(bf16[256,768]{1,0:T(8,128)(2,1)S(1)} %fusion.14), channel_id=1, source_target_pairs={{0,4},{4,0},{1,5},{5,1},{2,6},{6,2},{3,7},{7,3},{8,12},{12,8},{9,1... | collective-permute-start | bytes 1179656 | tf_op jit(solution)/shard_map/ppermute | solution.py:536
  264.4 24.8 %collective-permute-start.42 = (bf16[256,768]{1,0:T(8,128)(2,1)}, bf16[256,768]{1,0:T(8,128)(2,1)}, u32[]{:S(2)}, u32[]{:S(2)}) collective-permute-start(bf16[256,768]{1,0:T(8,128)(2,1)} %add_convert_fusion.5), channel_id=1, source_target_pairs={{8,0},{16,8},{24,16},{0,24},{9,1},{17,9},{25,17},{1,25},{10,2},{18... | collective-permute-start | bytes 1179656 | tf_op jit(solution)/shard_map/ppermute | solution.py:527
  268.5 20.8 %collective-permute-start.41 = (bf16[4,24,2304]{2,1,0:T(8,128)(2,1)}, bf16[4,24,2304]{2,1,0:T(8,128)(2,1)S(1)}, u32[]{:S(2)}, u32[]{:S(2)}) collective-permute-start(bf16[4,24,2304]{2,1,0:T(8,128)(2,1)} %fusion.11), channel_id=1, source_target_pairs={{4,0},{0,4},{5,1},{1,5},{6,2},{2,6},{7,3},{3,7},{12,8},{8,12},{13,... | collective-permute-start | bytes 1327112 | tf_op jit(solution)/shard_map/ppermute | solution.py:527
  270.2 19.0 %collective-permute-start.40 = (bf16[2,24,2304]{2,1,0:T(8,128)(2,1)S(1)}, bf16[2,24,2304]{2,1,0:T(8,128)(2,1)}, u32[]{:S(2)}, u32[]{:S(2)}) collective-permute-start(bf16[2,24,2304]{2,1,0:T(8,128)(2,1)S(1)} %slice.383), channel_id=1, source_target_pairs={{0,16},{8,24},{16,0},{24,8},{1,17},{9,25},{17,1},{25,9},{2,18},{10... | collective-permute-start | bytes 663560 | tf_op jit(solution)/shard_map/ppermute | solution.py:584
  270.7 18.5 %collective-permute-start.39 = (bf16[1,24,2304]{2,1,0:T(8,128)(2,1)S(1)}, bf16[1,24,2304]{2,1,0:T(8,128)(2,1)}, u32[]{:S(2)}, u32[]{:S(2)}) collective-permute-start(bf16[1,24,2304]{2,1,0:T(8,128)(2,1)S(1)} %slice.387), channel_id=1, source_target_pairs={{0,8},{8,0},{16,24},{24,16},{1,9},{9,1},{17,25},{25,17},{2,10},{10... | collective-permute-start | bytes 331784 | tf_op jit(solution)/shard_map/ppermute | solution.py:584
  272.3 17.1 %collective-permute-start.43 = (bf16[256,768]{1,0:T(8,128)(2,1)S(1)}, bf16[256,768]{1,0:T(8,128)(2,1)S(1)}, u32[]{:S(2)}, u32[]{:S(2)}) collective-permute-start(bf16[256,768]{1,0:T(8,128)(2,1)S(1)} %fusion.15), channel_id=1, source_target_pairs={{0,4},{4,0},{1,5},{5,1},{2,6},{6,2},{3,7},{7,3},{8,12},{12,8},{9,1... | collective-permute-start | bytes 1179656 | tf_op jit(solution)/shard_map/ppermute | solution.py:536
  291.2 21.9 %collective-permute-start.47 = (bf16[256,768]{1,0:T(8,128)(2,1)}, bf16[256,768]{1,0:T(8,128)(2,1)S(1)}, u32[]{:S(2)}, u32[]{:S(2)}) collective-permute-start(bf16[256,768]{1,0:T(8,128)(2,1)} %add_convert_fusion.4), channel_id=1, source_target_pairs={{24,0},{0,8},{8,16},{16,24},{25,1},{1,9},{9,17},{17,25},{26,2},{2,... | collective-permute-start | bytes 1179656 | tf_op jit(solution)/shard_map/ppermute | solution.py:527
  292.4 20.7 %collective-permute-start.46 = (bf16[2,24,2304]{2,1,0:T(8,128)(2,1)S(1)}, bf16[2,24,2304]{2,1,0:T(8,128)(2,1)}, u32[]{:S(2)}, u32[]{:S(2)}) collective-permute-start(bf16[2,24,2304]{2,1,0:T(8,128)(2,1)S(1)} %slice.382), channel_id=1, source_target_pairs={{0,16},{8,24},{16,0},{24,8},{1,17},{9,25},{17,1},{25,9},{2,18},{10... | collective-permute-start | bytes 663560 | tf_op jit(solution)/shard_map/ppermute | solution.py:584
  298.3 14.7 %collective-permute-start.48 = (bf16[2,256,768]{2,1,0:T(8,128)(2,1)}, bf16[2,256,768]{2,1,0:T(8,128)(2,1)S(1)}, u32[]{:S(2)}, u32[]{:S(2)}) collective-permute-start(bf16[2,256,768]{2,1,0:T(8,128)(2,1)} %get-tuple-element.399), channel_id=1, source_target_pairs={{0,2},{2,0},{1,3},{3,1},{4,6},{6,4},{5,7},{7,5},{8,10},{10,8},{9,1... | collective-permute-start | bytes 2359304 | tf_op jit(solution)/shard_map/ppermute | solution.py:534
  298.9 14.2 %collective-permute-start.44 = (bf16[4,4,24,640]{3,2,1,0:T(8,128)(2,1)S(1)}, bf16[4,4,24,640]{3,2,1,0:T(8,128)(2,1)S(1)}, u32[]{:S(2)}, u32[]{:S(2)}) collective-permute-start(bf16[4,4,24,640]{3,2,1,0:T(8,128)(2,1)S(1)} %get-tuple-element.436), channel_id=1, source_target_pairs={{1,0},{0,1},{3,2},{2,3},{5,4},{4,5},{7,6},{6,7},{9,8},{8,9},{11,10... | collective-permute-start | bytes 1474568 | tf_op jit(solution)/shard_map/ppermute | solution.py:527
  313.3 15.6 %collective-permute-start.53 = (bf16[256,768]{1,0:T(8,128)(2,1)S(1)}, bf16[256,768]{1,0:T(8,128)(2,1)}, u32[]{:S(2)}, u32[]{:S(2)}) collective-permute-start(bf16[256,768]{1,0:T(8,128)(2,1)S(1)} %fusion.16), channel_id=1, source_target_pairs={{0,4},{4,0},{1,5},{5,1},{2,6},{6,2},{3,7},{7,3},{8,12},{12,8},{9,1... | collective-permute-start | bytes 1179656 | tf_op jit(solution)/shard_map/ppermute | solution.py:536
  (84 other events, 611.1 us)
Sparse Core Ops, SparseCore 0:
  11.5 106.3 all-gather.1

commit v5 on v4

--- a/solution.py
+++ b/solution.py
@@ -23,7 +23,7 @@
 norm_eps = 1e-12
 log2_e = 1.4426950408889634
 CONTRACT_LAST = (((1,), (1,)), ((), ()))
-VMEM_BYTES = 60 * 1024 * 1024
+MIB = 1024 * 1024
 AXES = ("q", "x", "c", "b")
 
 
@@ -167,12 +167,12 @@
             jax.ShapeDtypeStruct((OWN_HEADS, 80, rows), f32),
         ]
     return pl.pallas_call(
-        partial(forward_kernel, first, last, min(512, rows), min(1024, rows)),
+        partial(forward_kernel, first, last, min(1024, rows), min(1024, rows)),
         out_shape=out_shape,
         in_specs=[pl.BlockSpec(memory_space=pltpu.SMEM)] + vmem_specs(len(operands) - 1),
         out_specs=vmem_specs(len(out_shape)),
         scratch_shapes=[pltpu.VMEM((OWN_HEADS, 80, rows), bf16)],
-        compiler_params=pltpu.CompilerParams(vmem_limit_bytes=VMEM_BYTES),
+        compiler_params=pltpu.CompilerParams(vmem_limit_bytes=24 * MIB),
         cost_estimate=pl.CostEstimate(
             flops=int(8e9), transcendentals=OWN_HEADS * rows * rows, bytes_accessed=int(1e7)
         ),
@@ -309,12 +309,12 @@
         out_shape.append(jax.ShapeDtypeStruct((width, WIDE - LANES), f32))
         out_shape.append(jax.ShapeDtypeStruct((8, WIDE - LANES), f32))
     return pl.pallas_call(
-        partial(backward_kernel, first, last, min(512, rows), min(512, rows)),
+        partial(backward_kernel, first, last, min(256, rows), min(1024, rows)),
         out_shape=out_shape,
         in_specs=vmem_specs(len(operands)),
         out_specs=vmem_specs(len(out_shape)),
         scratch_shapes=scratch,
-        compiler_params=pltpu.CompilerParams(vmem_limit_bytes=VMEM_BYTES),
+        compiler_params=pltpu.CompilerParams(vmem_limit_bytes=26 * MIB),
         cost_estimate=pl.CostEstimate(
             flops=int(1.5e10), transcendentals=OWN_HEADS * rows * rows, bytes_accessed=int(1e7)
         ),
@@ -490,7 +490,7 @@
             pltpu.SemaphoreType.DMA((1 + 2 * fold,)),
             pltpu.SemaphoreType.DMA((6,)),
         ],
-        compiler_params=pltpu.CompilerParams(vmem_limit_bytes=VMEM_BYTES),
+        compiler_params=pltpu.CompilerParams(vmem_limit_bytes=34 * MIB),
         cost_estimate=pl.CostEstimate(
             flops=int(2e10), transcendentals=2 * rows * ff, bytes_accessed=int(3e7)
         ),
@@ -518,7 +518,7 @@
         out_shape=jax.ShapeDtypeStruct((4 * n_q * n_b * rows, lanes), bf16),
         in_specs=[pl.BlockSpec(memory_space=pltpu.SMEM)] + vmem_specs(1),
         out_specs=vmem_specs(1)[0],
-        compiler_params=pltpu.CompilerParams(vmem_limit_bytes=VMEM_BYTES),
+        compiler_params=pltpu.CompilerParams(vmem_limit_bytes=12 * MIB),
         name="order_rows",
     )(where, blocks)
 
@@ -546,11 +546,16 @@
         self.state, self.steps = tuple(state), list(steps)
 
 
-def run_stage(chains, outs=()):
+def launch(chain):
+    chain.state = tuple(chain.steps.pop(0)(*chain.state))
+
+
+def run_stage(chains, outs=(), settle=()):
     for chain in chains:
-        chain.state = tuple(chain.steps.pop(0)(*chain.state))
-    outs, states = lax.optimization_barrier((tuple(outs), [c.state for c in chains]))
-    for chain, state in zip(chains, states):
+        launch(chain)
+    joined = [*chains, *settle]
+    outs, states = lax.optimization_barrier((tuple(outs), [c.state for c in joined]))
+    for chain, state in zip(joined, states):
         chain.state = tuple(state)
     return outs
 
@@ -690,6 +695,8 @@
         def over_q():
             source, step = toward(j, n_q)
             own = chunks[source].state[0] if source else x_own
+            if j not in (0, 1):
+                own = lax.optimization_barrier((own, weight_rows.state))[0]
             return (from_shift(own, "q", n_q, n_q - step),)
 
         def over_x(own):
@@ -708,12 +715,8 @@
     chunks = {j: token_chunk(j) for j in arrival}
     line = [chunks[j] for j in arrival]
 
-    def moving_at(slot):
-        begun = [c for i, c in enumerate(line) if slot >= (i if i > 1 else 0)]
-        return [c for c in begun if c.steps]
-
     for slot in range(3):
-        run_stage([weight_rows] + moving_at(slot))
+        run_stage([weight_rows] + [c for c in line[:2] if c.steps and (slot < 2 or c is line[1])])
     chunk_x = {}
 
     by_distance = jnp.stack(weight_rows.state)
@@ -745,10 +748,12 @@
     carry = None
     for step, j in enumerate(arrival):
         first, last = step == 0, step == n_q - 1
+        if chunks[j].steps:
+            run_stage([chunks[j]])
         assert not chunks[j].steps
         chunk_x[j] = chunks[j].state
         outs = attend_chunk(first, last, where_of(j), chunk_x[j], weights, carry)
-        outs = run_stage(moving_at(3 + step), outs)
+        outs = run_stage([c for i in (step + 1, step + 2) if i > 1 for c in line[i : i + 1]], outs)
         kept[j] = (outs[0], outs[1])
         outs = outs[2:]
         if first:
@@ -772,15 +777,27 @@
             sums.append(weight_sum(summands[2 * i], summands[2 * i + 1], n_q, n_b, bi))
     else:
         summed = lax.psum_scatter(summands[0], AXES, scatter_dimension=0, tiled=True).astype(f32)
-    run_stage([square] + sums[:1])
+    run_stage([square] + sums[:2])
+    for chain in sums[2:]:
+        launch(chain)
+    plan = [
+        ([0], [2], [1], []),
+        ([0], [1], [2], [2]),
+        ([1, 0], [], [2], [2]),
+        ([1, 2, 0], [], [], []),
+    ]
     shared = (qx2, qp, w_own, square.state, attx)
     carry = None
     moving, moving_to = [], {}
     for step, j in enumerate(reversed(arrival)):
         first, last = step == 0, step == n_q - 1
+        with_it, ending, going_on, after_it = [], [], [], []
+        if sums and step < len(plan):
+            with_it, ending, going_on, after_it = [[sums[i] for i in part] for part in plan[step]]
         outs = attend_back_chunk(first, last, kept[j], chunk_x[j], shared, carry)
-        begun = [c for c in sums[: step + 2] if c.steps]
-        outs = run_stage(begun + [c for c in moving if c.steps], outs)
+        for chain in going_on:
+            launch(chain)
+        outs = run_stage(with_it + [c for c in moving if c.steps], outs, settle=ending)
         keep, send = outs[:2]
         farther = [c for k, c in moving_to.items() if k and toward(k, n_q)[0] == j and j]
         moving_to[j] = token_sum(keep, send, n_q, j, farther)
@@ -791,7 +808,7 @@
             outs = outs[1:]
         carry = (dox, *outs)
         if not last:
-            carry = run_stage(moving[-1:], carry)
+            carry = run_stage(moving[-1:], carry, settle=after_it)
     grad_joint, col = carry[1:]
 
     own_bias = jnp.stack([col[0, :OWN_WIDTH], col[0, 2 * OWN_WIDTH : 3 * OWN_WIDTH]])
@@ -819,6 +836,7 @@
         return [square_swap(pick(total, group ^ r), r) for r in range(4)]
 
     rows = Chain((total,), rows_over_b, rows_over_q, rows_over_square)
+    run_stage([], settle=[rows, *sums, *moving])
     while any(c.steps for c in [rows, *sums, *moving]):
         run_stage([c for c in [rows, *sums, *moving] if c.steps])
     token_grad = resid_first_grad

time: 353 us -> 374 us (1.059)
  Pallas kernels: 130 us -> 88.3 us
  waiting for transfers between devices: 78.8 us -> 116 us
  local copies, waits for them, and re-layouts: 26.1 us -> 59.4 us
  other arithmetic: 32.2 us -> 23.6 us
    pallas_call x8, Pallas kernels: 107 us -> 70.1 us  [the longest x4 41.7 us: attend_back_chunk(): pl.pallas_call(partial(backward_kernel, first, last, min(256, rows), min(...]
    unnamed x115 -> x239, local copies, waits for them, and re-layouts: 3.42 us -> 40.4 us
    ppermute x12, waiting for transfers between devices: 9.77 us -> 24 us  [square_swap(): return lax.ppermute(value, 'x', [(0, 1), (1, 0)])]
    ppermute x6, waiting for transfers between devices: 14.3 us -> 26.1 us  [over_q(): return (total[:half], lax.ppermute(total[half:].astype(bf16), 'q', pairs))]
    ppermute x20, waiting for transfers between devices: 50.9 us -> 57.3 us  [from_shift(): lax.ppermute(value, axis, [((i + step) % count, i) for i in range(count)])]
    ppermute x15, waiting for transfers between devices: 0.04 us -> 5.87 us  [square_swap(): return lax.ppermute(value, 'c', [(0, 1), (1, 0)])]
    convert_element_type x3, other arithmetic: 5.67 us -> 0.28 us  [over_q(): return (from_shift(total.astype(bf16), 'q', n_q, toward(j, n_q)[1]),)]
    another operation x4, other arithmetic: 0.3 us -> 5.54 us  [over_core(): halves = square_swap(jnp.stack([own, other]), 1)]
  transfers between devices with their start and end apart: 58 -> 58, of which waited for: 21 -> 29; matrix products, arithmetic and copies ran while one was open for 13% -> 9% of each run, Pallas kernels for 31% -> 19%
where the time goes in v5:
time: 374 us; the launch traced here: 370 us
  waiting for transfers between devices  116 us (31%)
  Pallas kernels  88.3 us (24%)
  starting transfers between devices  64.1 us (17%)
  local copies, waits for them, and re-layouts  59.4 us (16%)
  other arithmetic  23.6 us (6%)
  between operations  17 us (5%)
    ppermute x20, waiting for transfers between devices, from_shift(): lax.ppermute(value, axis, [((i + step) % count, i) for i in range(count)])  57.3 us
    pallas_call x4, Pallas kernels, attend_back_chunk(): pl.pallas_call(partial(backward_kernel, first, last, min(256, rows), min(...  41.7 us
    unnamed x239, local copies, waits for them, and re-layouts  40.4 us
    ppermute x20, starting transfers between devices, from_shift(): lax.ppermute(value, axis, [((i + step) % count, i) for i in range(count)])  36.3 us
    pallas_call x4, Pallas kernels, attend_chunk(): pl.pallas_call(partial(forward_kernel, first, last, min(1024, rows), min(...  28.4 us
    ppermute x6, waiting for transfers between devices, over_q(): return (total[:half], lax.ppermute(total[half:].astype(bf16), 'q', pairs))  26.1 us
    ppermute x12, waiting for transfers between devices, square_swap(): return lax.ppermute(value, 'x', [(0, 1), (1, 0)])  24 us
    pallas_call x1, Pallas kernels, ffn_block(): pl.pallas_call(partial(ffn_kernel, layout), out_shape=out_shape + targets...  17.6 us
  transfers between devices with their start and end apart: 58, of which 29 were waited for; matrix products, arithmetic and copies ran while one was open for 9% of the time, Pallas kernels for 19%

profile of v5, /device:TPU:0, one launch (start us, length us, event | category | flops | bytes accessed | tf_op | source)
XLA Modules:
  0.0 369.5 jit_solution(6253123213631336735)
XLA Ops:
  10.1 3.0 collective-permute-start.3
  13.1 3.6 collective-permute-start.4
  20.7 2.4 collective-permute-done.1
  23.3 3.8 %collective-permute-done.4.refs_1_.refs_5_ = bf16[256,768]{1,0:T(8,128)(2,1)S(1)} collective-permute-done((bf16[256,768]{1,0:T(8,128)(2,1)S(1)}, bf16[256,768]{1,0:T(8,128)(2,1)S(1)}, u32[]{:S(2)}, u32[]{:S(2)}) %collective-permute-start.4) | collective-permute-done | bytes 393248 | tf_op jit(solution)/shard_map/ppermute | solution.py:527
  27.4 4.4 %collective-permute-start.5 = (bf16[4,24,640]{2,1,0:T(8,128)(2,1)S(1)}, bf16[4,24,640]{2,1,0:T(8,128)(2,1)S(1)}, u32[]{:S(2)}, u32[]{:S(2)}) collective-permute-start(bf16[4,24,640]{2,1,0:T(8,128)(2,1)S(1)} %pad_maximum_fusion.9), channel_id=1, source_target_pairs={{8,0},{16,8},{24,16},{0,24},{9,1},{17,9},{25,17},{1,25},{10,2},{18... | collective-permute-start | bytes 368648 | tf_op jit(solution)/shard_map/ppermute | solution.py:527
  32.5 6.5 %collective-permute-done.5 = bf16[4,24,640]{2,1,0:T(8,128)(2,1)S(1)} collective-permute-done((bf16[4,24,640]{2,1,0:T(8,128)(2,1)S(1)}, bf16[4,24,640]{2,1,0:T(8,128)(2,1)S(1)}, u32[]{:S(2)}, u32[]{:S(2)}) %collective-permute-start.5) | collective-permute-done | bytes 122912 | tf_op jit(solution)/shard_map/ppermute | solution.py:527
  38.9 5.8 %collective-permute-done.6 = bf16[4,24,640]{2,1,0:T(8,128)(2,1)S(1)} collective-permute-done((bf16[4,24,640]{2,1,0:T(8,128)(2,1)S(1)}, bf16[4,24,640]{2,1,0:T(8,128)(2,1)S(1)}, u32[]{:S(2)}, u32[]{:S(2)}) %collective-permute-start.6) | collective-permute-done | bytes 122912 | tf_op jit(solution)/shard_map/ppermute | solution.py:527
  51.1 13.2 %collective-permute-done.10 = bf16[4,4,24,640]{3,2,1,0:T(8,128)(2,1)S(1)} collective-permute-done((bf16[4,4,24,640]{3,2,1,0:T(8,128)(2,1)S(1)}, bf16[4,4,24,640]{3,2,1,0:T(8,128)(2,1)S(1)}, u32[]{:S(2)}, u32[]{:S(2)}) %collective-permute-start.10) | collective-permute-done | bytes 491552 | tf_op jit(solution)/shard_map/ppermute | solution.py:527
  70.7 7.0 %attend_forward.4 = (bf16[3,1024,256]{2,1,0:T(8,128)(2,1)S(1)}, bf16[3,1024,128]{2,1,0:T(8,128)(2,1)S(1)}, bf16[3,1024,256]{2,1,0:T(8,128)(2,1)S(1)}, bf16[3,102...) custom-call(s32[5]{0:T(128)S(1)} %stack.273.refs_0_, ...), custom_call_target="tpu_custom_call" | custom-call | flops 8000000000 | bytes 10000000 | tf_op jit(solution)/shard_map/attend_forward/pallas_call | solution.py:169
  79.4 16.7 %collective-permute-done.12.refs_1_.refs_5_ = bf16[256,768]{1,0:T(8,128)(2,1)} collective-permute-done((bf16[256,768]{1,0:T(8,128)(2,1)S(1)}, bf16[256,768]{1,0:T(8,128)(2,1)}, u32[]{:S(2)}, u32[]{:S(2)}) %collective-permute-start.12) | collective-permute-done | bytes 393248 | tf_op jit(solution)/shard_map/ppermute | solution.py:527
  97.6 6.5 %attend_forward.5 = (bf16[3,1024,256]{2,1,0:T(8,128)(2,1)S(1)}, bf16[3,1024,128]{2,1,0:T(8,128)(2,1)S(1)}, f32[3,8,1024]{2,1,0:T(8,128)S(1)}, f32[3,80,1024]{2,1,0:T(8,128)S(1)}) custom-call(s32[5]{0:T(128)S(1)} %stack.240.refs_0_, bf16[256,768]{1,0:T(8,128)(2,1)S(1)} %collective-permute-done.4.refs_1_.refs_5_, bf16[256,768]{1,0:T(8,128)(2,1)S(1)} %copy-done.21, ...), custom_call_target="tpu_custom_call" | custom-call | flops 8000000000 | bytes 10000000 | tf_op jit(solution)/shard_map/attend_forward/pallas_call | solution.py:169
  115.5 6.9 %attend_forward.6 = (bf16[3,1024,256]{2,1,0:T(8,128)(2,1)S(1)}, bf16[3,1024,128]{2,1,0:T(8,128)(2,1)S(1)}, f32[3,8,1024]{2,1,0:T(8,128)S(1)}, f32[3,80,1024]{2,1,0:T(8,128)S(1)}) custom-call(s32[5]{0:T(128)S(1)} %stack.235.refs_0_, bf16[256,768]{1,0:T(8,128)(2,1)} %collective-permute-done.12.refs_1_.refs_5_, ...), custom_call_target="tpu_custom_call" | custom-call | flops 8000000000 | bytes 10000000 | tf_op jit(solution)/shard_map/attend_forward/pallas_call | solution.py:169
  134.1 8.0 %attend_forward.7 = (bf16[3,1024,256]{2,1,0:T(8,128)(2,1)S(1)}, bf16[3,1024,128]{2,1,0:T(8,128)(2,1)S(1)}, bf16[256,192]{1,0:T(8,128)(2,1)S(1)}, bf16[256,192]{1...) custom-call(s32[5]{0:T(128)S(1)} %stack.230.refs_0_, ...), custom_call_target="tpu_custom_call" | custom-call | flops 8000000000 | bytes 10000000 | tf_op jit(solution)/shard_map/attend_forward/pallas_call | solution.py:169
  149.8 4.1 %collective-permute-done.19.refs_3_ = bf16[256,192]{1,0:T(8,128)(2,1)S(1)} collective-permute-done((bf16[256,192]{1,0:T(8,128)(2,1)}, bf16[256,192]{1,0:T(8,128)(2,1)S(1)}, u32[]{:S(2)}, u32[]{:S(2)}) %collective-permute-start.19) | collective-permute-done | bytes 98336 | tf_op jit(solution)/shard_map/ppermute | solution.py:536
  162.6 17.6 %feed_forward.1 = (bf16[256,768]{1,0:T(8,128)(2,1)}, f32[256,768]{1,0:T(8,128)S(1)}, bf16[256,192]{1,0:T(8,128)(2,1)S(1)}, bf16[256,192]{1,0:T(8,128)(2,1)}, bf1...) custom-call(s32[7]{0:T(128)S(1)} %stack.225.refs_0_, ...), custom_call_target="tpu_custom_call" | custom-call | flops 20000000000 | bytes 30000000 | tf_op jit(solution)/shard_map/feed_forward/pallas_call | solution.py:480
  203.6 10.8 %attend_backward.4 = (bf16[2,256,768]{2,1,0:T(8,128)(2,1)S(1)}, bf16[2,256,768]{2,1,0:T(8,128)(2,1)S(1)}, bf16[3,1024,128]{2,1,0:T(8,128)(2,1)S(1)}, f32[3,64,10...) custom-call(bf16[3,1024,256]{2,1,0:T(8,128)(2,1)S(1)} %copy-done.53, ...), custom_call_target="tpu_custom_call" | custom-call | flops 15000000512 | bytes 10000000 | tf_op jit(solution)/shard_map/attend_backward/pallas_call | solution.py:311
  214.4 3.6 collective-permute-done.26
  223.5 10.7 %attend_backward.5 = (bf16[2,256,768]{2,1,0:T(8,128)(2,1)S(1)}, bf16[2,256,768]{2,1,0:T(8,128)(2,1)S(1)}, f32[3,64,1024]{2,1,0:T(8,128)S(1)}, f32[768,512]{1,0:T(8,128)S(1)}, f32[8,512]{1,0:T(8,128)S(1)}) custom-call(bf16[3,1024,256]{2,1,0:T(8,128)(2,1)S(1)} %copy-done.51, bf16[3,1024,128]{2,1,0:T(8,128)(2,1)S(1)} %copy-done.68, ...), custom_call_target="tpu_custom_call" | custom-call | flops 15000000512 | bytes 10000000 | tf_op jit(solution)/shard_map/attend_backward/pallas_call | solution.py:311
  234.3 2.7 collective-permute-done.31
  237.0 4.0 %collective-permute-done.30 = bf16[256,768]{1,0:T(8,128)(2,1)S(1)} collective-permute-done((bf16[256,768]{1,0:T(8,128)(2,1)S(1)}, bf16[256,768]{1,0:T(8,128)(2,1)S(1)}, u32[]{:S(2)}, u32[]{:S(2)}) %collective-permute-start.30) | collective-permute-done | bytes 393248 | tf_op jit(solution)/shard_map/ppermute | solution.py:536
  241.3 5.7 %collective-permute-start.36 = (bf16[256,768]{1,0:T(8,128)(2,1)S(1)}, bf16[256,768]{1,0:T(8,128)(2,1)S(1)}, u32[]{:S(2)}, u32[]{:S(2)}) collective-permute-start(bf16[256,768]{1,0:T(8,128)(2,1)S(1)} %add_convert_fusion.6), channel_id=1, source_target_pairs={{24,0},{0,8},{8,16},{16,24},{25,1},{1,9},{9,17},{17,25},{26,2},{2,... | collective-permute-start | bytes 1179656 | tf_op jit(solution)/shard_map/ppermute | solution.py:527
  247.0 3.7 %collective-permute-start.35 = (bf16[2,24,2304]{2,1,0:T(8,128)(2,1)S(1)}, bf16[2,24,2304]{2,1,0:T(8,128)(2,1)S(1)}, u32[]{:S(2)}, u32[]{:S(2)}) collective-permute-start(bf16[2,24,2304]{2,1,0:T(8,128)(2,1)S(1)} %slice.384), channel_id=1, source_target_pairs={{0,16},{8,24},{16,0},{24,8},{1,17},{9,25},{17,1},{25,9},{2,18},{10... | collective-permute-start | bytes 663560 | tf_op jit(solution)/shard_map/ppermute | solution.py:589
  258.5 9.6 %attend_backward.6 = (bf16[2,256,768]{2,1,0:T(8,128)(2,1)S(1)}, bf16[2,256,768]{2,1,0:T(8,128)(2,1)S(1)}, f32[3,64,1024]{2,1,0:T(8,128)S(1)}, f32[768,512]{1,0:T(8,128)S(1)}, f32[8,512]{1,0:T(8,128)S(1)}) custom-call(bf16[3,1024,256]{2,1,0:T(8,128)(2,1)S(1)} %copy-done.47, bf16[3,1024,128]{2,1,0:T(8,128)(2,1)S(1)} %copy-done.66, ...), custom_call_target="tpu_custom_call" | custom-call | flops 15000000512 | bytes 10000000 | tf_op jit(solution)/shard_map/attend_backward/pallas_call | solution.py:311
  269.4 12.8 %collective-permute-done.37 = bf16[256,768]{1,0:T(8,128)(2,1)S(1)} collective-permute-done((bf16[256,768]{1,0:T(8,128)(2,1)S(1)}, bf16[256,768]{1,0:T(8,128)(2,1)S(1)}, u32[]{:S(2)}, u32[]{:S(2)}) %collective-permute-start.37) | collective-permute-done | bytes 393248 | tf_op jit(solution)/shard_map/ppermute | solution.py:536
  283.4 2.6 collective-permute-start.43
  290.8 10.6 %attend_backward.7 = (bf16[2,256,768]{2,1,0:T(8,128)(2,1)S(1)}, bf16[2,256,768]{2,1,0:T(8,128)(2,1)S(1)}, bf16[768,640]{1,0:T(8,128)(2,1)S(1)}, f32[8,640]{1,0:T(8,128)S(1)}) custom-call(bf16[3,1024,256]{2,1,0:T(8,128)(2,1)S(1)} %copy-done.60, bf16[3,1024,128]{2,1,0:T(8,128)(2,1)S(1)} %copy-done.72, bf16[3,1024,256]{2,1,0:T(8,128)(2,1)S(1)} %copy-done.49, ...), custom_call_target="tpu_custom_call" | custom-call | flops 15000000512 | bytes 10000000 | tf_op jit(solution)/shard_map/attend_backward/pallas_call | solution.py:311
  301.5 8.5 %collective-permute-done.40 = bf16[2,24,2304]{2,1,0:T(8,128)(2,1)S(1)} collective-permute-done((bf16[2,24,2304]{2,1,0:T(8,128)(2,1)S(1)}, bf16[2,24,2304]{2,1,0:T(8,128)(2,1)S(1)}, u32[]{:S(2)}, u32[]{:S(2)}) %collective-permute-start.40) | collective-permute-done | bytes 221216 | tf_op jit(solution)/shard_map/ppermute | solution.py:589
  310.0 4.6 %collective-permute-done.41 = bf16[2,24,2304]{2,1,0:T(8,128)(2,1)S(1)} collective-permute-done((bf16[2,24,2304]{2,1,0:T(8,128)(2,1)S(1)}, bf16[2,24,2304]{2,1,0:T(8,128)(2,1)S(1)}, u32[]{:S(2)}, u32[]{:S(2)}) %collective-permute-start.41) | collective-permute-done | bytes 221216 | tf_op jit(solution)/shard_map/ppermute | solution.py:589
  323.4 10.6 %collective-permute-done.47 = bf16[1,24,2304]{2,1,0:T(8,128)(2,1)S(1)} collective-permute-done((bf16[1,24,2304]{2,1,0:T(8,128)(2,1)S(1)}, bf16[1,24,2304]{2,1,0:T(8,128)(2,1)S(1)}, u32[]{:S(2)}, u32[]{:S(2)}) %collective-permute-start.47) | collective-permute-done | bytes 110624 | tf_op jit(solution)/shard_map/ppermute | solution.py:589
  341.6 3.4 collective-permute-start.51
  345.0 2.7 collective-permute-start.52
  350.8 2.8 collective-permute-done.51
  (489 shorter events, 133.8 us)
Async XLA Ops:
  7.2 149.0 %all-gather.2.cloned.1.call-start = ((), (), s32[]{:S(2)}) async-start(), calls=%async_computation | async-start | bytes 10948608 | tf_op jit(solution)/shard_map/all_gather | solution.py:667
  10.1 13.2 %collective-permute-start.3 = (bf16[256,768]{1,0:T(8,128)(2,1)S(1)}, bf16[256,768]{1,0:T(8,128)(2,1)S(1)}, u32[]{:S(2)}, u32[]{:S(2)}) collective-permute-start(bf16[256,768]{1,0:T(8,128)(2,1)S(1)} %bitcast.255), channel_id=1, source_target_pairs={{0,4},{4,0},{1,5},{5,1},{2,6},{6,2},{3,7},{7,3},{8,12},{12,8},{9,1... | collective-permute-start | bytes 1179656 | tf_op jit(solution)/shard_map/ppermute | solution.py:536
  13.1 14.0 %collective-permute-start.4 = (bf16[256,768]{1,0:T(8,128)(2,1)S(1)}, bf16[256,768]{1,0:T(8,128)(2,1)S(1)}, u32[]{:S(2)}, u32[]{:S(2)}) collective-permute-start(bf16[256,768]{1,0:T(8,128)(2,1)S(1)} %bitcast.256), channel_id=1, source_target_pairs={{8,0},{16,8},{24,16},{0,24},{9,1},{17,9},{25,17},{1,25},{10,2},{18... | collective-permute-start | bytes 1179656 | tf_op jit(solution)/shard_map/ppermute | solution.py:527
  27.3 17.4 %collective-permute-start.9 = (bf16[256,768]{1,0:T(8,128)(2,1)S(1)}, bf16[256,768]{1,0:T(8,128)(2,1)S(1)}, u32[]{:S(2)}, u32[]{:S(2)}) collective-permute-start(bf16[256,768]{1,0:T(8,128)(2,1)S(1)} %collective-permute-done.4.refs_1_.refs_5_), channel_id=1, source_target_pairs={{0,4},{4,0},{1,5},{5,1},{2,6},{6,2},{3,7},{7,3},{8,12},{12,8},{9,1... | collective-permute-start | bytes 1179656 | tf_op jit(solution)/shard_map/ppermute | solution.py:536
  31.8 13.0 %collective-permute-start.6 = (bf16[4,24,640]{2,1,0:T(8,128)(2,1)S(1)}, bf16[4,24,640]{2,1,0:T(8,128)(2,1)S(1)}, u32[]{:S(2)}, u32[]{:S(2)}) collective-permute-start(bf16[4,24,640]{2,1,0:T(8,128)(2,1)S(1)} %pad_maximum_fusion.9), channel_id=1, source_target_pairs={{16,0},{24,8},{0,16},{8,24},{17,1},{25,9},{1,17},{9,25},{18,2},{26... | collective-permute-start | bytes 368648 | tf_op jit(solution)/shard_map/ppermute | solution.py:527
  45.8 18.4 %collective-permute-start.10 = (bf16[4,4,24,640]{3,2,1,0:T(8,128)(2,1)S(1)}, bf16[4,4,24,640]{3,2,1,0:T(8,128)(2,1)S(1)}, u32[]{:S(2)}, u32[]{:S(2)}) collective-permute-start(bf16[4,4,24,640]{3,2,1,0:T(8,128)(2,1)S(1)} %pad_maximum_fusion.5), channel_id=1, source_target_pairs={{1,0},{0,1},{3,2},{2,3},{5,4},{4,5},{7,6},{6,7},{9,8},{8,9},{11,10... | collective-permute-start | bytes 1474568 | tf_op jit(solution)/shard_map/ppermute | solution.py:527
  64.3 42.0 %collective-permute-start.14 = (bf16[256,768]{1,0:T(8,128)(2,1)S(1)}, bf16[256,768]{1,0:T(8,128)(2,1)}, u32[]{:S(2)}, u32[]{:S(2)}) collective-permute-start(bf16[256,768]{1,0:T(8,128)(2,1)S(1)} %collective-permute-done.4.refs_1_.refs_5_), channel_id=1, source_target_pairs={{8,0},{16,8},{24,16},{0,24},{9,1},{17,9},{25,17},{1,25},{10,2},{18... | collective-permute-start | bytes 1179656 | tf_op jit(solution)/shard_map/ppermute | solution.py:527
  65.5 30.7 %collective-permute-start.12 = (bf16[256,768]{1,0:T(8,128)(2,1)S(1)}, bf16[256,768]{1,0:T(8,128)(2,1)}, u32[]{:S(2)}, u32[]{:S(2)}) collective-permute-start(bf16[256,768]{1,0:T(8,128)(2,1)S(1)} %bitcast.257), channel_id=1, source_target_pairs={{24,0},{0,8},{8,16},{16,24},{25,1},{1,9},{9,17},{17,25},{26,2},{2,... | collective-permute-start | bytes 1179656 | tf_op jit(solution)/shard_map/ppermute | solution.py:527
  108.7 16.8 %collective-permute-start.16 = (bf16[256,768]{1,0:T(8,128)(2,1)}, bf16[256,768]{1,0:T(8,128)(2,1)S(1)}, u32[]{:S(2)}, u32[]{:S(2)}) collective-permute-start(bf16[256,768]{1,0:T(8,128)(2,1)} %collective-permute-done.14.refs_1_.refs_5_), channel_id=1, source_target_pairs={{0,4},{4,0},{1,5},{5,1},{2,6},{6,2},{3,7},{7,3},{8,12},{12,8},{9,1... | collective-permute-start | bytes 1179656 | tf_op jit(solution)/shard_map/ppermute | solution.py:536
  191.6 22.8 %collective-permute-start.27 = (bf16[2,4,48,2304]{3,2,1,0:T(8,128)(2,1)}, bf16[2,4,48,2304]{3,2,1,0:T(8,128)(2,1)S(1)}, u32[]{:S(2)}, u32[]{:S(2)}) collective-permute-start(bf16[2,4,48,2304]{3,2,1,0:T(8,128)(2,1)} %copy-done.38), channel_id=1, source_target_pairs={{0,2},{2,0},{1,3},{3,1},{4,6},{6,4},{5,7},{7,5},{8,10},{10,8},{9,1... | collective-permute-start | bytes 5308424 | tf_op jit(solution)/shard_map/ppermute | solution.py:534
  195.4 22.6 %collective-permute-start.26 = (bf16[2,4,24,2304]{3,2,1,0:T(8,128)(2,1)S(1)}, bf16[2,4,24,2304]{3,2,1,0:T(8,128)(2,1)S(1)}, u32[]{:S(2)}, u32[]{:S(2)}) collective-permute-start(bf16[2,4,24,2304]{3,2,1,0:T(8,128)(2,1)S(1)} %fusion.4), channel_id=1, source_target_pairs={{1,0},{0,1},{3,2},{2,3},{5,4},{4,5},{7,6},{6,7},{9,8},{8,9},{11,10... | collective-permute-start | bytes 2654216 | tf_op jit(solution)/shard_map/ppermute | solution.py:527
  197.0 39.9 %collective-permute-start.31 = (bf16[2,4,24,2304]{3,2,1,0:T(8,128)(2,1)S(1)}, bf16[2,4,24,2304]{3,2,1,0:T(8,128)(2,1)S(1)}, u32[]{:S(2)}, u32[]{:S(2)}) collective-permute-start(bf16[2,4,24,2304]{3,2,1,0:T(8,128)(2,1)S(1)} %fusion.5), channel_id=1, source_target_pairs={{1,0},{0,1},{3,2},{2,3},{5,4},{4,5},{7,6},{6,7},{9,8},{8,9},{11,10... | collective-permute-start | bytes 2654216 | tf_op jit(solution)/shard_map/ppermute | solution.py:527
  218.2 37.4 %collective-permute-start.33 = (bf16[2,4,24,2304]{3,2,1,0:T(8,128)(2,1)S(1)}, bf16[2,4,24,2304]{3,2,1,0:T(8,128)(2,1)S(1)}, u32[]{:S(2)}, u32[]{:S(2)}) collective-permute-start(bf16[2,4,24,2304]{3,2,1,0:T(8,128)(2,1)S(1)} %fusion.6), channel_id=1, source_target_pairs={{1,0},{0,1},{3,2},{2,3},{5,4},{4,5},{7,6},{6,7},{9,8},{8,9},{11,10... | collective-permute-start | bytes 2654216 | tf_op jit(solution)/shard_map/ppermute | solution.py:527
  220.0 17.0 %collective-permute-start.29 = (bf16[4,24,2304]{2,1,0:T(8,128)(2,1)S(1)}, bf16[4,24,2304]{2,1,0:T(8,128)(2,1)S(1)}, u32[]{:S(2)}, u32[]{:S(2)}) collective-permute-start(bf16[4,24,2304]{2,1,0:T(8,128)(2,1)S(1)} %fusion.9), channel_id=1, source_target_pairs={{4,0},{0,4},{5,1},{1,5},{6,2},{2,6},{7,3},{3,7},{12,8},{8,12},{13,... | collective-permute-start | bytes 1327112 | tf_op jit(solution)/shard_map/ppermute | solution.py:527
  221.8 19.2 %collective-permute-start.30 = (bf16[256,768]{1,0:T(8,128)(2,1)S(1)}, bf16[256,768]{1,0:T(8,128)(2,1)S(1)}, u32[]{:S(2)}, u32[]{:S(2)}) collective-permute-start(bf16[256,768]{1,0:T(8,128)(2,1)S(1)} %fusion.13), channel_id=1, source_target_pairs={{0,4},{4,0},{1,5},{5,1},{2,6},{6,2},{3,7},{7,3},{8,12},{12,8},{9,1... | collective-permute-start | bytes 1179656 | tf_op jit(solution)/shard_map/ppermute | solution.py:536
  241.1 14.5 %collective-permute-start.32 = (bf16[2,256,768]{2,1,0:T(8,128)(2,1)S(1)}, bf16[2,256,768]{2,1,0:T(8,128)(2,1)S(1)}, u32[]{:S(2)}, u32[]{:S(2)}) collective-permute-start(bf16[2,256,768]{2,1,0:T(8,128)(2,1)S(1)} %get-tuple-element.359), channel_id=1, source_target_pairs={{0,2},{2,0},{1,3},{3,1},{4,6},{6,4},{5,7},{7,5},{8,10},{10,8},{9,1... | collective-permute-start | bytes 2359304 | tf_op jit(solution)/shard_map/ppermute | solution.py:534
  241.3 28.1 %collective-permute-start.36 = (bf16[256,768]{1,0:T(8,128)(2,1)S(1)}, bf16[256,768]{1,0:T(8,128)(2,1)S(1)}, u32[]{:S(2)}, u32[]{:S(2)}) collective-permute-start(bf16[256,768]{1,0:T(8,128)(2,1)S(1)} %add_convert_fusion.6), channel_id=1, source_target_pairs={{24,0},{0,8},{8,16},{16,24},{25,1},{1,9},{9,17},{17,25},{26,2},{2,... | collective-permute-start | bytes 1179656 | tf_op jit(solution)/shard_map/ppermute | solution.py:527
  247.0 22.4 %collective-permute-start.35 = (bf16[2,24,2304]{2,1,0:T(8,128)(2,1)S(1)}, bf16[2,24,2304]{2,1,0:T(8,128)(2,1)S(1)}, u32[]{:S(2)}, u32[]{:S(2)}) collective-permute-start(bf16[2,24,2304]{2,1,0:T(8,128)(2,1)S(1)} %slice.384), channel_id=1, source_target_pairs={{0,16},{8,24},{16,0},{24,8},{1,17},{9,25},{17,1},{25,9},{2,18},{10... | collective-permute-start | bytes 663560 | tf_op jit(solution)/shard_map/ppermute | solution.py:589
  252.2 17.2 %collective-permute-start.34 = (bf16[4,24,2304]{2,1,0:T(8,128)(2,1)S(1)}, bf16[4,24,2304]{2,1,0:T(8,128)(2,1)S(1)}, u32[]{:S(2)}, u32[]{:S(2)}) collective-permute-start(bf16[4,24,2304]{2,1,0:T(8,128)(2,1)S(1)} %fusion.10), channel_id=1, source_target_pairs={{4,0},{0,4},{5,1},{1,5},{6,2},{2,6},{7,3},{3,7},{12,8},{8,12},{13,... | collective-permute-start | bytes 1327112 | tf_op jit(solution)/shard_map/ppermute | solution.py:527
  256.1 31.7 %collective-permute-start.39 = (bf16[4,24,2304]{2,1,0:T(8,128)(2,1)S(1)}, bf16[4,24,2304]{2,1,0:T(8,128)(2,1)S(1)}, u32[]{:S(2)}, u32[]{:S(2)}) collective-permute-start(bf16[4,24,2304]{2,1,0:T(8,128)(2,1)S(1)} %fusion.11), channel_id=1, source_target_pairs={{4,0},{0,4},{5,1},{1,5},{6,2},{2,6},{7,3},{3,7},{12,8},{8,12},{13,... | collective-permute-start | bytes 1327112 | tf_op jit(solution)/shard_map/ppermute | solution.py:527
  257.7 24.5 %collective-permute-start.37 = (bf16[256,768]{1,0:T(8,128)(2,1)S(1)}, bf16[256,768]{1,0:T(8,128)(2,1)S(1)}, u32[]{:S(2)}, u32[]{:S(2)}) collective-permute-start(bf16[256,768]{1,0:T(8,128)(2,1)S(1)} %fusion.14), channel_id=1, source_target_pairs={{0,4},{4,0},{1,5},{5,1},{2,6},{6,2},{3,7},{7,3},{8,12},{12,8},{9,1... | collective-permute-start | bytes 1179656 | tf_op jit(solution)/shard_map/ppermute | solution.py:536
  283.4 26.6 %collective-permute-start.43 = (bf16[256,768]{1,0:T(8,128)(2,1)S(1)}, bf16[256,768]{1,0:T(8,128)(2,1)S(1)}, u32[]{:S(2)}, u32[]{:S(2)}) collective-permute-start(bf16[256,768]{1,0:T(8,128)(2,1)S(1)} %add_convert_fusion.5), channel_id=1, source_target_pairs={{8,0},{16,8},{24,16},{0,24},{9,1},{17,9},{25,17},{1,25},{10,2},{18... | collective-permute-start | bytes 1179656 | tf_op jit(solution)/shard_map/ppermute | solution.py:527
  286.0 15.6 %collective-permute-start.42 = (bf16[1,24,2304]{2,1,0:T(8,128)(2,1)S(1)}, bf16[1,24,2304]{2,1,0:T(8,128)(2,1)S(1)}, u32[]{:S(2)}, u32[]{:S(2)}) collective-permute-start(bf16[1,24,2304]{2,1,0:T(8,128)(2,1)S(1)} %slice.387), channel_id=1, source_target_pairs={{0,8},{8,0},{16,24},{24,16},{1,9},{9,1},{17,25},{25,17},{2,10},{10... | collective-permute-start | bytes 331784 | tf_op jit(solution)/shard_map/ppermute | solution.py:589
  286.0 24.0 %collective-permute-start.40 = (bf16[2,24,2304]{2,1,0:T(8,128)(2,1)S(1)}, bf16[2,24,2304]{2,1,0:T(8,128)(2,1)S(1)}, u32[]{:S(2)}, u32[]{:S(2)}) collective-permute-start(bf16[2,24,2304]{2,1,0:T(8,128)(2,1)S(1)} %slice.383), channel_id=1, source_target_pairs={{0,16},{8,24},{16,0},{24,8},{1,17},{9,25},{17,1},{25,9},{2,18},{10... | collective-permute-start | bytes 663560 | tf_op jit(solution)/shard_map/ppermute | solution.py:589
  288.1 26.5 %collective-permute-start.44 = (bf16[256,768]{1,0:T(8,128)(2,1)S(1)}, bf16[256,768]{1,0:T(8,128)(2,1)S(1)}, u32[]{:S(2)}, u32[]{:S(2)}) collective-permute-start(bf16[256,768]{1,0:T(8,128)(2,1)S(1)} %fusion.15), channel_id=1, source_target_pairs={{0,4},{4,0},{1,5},{5,1},{2,6},{6,2},{3,7},{7,3},{8,12},{12,8},{9,1... | collective-permute-start | bytes 1179656 | tf_op jit(solution)/shard_map/ppermute | solution.py:536
  289.8 24.8 %collective-permute-start.41 = (bf16[2,24,2304]{2,1,0:T(8,128)(2,1)S(1)}, bf16[2,24,2304]{2,1,0:T(8,128)(2,1)S(1)}, u32[]{:S(2)}, u32[]{:S(2)}) collective-permute-start(bf16[2,24,2304]{2,1,0:T(8,128)(2,1)S(1)} %slice.382), channel_id=1, source_target_pairs={{0,16},{8,24},{16,0},{24,8},{1,17},{9,25},{17,1},{25,9},{2,18},{10... | collective-permute-start | bytes 663560 | tf_op jit(solution)/shard_map/ppermute | solution.py:589
  318.2 17.0 %collective-permute-start.48 = (bf16[256,768]{1,0:T(8,128)(2,1)S(1)}, bf16[256,768]{1,0:T(8,128)(2,1)S(1)}, u32[]{:S(2)}, u32[]{:S(2)}) collective-permute-start(bf16[256,768]{1,0:T(8,128)(2,1)S(1)} %add_convert_fusion.4), channel_id=1, source_target_pairs={{24,0},{0,8},{8,16},{16,24},{25,1},{1,9},{9,17},{17,25},{26,2},{2,... | collective-permute-start | bytes 1179656 | tf_op jit(solution)/shard_map/ppermute | solution.py:527
  319.6 14.4 %collective-permute-start.47 = (bf16[1,24,2304]{2,1,0:T(8,128)(2,1)S(1)}, bf16[1,24,2304]{2,1,0:T(8,128)(2,1)S(1)}, u32[]{:S(2)}, u32[]{:S(2)}) collective-permute-start(bf16[1,24,2304]{2,1,0:T(8,128)(2,1)S(1)} %slice.385), channel_id=1, source_target_pairs={{0,8},{8,0},{16,24},{24,16},{1,9},{9,1},{17,25},{25,17},{2,10},{10... | collective-permute-start | bytes 331784 | tf_op jit(solution)/shard_map/ppermute | solution.py:589
  319.9 15.4 %collective-permute-start.46 = (bf16[1,24,2304]{2,1,0:T(8,128)(2,1)S(1)}, bf16[1,24,2304]{2,1,0:T(8,128)(2,1)S(1)}, u32[]{:S(2)}, u32[]{:S(2)}) collective-permute-start(bf16[1,24,2304]{2,1,0:T(8,128)(2,1)S(1)} %slice.386), channel_id=1, source_target_pairs={{0,8},{8,0},{16,24},{24,16},{1,9},{9,1},{17,25},{25,17},{2,10},{10... | collective-permute-start | bytes 331784 | tf_op jit(solution)/shard_map/ppermute | solution.py:589
  321.8 13.8 %collective-permute-start.49 = (bf16[2,256,768]{2,1,0:T(8,128)(2,1)S(1)}, bf16[2,256,768]{2,1,0:T(8,128)(2,1)S(1)}, u32[]{:S(2)}, u32[]{:S(2)}) collective-permute-start(bf16[2,256,768]{2,1,0:T(8,128)(2,1)S(1)} %get-tuple-element.431), channel_id=1, source_target_pairs={{0,2},{2,0},{1,3},{3,1},{4,6},{6,4},{5,7},{7,5},{8,10},{10,8},{9,1... | collective-permute-start | bytes 2359304 | tf_op jit(solution)/shard_map/ppermute | solution.py:534
  321.9 13.7 %collective-permute-start.45 = (bf16[4,4,24,640]{3,2,1,0:T(8,128)(2,1)S(1)}, bf16[4,4,24,640]{3,2,1,0:T(8,128)(2,1)S(1)}, u32[]{:S(2)}, u32[]{:S(2)}) collective-permute-start(bf16[4,4,24,640]{3,2,1,0:T(8,128)(2,1)S(1)} %get-tuple-element.466), channel_id=1, source_target_pairs={{1,0},{0,1},{3,2},{2,3},{5,4},{4,5},{7,6},{6,7},{9,8},{8,9},{11,10... | collective-permute-start | bytes 1474568 | tf_op jit(solution)/shard_map/ppermute | solution.py:527
  339.2 14.4 %collective-permute-start.53 = (bf16[256,768]{1,0:T(8,128)(2,1)}, bf16[256,768]{1,0:T(8,128)(2,1)}, u32[]{:S(2)}, u32[]{:S(2)}) collective-permute-start(bf16[256,768]{1,0:T(8,128)(2,1)} %fusion.16), channel_id=1, source_target_pairs={{0,4},{4,0},{1,5},{5,1},{2,6},{6,2},{3,7},{7,3},{8,12},{12,8},{9,1... | collective-permute-start | bytes 1179656 | tf_op jit(solution)/shard_map/ppermute | solution.py:536
  (145 other events, 981.0 us)
Sparse Core Ops, SparseCore 0:
  11.5 104.9 all-gather.1

commit v6 on v5

--- a/solution.py
+++ b/solution.py
@@ -49,11 +49,11 @@
 def forward_kernel(first, last, block_q, block_k, *refs):
     refs = list(refs)
     where_ref = refs.pop(0)
-    pieces = [refs.pop(0) for _ in range(4)]
-    w_ref, bias_ref = [refs.pop(0) for _ in range(2)]
+    far = [refs.pop(0) for _ in range(5)]
+    bias_ref = refs.pop(0)
     if not first:
         qx_ref, peak_in, sum_in = [refs.pop(0) for _ in range(3)]
-    kx_ref, vx_ref = [refs.pop(0) for _ in range(2)]
+    kept = [refs.pop(0) for _ in range(2)]
     if first:
         qx_ref, qp_ref = [refs.pop(0) for _ in range(2)]
     if last:
@@ -61,7 +61,15 @@
         attx_ref, qx2_ref = [refs.pop(0) for _ in range(2)]
     else:
         peak_out, sum_out = [refs.pop(0) for _ in range(2)]
-    (vt_ref,) = refs
+    vt_ref, kx_ref, vx_ref, sem, *near = refs
+    loads = [pltpu.make_async_copy(f, n, sem.at[2 + i]) for i, (f, n) in enumerate(zip(far, near))]
+    for i in (4, 0, 1, 2, 3):
+        loads[i].start()
+    *pieces, w_ref = near
+    stores = [
+        pltpu.make_async_copy(kx_ref, kept[0], sem.at[0]),
+        pltpu.make_async_copy(vx_ref, kept[1], sem.at[1]),
+    ]
     piece_rows = pieces[0].shape[0]
     rows_in = 4 * piece_rows
     lane = lax.broadcasted_iota(jnp.int32, (piece_rows, LANES), 1)
@@ -72,6 +80,9 @@
     skip = 0 if first else LANES
     for p in range(4):
         rows = slice(p * piece_rows, (p + 1) * piece_rows)
+        if p == 0:
+            loads[4].wait()
+        loads[p].wait()
         joint = jnp.dot(pieces[p][...], w_ref[:, skip:], preferred_element_type=f32)
         joint = joint + bias_ref[:, skip:]
         bias = jnp.where(where_ref[p] + row < length, 0.0, masked_score)
@@ -96,6 +107,8 @@
                 qx_ref[h, rows, :LANES] = jnp.where(low, high, mid).astype(bf16)
                 one = jnp.where(lane == HEAD_DIM + 3, 1.0, 0.0)
                 qx_ref[h, rows, LANES:] = jnp.where(low, rest, one).astype(bf16)
+    for store in stores:
+        store.start()
     for h in range(OWN_HEADS):
         for i in range(rows_in // block_q):
             cols = slice(i * block_q, (i + 1) * block_q)
@@ -143,6 +156,12 @@
                 qx2_ref[h, rows, :LANES] = qx_ref[h, rows, :LANES]
                 old = qx_ref[h, rows, LANES:].astype(f32)
                 qx2_ref[h, rows, LANES:] = jnp.where(three, heads[h], old).astype(bf16)
+    for store in stores:
+        store.wait()
+
+
+def in_hbm(value):
+    return pltpu.with_memory_space_constraint(value, pltpu.HBM)
 
 
 def vmem_specs(n):
@@ -152,10 +171,12 @@
 def attend_chunk(first, last, where, pieces, weights, carry):
     piece_rows = pieces[0].shape[0]
     rows = 4 * piece_rows
-    operands = [where, *pieces, *weights]
+    w, bias_row = weights
+    far = [in_hbm(v) for v in (*pieces, w)]
+    operands = [where, *far, bias_row]
     operands += [] if first else list(carry)
     wide_keys = jax.ShapeDtypeStruct((OWN_HEADS, rows, 2 * LANES), bf16)
-    out_shape = [wide_keys, jax.ShapeDtypeStruct((OWN_HEADS, rows, LANES), bf16)]
+    out_shape = [pltpu.HBM(wide_keys.shape, bf16), pltpu.HBM((OWN_HEADS, rows, LANES), bf16)]
     if first:
         out_shape += [wide_keys, jax.ShapeDtypeStruct((OWN_HEADS, rows, LANES), bf16)]
     if last:
@@ -169,10 +190,18 @@
     return pl.pallas_call(
         partial(forward_kernel, first, last, min(1024, rows), min(1024, rows)),
         out_shape=out_shape,
-        in_specs=[pl.BlockSpec(memory_space=pltpu.SMEM)] + vmem_specs(len(operands) - 1),
-        out_specs=vmem_specs(len(out_shape)),
-        scratch_shapes=[pltpu.VMEM((OWN_HEADS, 80, rows), bf16)],
-        compiler_params=pltpu.CompilerParams(vmem_limit_bytes=24 * MIB),
+        in_specs=[pl.BlockSpec(memory_space=pltpu.SMEM)]
+        + [pl.BlockSpec(memory_space=pltpu.HBM)] * len(far)
+        + vmem_specs(len(operands) - 1 - len(far)),
+        out_specs=[pl.BlockSpec(memory_space=pltpu.HBM)] * 2 + vmem_specs(len(out_shape) - 2),
+        scratch_shapes=[
+            pltpu.VMEM((OWN_HEADS, 80, rows), bf16),
+            pltpu.VMEM((OWN_HEADS, rows, 2 * LANES), bf16),
+            pltpu.VMEM((OWN_HEADS, rows, LANES), bf16),
+            pltpu.SemaphoreType.DMA((7,)),
+            *[pltpu.VMEM(v.shape, v.dtype) for v in (*pieces, w)],
+        ],
+        compiler_params=pltpu.CompilerParams(vmem_limit_bytes=20 * MIB),
         cost_estimate=pl.CostEstimate(
             flops=int(8e9), transcendentals=OWN_HEADS * rows * rows, bytes_accessed=int(1e7)
         ),
@@ -182,8 +211,8 @@
 
 def backward_kernel(first, last, block_q, block_k, *refs):
     refs = list(refs)
-    kx_ref, vx_ref, qx_ref, qp_ref, w_ref = [refs.pop(0) for _ in range(5)]
-    pieces = [refs.pop(0) for _ in range(4)]
+    far = [refs.pop(0) for _ in range(7)]
+    qx_ref, qp_ref = [refs.pop(0) for _ in range(2)]
     if first:
         grads = [refs.pop(0) for _ in range(4)]
         attx_ref = refs.pop(0)
@@ -197,7 +226,16 @@
         dqt_ref = refs.pop()
     else:
         dqt_ref, dw_out, col_out = [refs.pop(0) for _ in range(3)]
-    kt_ref, all_ref = refs
+    kt_ref, all_ref, sem = refs[:3]
+    near = refs[3:]
+    kx_ref, vx_ref, w_ref, *pieces = near
+    loads = []
+    for f, n in zip(far[:2], near[:2]):
+        loads += [(f.at[h], n.at[h]) for h in range(OWN_HEADS)]
+    loads += list(zip(far[2:], near[2:]))
+    loads = [pltpu.make_async_copy(f, n, sem.at[i]) for i, (f, n) in enumerate(loads)]
+    for i in (0, OWN_HEADS, *range(1, OWN_HEADS), *range(OWN_HEADS + 1, len(loads))):
+        loads[i].start()
     rows_in = kx_ref.shape[1]
     piece_rows = rows_in // 4
     scale = HEAD_DIM**-0.5
@@ -219,14 +257,16 @@
         dqt_ref[...] = jnp.zeros_like(dqt_ref)
     else:
         dqt_ref[...] = dqt_in[...]
-    for h in range(OWN_HEADS):
-        kt_ref[h] = kx_ref[h, :, LANES:].astype(f32).T[:HEAD_DIM].astype(bf16)
     lane_k = lax.broadcasted_iota(jnp.int32, (block_k, LANES), 1)
     low_k = lane_k < HEAD_DIM
     for j in range(rows_in // block_k):
         ks = slice(j * block_k, (j + 1) * block_k)
         parts = {}
         for h in range(OWN_HEADS):
+            if j == 0:
+                loads[h].wait()
+                loads[OWN_HEADS + h].wait()
+                kt_ref[h] = kx_ref[h, :, LANES:].astype(f32).T[:HEAD_DIM].astype(bf16)
             k = kx_ref[h, ks, :]
             v = vx_ref[h, ks, :]
             kt = kt_ref[h, :, ks]
@@ -259,6 +299,8 @@
         old = all_ref[:, LANES : 2 * LANES].astype(f32)
         all_ref[:, LANES : 2 * LANES] = jnp.where(lane_all < HEAD_DIM, tall, old).astype(bf16)
     skip = 0 if last else LANES
+    for load in loads[2 * OWN_HEADS :]:
+        load.wait()
     d_weight = [None, None]
     for p in range(4):
         rows = slice(p * piece_rows, (p + 1) * piece_rows)
@@ -290,13 +332,16 @@
     kx, vx = chunk
     qx2, qp, w, grads, attx = shared
     rows, width = kx.shape[1], w.shape[0]
-    operands = [kx, vx, qx2, qp, w, *pieces]
+    far = [in_hbm(v) for v in (kx, vx, w, *pieces)]
+    operands = [*far, qx2, qp]
     operands += [*grads, attx] if first else list(carry)
     half = jax.ShapeDtypeStruct((2, rows // 4, width), bf16)
     out_shape = [half, half]
     scratch = [
         pltpu.VMEM((OWN_HEADS, HEAD_DIM, rows), bf16),
         pltpu.VMEM((rows, WIDE), bf16),
+        pltpu.SemaphoreType.DMA((2 * OWN_HEADS + 5,)),
+        *[pltpu.VMEM(v.shape, v.dtype) for v in far],
     ]
     if first:
         out_shape.append(jax.ShapeDtypeStruct((OWN_HEADS, rows, LANES), bf16))
@@ -311,7 +356,8 @@
     return pl.pallas_call(
         partial(backward_kernel, first, last, min(256, rows), min(1024, rows)),
         out_shape=out_shape,
-        in_specs=vmem_specs(len(operands)),
+        in_specs=[pl.BlockSpec(memory_space=pltpu.HBM)] * len(far)
+        + vmem_specs(len(operands) - len(far)),
         out_specs=vmem_specs(len(out_shape)),
         scratch_shapes=scratch,
         compiler_params=pltpu.CompilerParams(vmem_limit_bytes=26 * MIB),
@@ -457,9 +503,9 @@
     n_q, n_b, own_rows, fold, aligned = layout
     rows, width = x.shape
     ff = fold * width
-    operands = [where, *att, x, cot, vectors, ebias, packed]
+    operands = [where, *att, x, cot, vectors, ebias, in_hbm(packed)]
     in_specs = [pl.BlockSpec(memory_space=pltpu.SMEM)] + vmem_specs(8)
-    in_specs += [pl.BlockSpec(memory_space=pl.ANY)]
+    in_specs += [pl.BlockSpec(memory_space=pltpu.HBM)]
     out_shape = [
         jax.ShapeDtypeStruct((rows, width), bf16),
         jax.ShapeDtypeStruct((rows, width), f32),
@@ -469,9 +515,9 @@
     if aligned:
         lead = (2, n_q, n_b * own_rows)
         sizes = [len(part) * width for part in unit_parts(fold)]
-        targets = [jax.ShapeDtypeStruct((*lead, size), bf16) for size in sizes for _ in range(2)]
-    else:
-        targets = [jax.ShapeDtypeStruct((width, width + 2 * ff), bf16)]
+        targets = [pltpu.HBM((*lead, size), bf16) for size in sizes for _ in range(2)]
+    else:
+        targets = [pltpu.HBM((width, width + 2 * ff), bf16)]
     weight_scratch = [
         pltpu.VMEM((width, width), bf16),
         pltpu.VMEM((fold, width, width), bf16),
@@ -481,7 +527,7 @@
         partial(ffn_kernel, layout),
         out_shape=out_shape + targets,
         in_specs=in_specs,
-        out_specs=vmem_specs(len(out_shape)) + [pl.BlockSpec(memory_space=pl.ANY)] * len(targets),
+        out_specs=vmem_specs(len(out_shape)) + [pl.BlockSpec(memory_space=pltpu.HBM)] * len(targets),
         scratch_shapes=weight_scratch
         + weight_scratch
         + [
@@ -490,7 +536,7 @@
             pltpu.SemaphoreType.DMA((1 + 2 * fold,)),
             pltpu.SemaphoreType.DMA((6,)),
         ],
-        compiler_params=pltpu.CompilerParams(vmem_limit_bytes=34 * MIB),
+        compiler_params=pltpu.CompilerParams(vmem_limit_bytes=32 * MIB),
         cost_estimate=pl.CostEstimate(
             flops=int(2e10), transcendentals=2 * rows * ff, bytes_accessed=int(3e7)
         ),
@@ -695,8 +741,6 @@
         def over_q():
             source, step = toward(j, n_q)
             own = chunks[source].state[0] if source else x_own
-            if j not in (0, 1):
-                own = lax.optimization_barrier((own, weight_rows.state))[0]
             return (from_shift(own, "q", n_q, n_q - step),)
 
         def over_x(own):
@@ -715,8 +759,24 @@
     chunks = {j: token_chunk(j) for j in arrival}
     line = [chunks[j] for j in arrival]
 
+
+    def stage(slot, outs=()):
+        with_it = [weight_rows] if slot < 3 else []
+        settle = []
+        for i, c in enumerate(line):
+            begin = max(0, i - 1) if i > 2 else 0
+            if i < 3 and (slot - begin) in range(len(c.steps) and 3 if i else 2):
+                with_it.append(c)
+            elif i > 2 and slot in (begin, begin + 3):
+                with_it.append(c)
+            elif i > 2 and slot == begin + 1:
+                launch(c)
+            elif i > 2 and slot == begin + 2:
+                settle.append(c)
+        return run_stage(with_it, outs, settle)
+
     for slot in range(3):
-        run_stage([weight_rows] + [c for c in line[:2] if c.steps and (slot < 2 or c is line[1])])
+        stage(slot)
     chunk_x = {}
 
     by_distance = jnp.stack(weight_rows.state)
@@ -748,12 +808,10 @@
     carry = None
     for step, j in enumerate(arrival):
         first, last = step == 0, step == n_q - 1
-        if chunks[j].steps:
-            run_stage([chunks[j]])
         assert not chunks[j].steps
         chunk_x[j] = chunks[j].state
         outs = attend_chunk(first, last, where_of(j), chunk_x[j], weights, carry)
-        outs = run_stage([c for i in (step + 1, step + 2) if i > 1 for c in line[i : i + 1]], outs)
+        outs = stage(3 + step, outs)
         kept[j] = (outs[0], outs[1])
         outs = outs[2:]
         if first:

time: 374 us -> 363 us (0.971)
  local copies, waits for them, and re-layouts: 59.4 us -> 31.6 us
  waiting for transfers between devices: 116 us -> 134 us
  Pallas kernels: 88.3 us -> 103 us
  starting transfers between devices: 64.1 us -> 52.4 us
    unnamed x239 -> x125, local copies, waits for them, and re-layouts: 40.4 us -> 11.1 us
    ppermute x20, waiting for transfers between devices: 57.3 us -> 77.2 us  [from_shift(): lax.ppermute(value, axis, [((i + step) % count, i) for i in range(count)])]
    ppermute x20, starting transfers between devices: 36.3 us -> 28 us  [from_shift(): lax.ppermute(value, axis, [((i + step) % count, i) for i in range(count)])]
    pallas_call x4, Pallas kernels: 28.4 us -> 36.3 us  [attend_chunk(): pl.pallas_call(partial(forward_kernel, first, last, min(1024, rows), min(...]
    pallas_call x4, Pallas kernels: 41.7 us -> 47.2 us  [attend_back_chunk(): pl.pallas_call(partial(backward_kernel, first, last, min(256, rows), min(...]
    ppermute x15, waiting for transfers between devices: 5.87 us -> 1.97 us  [square_swap(): return lax.ppermute(value, 'c', [(0, 1), (1, 0)])]
  transfers between devices with their start and end apart: 58 -> 58, of which waited for: 29 -> 30; matrix products, arithmetic and copies ran while one was open for 9% -> 7% of each run, Pallas kernels for 19% -> 23%
where the time goes in v6:
time: 363 us; the launch traced here: 359 us
  waiting for transfers between devices  134 us (37%)
  Pallas kernels  103 us (28%)
  starting transfers between devices  52.4 us (14%)
  local copies, waits for them, and re-layouts  31.6 us (9%)
  other arithmetic  21.1 us (6%)
  between operations  16.6 us (5%)
    ppermute x20, waiting for transfers between devices, from_shift(): lax.ppermute(value, axis, [((i + step) % count, i) for i in range(count)])  77.2 us
    pallas_call x4, Pallas kernels, attend_back_chunk(): pl.pallas_call(partial(backward_kernel, first, last, min(256, rows), min(...  47.2 us
    pallas_call x4, Pallas kernels, attend_chunk(): pl.pallas_call(partial(forward_kernel, first, last, min(1024, rows), min(...  36.3 us
    ppermute x20, starting transfers between devices, from_shift(): lax.ppermute(value, axis, [((i + step) % count, i) for i in range(count)])  28 us
    ppermute x12, waiting for transfers between devices, square_swap(): return lax.ppermute(value, 'x', [(0, 1), (1, 0)])  26.1 us
    ppermute x6, waiting for transfers between devices, over_q(): return (total[:half], lax.ppermute(total[half:].astype(bf16), 'q', pairs))  24.8 us
    pallas_call x1, Pallas kernels, ffn_block(): pl.pallas_call(partial(ffn_kernel, layout), out_shape=out_shape + targets...  18.6 us
    ppermute x12, starting transfers between devices, square_swap(): return lax.ppermute(value, 'x', [(0, 1), (1, 0)])  14.3 us
  transfers between devices with their start and end apart: 58, of which 30 were waited for; matrix products, arithmetic and copies ran while one was open for 7% of the time, Pallas kernels for 23%

profile of v6, /device:TPU:0, one launch (start us, length us, event | category | flops | bytes accessed | tf_op | source)
XLA Modules:
  0.0 359.2 jit_solution(12275118507930738206)
XLA Ops:
  10.1 3.0 collective-permute-start.3
  13.1 3.6 %collective-permute-start.4 = (bf16[256,768]{1,0:T(8,128)(2,1)S(1)}, bf16[256,768]{1,0:T(8,128)(2,1)S(1)}, u32[]{:S(2)}, u32[]{:S(2)}) collective-permute-start(bf16[256,768]{1,0:T(8,128)(2,1)S(1)} %bitcast.252), channel_id=1, source_target_pairs={{8,0},{16,8},{24,16},{0,24},{9,1},{17,9},{25,17},{1,25},{10,2},{18... | collective-permute-start | bytes 1179656 | tf_op jit(solution)/shard_map/ppermute | solution.py:573
  20.6 2.3 collective-permute-done.1
  23.2 5.6 %collective-permute-done.4.refs_1_.refs_3_ = bf16[256,768]{1,0:T(8,128)(2,1)S(1)} collective-permute-done((bf16[256,768]{1,0:T(8,128)(2,1)S(1)}, bf16[256,768]{1,0:T(8,128)(2,1)S(1)}, u32[]{:S(2)}, u32[]{:S(2)}) %collective-permute-start.4) | collective-permute-done | bytes 393248 | tf_op jit(solution)/shard_map/ppermute | solution.py:573
  28.8 12.5 %collective-permute-done.5.refs_1_.refs_3_ = bf16[256,768]{1,0:T(8,128)(2,1)S(1)} collective-permute-done((bf16[256,768]{1,0:T(8,128)(2,1)S(1)}, bf16[256,768]{1,0:T(8,128)(2,1)S(1)}, u32[]{:S(2)}, u32[]{:S(2)}) %collective-permute-start.5) | collective-permute-done | bytes 393248 | tf_op jit(solution)/shard_map/ppermute | solution.py:573
  47.6 4.2 %collective-permute-done.6 = bf16[4,24,640]{2,1,0:T(8,128)(2,1)S(1)} collective-permute-done((bf16[4,24,640]{2,1,0:T(8,128)(2,1)S(1)}, bf16[4,24,640]{2,1,0:T(8,128)(2,1)S(1)}, u32[]{:S(2)}, u32[]{:S(2)}) %collective-permute-start.6) | collective-permute-done | bytes 122912 | tf_op jit(solution)/shard_map/ppermute | solution.py:573
  51.8 15.1 %collective-permute-done.7 = bf16[4,24,640]{2,1,0:T(8,128)(2,1)S(1)} collective-permute-done((bf16[4,24,640]{2,1,0:T(8,128)(2,1)S(1)}, bf16[4,24,640]{2,1,0:T(8,128)(2,1)S(1)}, u32[]{:S(2)}, u32[]{:S(2)}) %collective-permute-start.7) | collective-permute-done | bytes 122912 | tf_op jit(solution)/shard_map/ppermute | solution.py:573
  66.9 4.0 %collective-permute-done.11.refs_3_.refs_5_ = bf16[256,768]{1,0:T(8,128)(2,1)S(1)} collective-permute-done((bf16[256,768]{1,0:T(8,128)(2,1)S(1)}, bf16[256,768]{1,0:T(8,128)(2,1)S(1)}, u32[]{:S(2)}, u32[]{:S(2)}) %collective-permute-start.11) | collective-permute-done | bytes 393248 | tf_op jit(solution)/shard_map/ppermute | solution.py:582
  80.6 15.4 %collective-permute-done.15.refs_1_.refs_3_ = bf16[256,768]{1,0:T(8,128)(2,1)S(1)} collective-permute-done((bf16[256,768]{1,0:T(8,128)(2,1)}, bf16[256,768]{1,0:T(8,128)(2,1)S(1)}, u32[]{:S(2)}, u32[]{:S(2)}) %collective-permute-start.15) | collective-permute-done | bytes 393248 | tf_op jit(solution)/shard_map/ppermute | solution.py:573
  96.0 4.7 %collective-permute-done.12 = bf16[4,4,24,640]{3,2,1,0:T(8,128)(2,1)S(1)} collective-permute-done((bf16[4,4,24,640]{3,2,1,0:T(8,128)(2,1)S(1)}, bf16[4,4,24,640]{3,2,1,0:T(8,128)(2,1)S(1)}, u32[]{:S(2)}, u32[]{:S(2)}) %collective-permute-start.12) | collective-permute-done | bytes 491552 | tf_op jit(solution)/shard_map/ppermute | solution.py:573
  102.4 8.6 %attend_forward.4 = (bf16[3,1024,256]{2,1,0:T(8,128)(2,1)}, bf16[3,1024,128]{2,1,0:T(8,128)(2,1)}, bf16[3,1024,256]{2,1,0:T(8,128)(2,1)S(1)}, bf16[3,1024,128]{2...) custom-call(s32[5]{0:T(128)S(1)} %stack.271.refs_0_, bf16[256,768]{1,0:T(8,128)(2,1)} %bitcast.249, ...), custom_call_target="tpu_custom_call" | custom-call | flops 8000000000 | bytes 10000000 | tf_op jit(solution)/shard_map/attend_forward/pallas_call | solution.py:190
  111.9 9.2 %attend_forward.5 = (bf16[3,1024,256]{2,1,0:T(8,128)(2,1)}, bf16[3,1024,128]{2,1,0:T(8,128)(2,1)}, f32[3,8,1024]{2,1,0:T(8,128)S(1)}, f32[3,80,1024]{2,1,0:T(8,128)S(1)}) custom-call(s32[5]{0:T(128)S(1)} %stack.276.refs_0_, bf16[256,768]{1,0:T(8,128)(2,1)} %copy-done.29, bf16[256,768]{1,0:T(8,128)(2,1)} %get-tuple-element.254.refs_2_.refs_4_, ...), custom_call_target="tpu_custom_call" | custom-call | flops 8000000000 | bytes 10000000 | tf_op jit(solution)/shard_map/attend_forward/pallas_call | solution.py:190
  124.5 9.2 %attend_forward.6 = (bf16[3,1024,256]{2,1,0:T(8,128)(2,1)}, bf16[3,1024,128]{2,1,0:T(8,128)(2,1)}, f32[3,8,1024]{2,1,0:T(8,128)S(1)}, f32[3,80,1024]{2,1,0:T(8,128)S(1)}) custom-call(s32[5]{0:T(128)S(1)} %stack.235.refs_0_, bf16[256,768]{1,0:T(8,128)(2,1)} %copy-done.30, bf16[256,768]{1,0:T(8,128)(2,1)} %get-tuple-element.243.refs_2_.refs_4_, ...), custom_call_target="tpu_custom_call" | custom-call | flops 8000000000 | bytes 10000000 | tf_op jit(solution)/shard_map/attend_forward/pallas_call | solution.py:190
  137.2 9.4 %attend_forward.7 = (bf16[3,1024,256]{2,1,0:T(8,128)(2,1)}, bf16[3,1024,128]{2,1,0:T(8,128)(2,1)}, bf16[256,192]{1,0:T(8,128)(2,1)S(1)}, bf16[256,192]{1,0:T(8,1...) custom-call(s32[5]{0:T(128)S(1)} %stack.230.refs_0_, ...), custom_call_target="tpu_custom_call" | custom-call | flops 8000000000 | bytes 10000000 | tf_op jit(solution)/shard_map/attend_forward/pallas_call | solution.py:190
  151.4 4.2 %collective-permute-done.19.refs_3_ = bf16[256,192]{1,0:T(8,128)(2,1)S(1)} collective-permute-done((bf16[256,192]{1,0:T(8,128)(2,1)S(1)}, bf16[256,192]{1,0:T(8,128)(2,1)S(1)}, u32[]{:S(2)}, u32[]{:S(2)}) %collective-permute-start.19) | collective-permute-done | bytes 98336 | tf_op jit(solution)/shard_map/ppermute | solution.py:582
  157.1 18.6 %feed_forward.1 = (bf16[256,768]{1,0:T(8,128)(2,1)}, f32[256,768]{1,0:T(8,128)S(1)}, bf16[256,192]{1,0:T(8,128)(2,1)S(1)}, bf16[256,192]{1,0:T(8,128)(2,1)S(1)},...) custom-call(s32[7]{0:T(128)S(1)} %stack.225.refs_0_, ...), custom_call_target="tpu_custom_call" | custom-call | flops 20000000000 | bytes 30000000 | tf_op jit(solution)/shard_map/feed_forward/pallas_call | solution.py:526
  180.3 2.7 collective-permute-done.22.refs_11_
  186.6 2.3 collective-permute-start.26
  190.8 12.0 %attend_backward.4 = (bf16[2,256,768]{2,1,0:T(8,128)(2,1)S(1)}, bf16[2,256,768]{2,1,0:T(8,128)(2,1)S(1)}, bf16[3,1024,128]{2,1,0:T(8,128)(2,1)S(1)}, f32[3,64,10...) custom-call(bf16[3,1024,256]{2,1,0:T(8,128)(2,1)} %get-tuple-element.288.refs_0_, ...), custom_call_target="tpu_custom_call" | custom-call | flops 15000000512 | bytes 10000000 | tf_op jit(solution)/shard_map/attend_backward/pallas_call | solution.py:356
  202.8 6.6 %collective-permute-done.26 = bf16[2,4,24,2304]{3,2,1,0:T(8,128)(2,1)S(1)} collective-permute-done((bf16[2,4,24,2304]{3,2,1,0:T(8,128)(2,1)S(1)}, bf16[2,4,24,2304]{3,2,1,0:T(8,128)(2,1)S(1)}, u32[]{:S(2)}, u32[]{:S(2)}) %collective-permute-start.26) | collective-permute-done | bytes 884768 | tf_op jit(solution)/shard_map/ppermute | solution.py:573
  215.6 11.6 %attend_backward.5 = (bf16[2,256,768]{2,1,0:T(8,128)(2,1)S(1)}, bf16[2,256,768]{2,1,0:T(8,128)(2,1)S(1)}, f32[3,64,1024]{2,1,0:T(8,128)S(1)}, f32[768,512]{1,0:T(8,128)S(1)}, f32[8,512]{1,0:T(8,128)S(1)}) custom-call(bf16[3,1024,256]{2,1,0:T(8,128)(2,1)} %get-tuple-element.316.refs_0_, bf16[3,1024,128]{2,1,0:T(8,128)(2,1)} %get-tuple-element.317.refs_1_, ...), custom_call_target="tpu_custom_call" | custom-call | flops 15000000512 | bytes 10000000 | tf_op jit(solution)/shard_map/attend_backward/pallas_call | solution.py:356
  228.3 5.9 %collective-permute-done.30 = bf16[256,768]{1,0:T(8,128)(2,1)S(1)} collective-permute-done((bf16[256,768]{1,0:T(8,128)(2,1)S(1)}, bf16[256,768]{1,0:T(8,128)(2,1)S(1)}, u32[]{:S(2)}, u32[]{:S(2)}) %collective-permute-start.30) | collective-permute-done | bytes 393248 | tf_op jit(solution)/shard_map/ppermute | solution.py:582
  239.2 8.1 %collective-permute-done.33 = bf16[2,4,24,2304]{3,2,1,0:T(8,128)(2,1)S(1)} collective-permute-done((bf16[2,4,24,2304]{3,2,1,0:T(8,128)(2,1)S(1)}, bf16[2,4,24,2304]{3,2,1,0:T(8,128)(2,1)S(1)}, u32[]{:S(2)}, u32[]{:S(2)}) %collective-permute-start.33) | collective-permute-done | bytes 884768 | tf_op jit(solution)/shard_map/ppermute | solution.py:573
  250.1 11.4 %attend_backward.6 = (bf16[2,256,768]{2,1,0:T(8,128)(2,1)S(1)}, bf16[2,256,768]{2,1,0:T(8,128)(2,1)S(1)}, f32[3,64,1024]{2,1,0:T(8,128)S(1)}, f32[768,512]{1,0:T(8,128)S(1)}, f32[8,512]{1,0:T(8,128)S(1)}) custom-call(bf16[3,1024,256]{2,1,0:T(8,128)(2,1)} %get-tuple-element.314.refs_0_, bf16[3,1024,128]{2,1,0:T(8,128)(2,1)} %get-tuple-element.315.refs_1_, ...), custom_call_target="tpu_custom_call" | custom-call | flops 15000000512 | bytes 10000000 | tf_op jit(solution)/shard_map/attend_backward/pallas_call | solution.py:356
  261.6 6.8 %collective-permute-done.37 = bf16[256,768]{1,0:T(8,128)(2,1)S(1)} collective-permute-done((bf16[256,768]{1,0:T(8,128)(2,1)S(1)}, bf16[256,768]{1,0:T(8,128)(2,1)S(1)}, u32[]{:S(2)}, u32[]{:S(2)}) %collective-permute-start.37) | collective-permute-done | bytes 393248 | tf_op jit(solution)/shard_map/ppermute | solution.py:582
  269.6 2.3 collective-permute-start.43
  277.0 12.2 %attend_backward.7 = (bf16[2,256,768]{2,1,0:T(8,128)(2,1)S(1)}, bf16[2,256,768]{2,1,0:T(8,128)(2,1)S(1)}, bf16[768,640]{1,0:T(8,128)(2,1)S(1)}, f32[8,640]{1,0:T(8,128)S(1)}) custom-call(bf16[3,1024,256]{2,1,0:T(8,128)(2,1)} %get-tuple-element.284.refs_0_, bf16[3,1024,128]{2,1,0:T(8,128)(2,1)} %get-tuple-element.285.refs_1_, bf16[768,640]{1,0:T(8,128)(2,1)} %copy-done, ...), custom_call_target="tpu_custom_call" | custom-call | flops 15000000512 | bytes 10000000 | tf_op jit(solution)/shard_map/attend_backward/pallas_call | solution.py:356
  290.2 7.5 %collective-permute-done.40 = bf16[2,24,2304]{2,1,0:T(8,128)(2,1)S(1)} collective-permute-done((bf16[2,24,2304]{2,1,0:T(8,128)(2,1)S(1)}, bf16[2,24,2304]{2,1,0:T(8,128)(2,1)S(1)}, u32[]{:S(2)}, u32[]{:S(2)}) %collective-permute-start.40) | collective-permute-done | bytes 221216 | tf_op jit(solution)/shard_map/ppermute | solution.py:635
  297.7 4.3 %collective-permute-done.41 = bf16[2,24,2304]{2,1,0:T(8,128)(2,1)S(1)} collective-permute-done((bf16[2,24,2304]{2,1,0:T(8,128)(2,1)S(1)}, bf16[2,24,2304]{2,1,0:T(8,128)(2,1)S(1)}, u32[]{:S(2)}, u32[]{:S(2)}) %collective-permute-start.41) | collective-permute-done | bytes 221216 | tf_op jit(solution)/shard_map/ppermute | solution.py:635
  309.2 11.7 %collective-permute-done.47 = bf16[1,24,2304]{2,1,0:T(8,128)(2,1)S(1)} collective-permute-done((bf16[1,24,2304]{2,1,0:T(8,128)(2,1)S(1)}, bf16[1,24,2304]{2,1,0:T(8,128)(2,1)S(1)}, u32[]{:S(2)}, u32[]{:S(2)}) %collective-permute-start.47) | collective-permute-done | bytes 110624 | tf_op jit(solution)/shard_map/ppermute | solution.py:635
  331.3 3.9 %collective-permute-start.51 = (bf16[4,24,640]{2,1,0:T(8,128)(2,1)S(1)}, bf16[4,24,640]{2,1,0:T(8,128)(2,1)}, u32[]{:S(2)}, u32[]{:S(2)}) collective-permute-start(bf16[4,24,640]{2,1,0:T(8,128)(2,1)S(1)} %get-tuple-element.448), channel_id=1, source_target_pairs={{16,0},{24,8},{0,16},{8,24},{17,1},{25,9},{1,17},{9,25},{18,2},{26... | collective-permute-start | bytes 368648 | tf_op jit(solution)/shard_map/ppermute | solution.py:573
  339.5 3.6 collective-permute-done.51
  (375 shorter events, 100.3 us)
Async XLA Ops:
  7.2 149.9 %all-gather.2.cloned.1.call-start = ((), (), s32[]{:S(2)}) async-start(), calls=%async_computation | async-start | bytes 10948608 | tf_op jit(solution)/shard_map/all_gather | solution.py:713
  10.1 13.2 %collective-permute-start.3 = (bf16[256,768]{1,0:T(8,128)(2,1)S(1)}, bf16[256,768]{1,0:T(8,128)(2,1)S(1)}, u32[]{:S(2)}, u32[]{:S(2)}) collective-permute-start(bf16[256,768]{1,0:T(8,128)(2,1)S(1)} %bitcast.251), channel_id=1, source_target_pairs={{0,4},{4,0},{1,5},{5,1},{2,6},{6,2},{3,7},{7,3},{8,12},{12,8},{9,1... | collective-permute-start | bytes 1179656 | tf_op jit(solution)/shard_map/ppermute | solution.py:582
  13.1 15.7 %collective-permute-start.4 = (bf16[256,768]{1,0:T(8,128)(2,1)S(1)}, bf16[256,768]{1,0:T(8,128)(2,1)S(1)}, u32[]{:S(2)}, u32[]{:S(2)}) collective-permute-start(bf16[256,768]{1,0:T(8,128)(2,1)S(1)} %bitcast.252), channel_id=1, source_target_pairs={{8,0},{16,8},{24,16},{0,24},{9,1},{17,9},{25,17},{1,25},{10,2},{18... | collective-permute-start | bytes 1179656 | tf_op jit(solution)/shard_map/ppermute | solution.py:573
  16.7 24.6 %collective-permute-start.5 = (bf16[256,768]{1,0:T(8,128)(2,1)S(1)}, bf16[256,768]{1,0:T(8,128)(2,1)S(1)}, u32[]{:S(2)}, u32[]{:S(2)}) collective-permute-start(bf16[256,768]{1,0:T(8,128)(2,1)S(1)} %bitcast.253), channel_id=1, source_target_pairs={{24,0},{0,8},{8,16},{16,24},{25,1},{1,9},{9,17},{17,25},{26,2},{2,... | collective-permute-start | bytes 1179656 | tf_op jit(solution)/shard_map/ppermute | solution.py:573
  41.4 25.4 %collective-permute-start.10 = (bf16[256,768]{1,0:T(8,128)(2,1)S(1)}, bf16[256,768]{1,0:T(8,128)(2,1)S(1)}, u32[]{:S(2)}, u32[]{:S(2)}) collective-permute-start(bf16[256,768]{1,0:T(8,128)(2,1)S(1)} %collective-permute-done.4.refs_1_.refs_3_), channel_id=1, source_target_pairs={{0,4},{4,0},{1,5},{5,1},{2,6},{6,2},{3,7},{7,3},{8,12},{12,8},{9,1... | collective-permute-start | bytes 1179656 | tf_op jit(solution)/shard_map/ppermute | solution.py:582
  41.8 29.0 %collective-permute-start.11 = (bf16[256,768]{1,0:T(8,128)(2,1)S(1)}, bf16[256,768]{1,0:T(8,128)(2,1)S(1)}, u32[]{:S(2)}, u32[]{:S(2)}) collective-permute-start(bf16[256,768]{1,0:T(8,128)(2,1)S(1)} %collective-permute-done.5.refs_1_.refs_3_), channel_id=1, source_target_pairs={{0,4},{4,0},{1,5},{5,1},{2,6},{6,2},{3,7},{7,3},{8,12},{12,8},{9,1... | collective-permute-start | bytes 1179656 | tf_op jit(solution)/shard_map/ppermute | solution.py:582
  45.3 21.6 %collective-permute-start.7 = (bf16[4,24,640]{2,1,0:T(8,128)(2,1)S(1)}, bf16[4,24,640]{2,1,0:T(8,128)(2,1)S(1)}, u32[]{:S(2)}, u32[]{:S(2)}) collective-permute-start(bf16[4,24,640]{2,1,0:T(8,128)(2,1)S(1)} %pad_maximum_fusion.9), channel_id=1, source_target_pairs={{16,0},{24,8},{0,16},{8,24},{17,1},{25,9},{1,17},{9,25},{18,2},{26... | collective-permute-start | bytes 368648 | tf_op jit(solution)/shard_map/ppermute | solution.py:573
  46.6 20.2 %collective-permute-start.8 = (bf16[4,24,640]{2,1,0:T(8,128)(2,1)S(1)}, bf16[4,24,640]{2,1,0:T(8,128)(2,1)S(1)}, u32[]{:S(2)}, u32[]{:S(2)}) collective-permute-start(bf16[4,24,640]{2,1,0:T(8,128)(2,1)S(1)} %pad_maximum_fusion.9), channel_id=1, source_target_pairs={{24,0},{0,8},{8,16},{16,24},{25,1},{1,9},{9,17},{17,25},{26,2},{2,... | collective-permute-start | bytes 368648 | tf_op jit(solution)/shard_map/ppermute | solution.py:573
  73.8 22.1 %collective-permute-start.15 = (bf16[256,768]{1,0:T(8,128)(2,1)}, bf16[256,768]{1,0:T(8,128)(2,1)S(1)}, u32[]{:S(2)}, u32[]{:S(2)}) collective-permute-start(bf16[256,768]{1,0:T(8,128)(2,1)} %copy-done.29), channel_id=1, source_target_pairs={{8,0},{16,8},{24,16},{0,24},{9,1},{17,9},{25,17},{1,25},{10,2},{18... | collective-permute-start | bytes 1179656 | tf_op jit(solution)/shard_map/ppermute | solution.py:573
  77.1 23.6 %collective-permute-start.12 = (bf16[4,4,24,640]{3,2,1,0:T(8,128)(2,1)S(1)}, bf16[4,4,24,640]{3,2,1,0:T(8,128)(2,1)S(1)}, u32[]{:S(2)}, u32[]{:S(2)}) collective-permute-start(bf16[4,4,24,640]{3,2,1,0:T(8,128)(2,1)S(1)} %pad_maximum_fusion.5), channel_id=1, source_target_pairs={{1,0},{0,1},{3,2},{2,3},{5,4},{4,5},{7,6},{6,7},{9,8},{8,9},{11,10... | collective-permute-start | bytes 1474568 | tf_op jit(solution)/shard_map/ppermute | solution.py:573
  180.0 22.8 %collective-permute-start.27 = (bf16[2,4,48,2304]{3,2,1,0:T(8,128)(2,1)}, bf16[2,4,48,2304]{3,2,1,0:T(8,128)(2,1)S(1)}, u32[]{:S(2)}, u32[]{:S(2)}) collective-permute-start(bf16[2,4,48,2304]{3,2,1,0:T(8,128)(2,1)} %get-tuple-element.312), channel_id=1, source_target_pairs={{0,2},{2,0},{1,3},{3,1},{4,6},{6,4},{5,7},{7,5},{8,10},{10,8},{9,1... | collective-permute-start | bytes 5308424 | tf_op jit(solution)/shard_map/ppermute | solution.py:580
  186.6 22.8 %collective-permute-start.26 = (bf16[2,4,24,2304]{3,2,1,0:T(8,128)(2,1)S(1)}, bf16[2,4,24,2304]{3,2,1,0:T(8,128)(2,1)S(1)}, u32[]{:S(2)}, u32[]{:S(2)}) collective-permute-start(bf16[2,4,24,2304]{3,2,1,0:T(8,128)(2,1)S(1)} %fusion.4), channel_id=1, source_target_pairs={{1,0},{0,1},{3,2},{2,3},{5,4},{4,5},{7,6},{6,7},{9,8},{8,9},{11,10... | collective-permute-start | bytes 2654216 | tf_op jit(solution)/shard_map/ppermute | solution.py:573
  190.5 37.8 %collective-permute-start.31 = (bf16[2,4,24,2304]{3,2,1,0:T(8,128)(2,1)S(1)}, bf16[2,4,24,2304]{3,2,1,0:T(8,128)(2,1)S(1)}, u32[]{:S(2)}, u32[]{:S(2)}) collective-permute-start(bf16[2,4,24,2304]{3,2,1,0:T(8,128)(2,1)S(1)} %fusion.5), channel_id=1, source_target_pairs={{1,0},{0,1},{3,2},{2,3},{5,4},{4,5},{7,6},{6,7},{9,8},{8,9},{11,10... | collective-permute-start | bytes 2654216 | tf_op jit(solution)/shard_map/ppermute | solution.py:573
  209.6 37.7 %collective-permute-start.33 = (bf16[2,4,24,2304]{3,2,1,0:T(8,128)(2,1)S(1)}, bf16[2,4,24,2304]{3,2,1,0:T(8,128)(2,1)S(1)}, u32[]{:S(2)}, u32[]{:S(2)}) collective-permute-start(bf16[2,4,24,2304]{3,2,1,0:T(8,128)(2,1)S(1)} %fusion.6), channel_id=1, source_target_pairs={{1,0},{0,1},{3,2},{2,3},{5,4},{4,5},{7,6},{6,7},{9,8},{8,9},{11,10... | collective-permute-start | bytes 2654216 | tf_op jit(solution)/shard_map/ppermute | solution.py:573
  213.2 15.1 %collective-permute-start.29 = (bf16[4,24,2304]{2,1,0:T(8,128)(2,1)S(1)}, bf16[4,24,2304]{2,1,0:T(8,128)(2,1)S(1)}, u32[]{:S(2)}, u32[]{:S(2)}) collective-permute-start(bf16[4,24,2304]{2,1,0:T(8,128)(2,1)S(1)} %fusion.9), channel_id=1, source_target_pairs={{4,0},{0,4},{5,1},{1,5},{6,2},{2,6},{7,3},{3,7},{12,8},{8,12},{13,... | collective-permute-start | bytes 1327112 | tf_op jit(solution)/shard_map/ppermute | solution.py:573
  214.9 19.4 %collective-permute-start.30 = (bf16[256,768]{1,0:T(8,128)(2,1)S(1)}, bf16[256,768]{1,0:T(8,128)(2,1)S(1)}, u32[]{:S(2)}, u32[]{:S(2)}) collective-permute-start(bf16[256,768]{1,0:T(8,128)(2,1)S(1)} %fusion.13), channel_id=1, source_target_pairs={{0,4},{4,0},{1,5},{5,1},{2,6},{6,2},{3,7},{7,3},{8,12},{12,8},{9,1... | collective-permute-start | bytes 1179656 | tf_op jit(solution)/shard_map/ppermute | solution.py:582
  234.6 27.0 %collective-permute-start.36 = (bf16[256,768]{1,0:T(8,128)(2,1)S(1)}, bf16[256,768]{1,0:T(8,128)(2,1)S(1)}, u32[]{:S(2)}, u32[]{:S(2)}) collective-permute-start(bf16[256,768]{1,0:T(8,128)(2,1)S(1)} %add_convert_fusion.6), channel_id=1, source_target_pairs={{24,0},{0,8},{8,16},{16,24},{25,1},{1,9},{9,17},{17,25},{26,2},{2,... | collective-permute-start | bytes 1179656 | tf_op jit(solution)/shard_map/ppermute | solution.py:573
  234.8 26.7 %collective-permute-start.35 = (bf16[2,24,2304]{2,1,0:T(8,128)(2,1)S(1)}, bf16[2,24,2304]{2,1,0:T(8,128)(2,1)S(1)}, u32[]{:S(2)}, u32[]{:S(2)}) collective-permute-start(bf16[2,24,2304]{2,1,0:T(8,128)(2,1)S(1)} %slice.384), channel_id=1, source_target_pairs={{0,16},{8,24},{16,0},{24,8},{1,17},{9,25},{17,1},{25,9},{2,18},{10... | collective-permute-start | bytes 663560 | tf_op jit(solution)/shard_map/ppermute | solution.py:635
  237.7 23.9 %collective-permute-start.34 = (bf16[4,24,2304]{2,1,0:T(8,128)(2,1)S(1)}, bf16[4,24,2304]{2,1,0:T(8,128)(2,1)S(1)}, u32[]{:S(2)}, u32[]{:S(2)}) collective-permute-start(bf16[4,24,2304]{2,1,0:T(8,128)(2,1)S(1)} %fusion.10), channel_id=1, source_target_pairs={{4,0},{0,4},{5,1},{1,5},{6,2},{2,6},{7,3},{3,7},{12,8},{8,12},{13,... | collective-permute-start | bytes 1327112 | tf_op jit(solution)/shard_map/ppermute | solution.py:573
  247.7 25.9 %collective-permute-start.39 = (bf16[4,24,2304]{2,1,0:T(8,128)(2,1)S(1)}, bf16[4,24,2304]{2,1,0:T(8,128)(2,1)S(1)}, u32[]{:S(2)}, u32[]{:S(2)}) collective-permute-start(bf16[4,24,2304]{2,1,0:T(8,128)(2,1)S(1)} %fusion.11), channel_id=1, source_target_pairs={{4,0},{0,4},{5,1},{1,5},{6,2},{2,6},{7,3},{3,7},{12,8},{8,12},{13,... | collective-permute-start | bytes 1327112 | tf_op jit(solution)/shard_map/ppermute | solution.py:573
  249.4 19.0 %collective-permute-start.37 = (bf16[256,768]{1,0:T(8,128)(2,1)S(1)}, bf16[256,768]{1,0:T(8,128)(2,1)S(1)}, u32[]{:S(2)}, u32[]{:S(2)}) collective-permute-start(bf16[256,768]{1,0:T(8,128)(2,1)S(1)} %fusion.14), channel_id=1, source_target_pairs={{0,4},{4,0},{1,5},{5,1},{2,6},{6,2},{3,7},{7,3},{8,12},{12,8},{9,1... | collective-permute-start | bytes 1179656 | tf_op jit(solution)/shard_map/ppermute | solution.py:582
  269.6 28.1 %collective-permute-start.43 = (bf16[256,768]{1,0:T(8,128)(2,1)S(1)}, bf16[256,768]{1,0:T(8,128)(2,1)S(1)}, u32[]{:S(2)}, u32[]{:S(2)}) collective-permute-start(bf16[256,768]{1,0:T(8,128)(2,1)S(1)} %add_convert_fusion.5), channel_id=1, source_target_pairs={{8,0},{16,8},{24,16},{0,24},{9,1},{17,9},{25,17},{1,25},{10,2},{18... | collective-permute-start | bytes 1179656 | tf_op jit(solution)/shard_map/ppermute | solution.py:573
  271.9 18.4 %collective-permute-start.42 = (bf16[1,24,2304]{2,1,0:T(8,128)(2,1)S(1)}, bf16[1,24,2304]{2,1,0:T(8,128)(2,1)S(1)}, u32[]{:S(2)}, u32[]{:S(2)}) collective-permute-start(bf16[1,24,2304]{2,1,0:T(8,128)(2,1)S(1)} %slice.387), channel_id=1, source_target_pairs={{0,8},{8,0},{16,24},{24,16},{1,9},{9,1},{17,25},{25,17},{2,10},{10... | collective-permute-start | bytes 331784 | tf_op jit(solution)/shard_map/ppermute | solution.py:635
  272.3 25.5 %collective-permute-start.40 = (bf16[2,24,2304]{2,1,0:T(8,128)(2,1)S(1)}, bf16[2,24,2304]{2,1,0:T(8,128)(2,1)S(1)}, u32[]{:S(2)}, u32[]{:S(2)}) collective-permute-start(bf16[2,24,2304]{2,1,0:T(8,128)(2,1)S(1)} %slice.383), channel_id=1, source_target_pairs={{0,16},{8,24},{16,0},{24,8},{1,17},{9,25},{17,1},{25,9},{2,18},{10... | collective-permute-start | bytes 663560 | tf_op jit(solution)/shard_map/ppermute | solution.py:635
  273.9 28.2 %collective-permute-start.44 = (bf16[256,768]{1,0:T(8,128)(2,1)S(1)}, bf16[256,768]{1,0:T(8,128)(2,1)S(1)}, u32[]{:S(2)}, u32[]{:S(2)}) collective-permute-start(bf16[256,768]{1,0:T(8,128)(2,1)S(1)} %fusion.15), channel_id=1, source_target_pairs={{0,4},{4,0},{1,5},{5,1},{2,6},{6,2},{3,7},{7,3},{8,12},{12,8},{9,1... | collective-permute-start | bytes 1179656 | tf_op jit(solution)/shard_map/ppermute | solution.py:582
  275.4 26.7 %collective-permute-start.41 = (bf16[2,24,2304]{2,1,0:T(8,128)(2,1)S(1)}, bf16[2,24,2304]{2,1,0:T(8,128)(2,1)S(1)}, u32[]{:S(2)}, u32[]{:S(2)}) collective-permute-start(bf16[2,24,2304]{2,1,0:T(8,128)(2,1)S(1)} %slice.382), channel_id=1, source_target_pairs={{0,16},{8,24},{16,0},{24,8},{1,17},{9,25},{17,1},{25,9},{2,18},{10... | collective-permute-start | bytes 663560 | tf_op jit(solution)/shard_map/ppermute | solution.py:635
  305.8 16.3 %collective-permute-start.48 = (bf16[256,768]{1,0:T(8,128)(2,1)S(1)}, bf16[256,768]{1,0:T(8,128)(2,1)S(1)}, u32[]{:S(2)}, u32[]{:S(2)}) collective-permute-start(bf16[256,768]{1,0:T(8,128)(2,1)S(1)} %add_convert_fusion.4), channel_id=1, source_target_pairs={{24,0},{0,8},{8,16},{16,24},{25,1},{1,9},{9,17},{17,25},{26,2},{2,... | collective-permute-start | bytes 1179656 | tf_op jit(solution)/shard_map/ppermute | solution.py:573
  306.5 14.4 %collective-permute-start.47 = (bf16[1,24,2304]{2,1,0:T(8,128)(2,1)S(1)}, bf16[1,24,2304]{2,1,0:T(8,128)(2,1)S(1)}, u32[]{:S(2)}, u32[]{:S(2)}) collective-permute-start(bf16[1,24,2304]{2,1,0:T(8,128)(2,1)S(1)} %slice.385), channel_id=1, source_target_pairs={{0,8},{8,0},{16,24},{24,16},{1,9},{9,1},{17,25},{25,17},{2,10},{10... | collective-permute-start | bytes 331784 | tf_op jit(solution)/shard_map/ppermute | solution.py:635
  306.8 15.3 %collective-permute-start.46 = (bf16[1,24,2304]{2,1,0:T(8,128)(2,1)S(1)}, bf16[1,24,2304]{2,1,0:T(8,128)(2,1)S(1)}, u32[]{:S(2)}, u32[]{:S(2)}) collective-permute-start(bf16[1,24,2304]{2,1,0:T(8,128)(2,1)S(1)} %slice.386), channel_id=1, source_target_pairs={{0,8},{8,0},{16,24},{24,16},{1,9},{9,1},{17,25},{25,17},{2,10},{10... | collective-permute-start | bytes 331784 | tf_op jit(solution)/shard_map/ppermute | solution.py:635
  308.7 13.8 %collective-permute-start.49 = (bf16[2,256,768]{2,1,0:T(8,128)(2,1)S(1)}, bf16[2,256,768]{2,1,0:T(8,128)(2,1)S(1)}, u32[]{:S(2)}, u32[]{:S(2)}) collective-permute-start(bf16[2,256,768]{2,1,0:T(8,128)(2,1)S(1)} %get-tuple-element.415), channel_id=1, source_target_pairs={{0,2},{2,0},{1,3},{3,1},{4,6},{6,4},{5,7},{7,5},{8,10},{10,8},{9,1... | collective-permute-start | bytes 2359304 | tf_op jit(solution)/shard_map/ppermute | solution.py:580
  308.8 13.7 %collective-permute-start.45 = (bf16[4,4,24,640]{3,2,1,0:T(8,128)(2,1)S(1)}, bf16[4,4,24,640]{3,2,1,0:T(8,128)(2,1)S(1)}, u32[]{:S(2)}, u32[]{:S(2)}) collective-permute-start(bf16[4,4,24,640]{3,2,1,0:T(8,128)(2,1)S(1)} %get-tuple-element.450), channel_id=1, source_target_pairs={{1,0},{0,1},{3,2},{2,3},{5,4},{4,5},{7,6},{6,7},{9,8},{8,9},{11,10... | collective-permute-start | bytes 1474568 | tf_op jit(solution)/shard_map/ppermute | solution.py:573
  329.5 13.8 %collective-permute-start.53 = (bf16[256,768]{1,0:T(8,128)(2,1)}, bf16[256,768]{1,0:T(8,128)(2,1)}, u32[]{:S(2)}, u32[]{:S(2)}) collective-permute-start(bf16[256,768]{1,0:T(8,128)(2,1)} %fusion.16), channel_id=1, source_target_pairs={{0,4},{4,0},{1,5},{5,1},{2,6},{6,2},{3,7},{7,3},{8,12},{12,8},{9,1... | collective-permute-start | bytes 1179656 | tf_op jit(solution)/shard_map/ppermute | solution.py:582
  (88 other events, 579.7 us)
Sparse Core Ops, SparseCore 0:
  11.5 111.4 all-gather.1
